TPU v7x, 128 devices: a whole 4x4x4 slice. The times are simulated.
128 devices in a mesh: dp: 4 (over z), expert: 32 (over x, y, core).
Axes of the slice: x: 4, y: 4, z: 4, core: 2. Of those that a mesh axis runs over, the one named last changes fastest.
Arguments:
- tokens: bfloat16 [4096, 3584], P('expert', 'dp'), may hold values from -6 to 6
- cotangent: bfloat16 [4096, 3584], P('expert', 'dp'), may hold values from -6 to 6
- routes: int32 [4096, 8], P('expert'), may hold values from 0 to 23, all different within a row; in each aligned block of 128 rows (0 to 127, 128 to 255, ...) at most 48 rows name the same one
- route_weight: float32 [4096, 8], P('expert'), may hold values from 0.1 to 0.6
- gate_weight: bfloat16 [32, 3584, 1024], P('expert', None, 'dp'), may hold values from -6 to 6
- up_weight: bfloat16 [32, 3584, 1024], P('expert', None, 'dp'), may hold values from -6 to 6
- down_weight: bfloat16 [32, 1024, 3584], P('expert', None, 'dp'), may hold values from -6 to 6
- first_moment: bfloat16 [32, 3584, 1024], P('expert', None, 'dp'), may hold values from -0.59765625 to 0.59765625
- second_moment: bfloat16 [32, 3584, 1024], P('expert', None, 'dp'), may hold values from 0.0009994507 to 0.029907227
- placement: int32 [32], replicated, may hold values from 0 to 23, as said below
- migration_plan: int32 [32], replicated, may hold values from 0 to 31, as said below
Outputs:
- layer_output: bfloat16 [4096, 3584], P('expert', 'dp')
- new_gate: bfloat16 [32, 3584, 1024], P('expert', None, 'dp')
- new_first: bfloat16 [32, 3584, 1024], P('expert', None, 'dp')
- new_second: bfloat16 [32, 3584, 1024], P('expert', None, 'dp')
Inputs may be any that keep to these rules, and one draw needn't show every extreme that they name: `routes`: each row names 8 different experts; among the rows of one index of the expert axis no expert is named more than 48 times. `placement`: every expert from 0 to 23 is held by one slot or more. `migration_plan`: every expert keeps one slot or more in the new placement.
All inputs are finite; a program needn't handle non-finite values.
Results may differ from a plain program's by a relative error of at most 0.033.
Values may be sent and summed in bfloat16 or wider, within the bound.
No kernel may reach another device: no remote copies, remote signals or barrier semaphores. Data moves between devices by JAX's collectives and lax.ppermute only.
A program may use at most 128 MiB of HBM per device.

v0:
```python
import math

import jax
import jax.numpy as jnp
from jax import lax
from jax.experimental import pallas as pl
from jax.experimental.pallas import tpu as pltpu
from jax.sharding import PartitionSpec as P


D = 3584
FF = 1024
N_DP = 4
SLOTS = 32
CAP = 48
TOK = 128
QD = D // N_DP
QF = FF // N_DP
PART = D // SLOTS
CHUNKS = ((0, 48),)
ROWS = SLOTS * CAP
HALF = ROWS // 2

beta_first = 0.9
beta_second = 0.95
learn_rate = 0.02
weight_decay = 0.1
epsilon = 1e-08
scale_in = 1.0 / math.sqrt(D)
scale_mid = 1.0 / math.sqrt(FF)


f32 = jnp.float32
bf16 = jnp.bfloat16
VMEM = pltpu.VMEM
SMEM = pltpu.SMEM


def vspec():
    return pl.BlockSpec(memory_space=VMEM)


def sspec():
    return pl.BlockSpec(memory_space=SMEM)


def cost(flops, nbytes):
    return pl.CostEstimate(flops=flops, transcendentals=0, bytes_accessed=nbytes)


def select_kernel(index, place_row, place_col, routes, weights, tokens, *outs):
    rows_out, sel_out, selw_out = outs[: len(CHUNKS)], outs[len(CHUNKS)], outs[len(CHUNKS) + 1]
    me = index[0].astype(f32)
    col = place_col[...]
    same = (col == place_row[...]).astype(f32)
    a = lax.broadcasted_iota(jnp.int32, (SLOTS, SLOTS), 0)
    b = lax.broadcasted_iota(jnp.int32, (SLOTS, SLOTS), 1)
    copies = jnp.sum(same, axis=1, keepdims=True)
    rank = jnp.sum(jnp.where(b < a, same, 0.0), axis=1, keepdims=True)
    turn = me - copies * jnp.floor((me + 0.5) / copies)
    active = jnp.abs(rank - turn) < 0.5
    hit = jnp.zeros((SLOTS, TOK), f32)
    wt = jnp.zeros((SLOTS, TOK), f32)
    for k in range(routes.shape[0]):
        match = (routes[k : k + 1, :] == col) & active
        hit = hit + jnp.where(match, 1.0, 0.0)
        wt = wt + jnp.where(match, weights[k : k + 1, :], 0.0)
    t0 = lax.broadcasted_iota(jnp.int32, (TOK, TOK), 0)
    t1 = lax.broadcasted_iota(jnp.int32, (TOK, TOK), 1)
    before = jnp.where(t0 < t1, 1.0, 0.0).astype(bf16)
    pos = jnp.dot(hit.astype(bf16), before, preferred_element_type=f32)
    pos = jnp.where(hit > 0.5, pos, -1.0)
    base = 0
    for lo, hi in CHUNKS:
        c = hi - lo
        want = (lax.broadcasted_iota(jnp.int32, (c, TOK), 0) + lo).astype(f32)
        for j in range(SLOTS):
            chosen = jnp.abs(pos[j : j + 1, :] - want) < 0.5
            sel_out[base + j * c : base + (j + 1) * c, :] = jnp.where(chosen, 1.0, 0.0).astype(bf16)
            selw_out[base + j * c : base + (j + 1) * c, :] = jnp.where(chosen, wt[j : j + 1, :], 0.0)
        base += SLOTS * c
    base = 0
    for (lo, hi), out in zip(CHUNKS, rows_out):
        total = SLOTS * (hi - lo)
        for r in range(0, total, 512):
            sel = sel_out[base + r : base + r + 512, :]
            out[r : r + 512, :] = jnp.dot(sel, tokens[...], preferred_element_type=f32).astype(bf16)
        base += total


def select_rows(index, placement, routes, weights, tokens):
    rows = SLOTS * CAP
    return pl.pallas_call(
        select_kernel,
        out_shape=[jax.ShapeDtypeStruct((SLOTS * (hi - lo), QD), bf16) for lo, hi in CHUNKS]
        + [jax.ShapeDtypeStruct((rows, TOK), bf16), jax.ShapeDtypeStruct((rows, TOK), f32)],
        in_specs=[sspec()] + [vspec()] * 5,
        out_specs=[vspec()] * (len(CHUNKS) + 2),
        cost_estimate=cost(2 * rows * TOK * QD, 4 << 20),
        name="select_rows",
    )(index, placement[None, :], placement[:, None], routes.T, weights.T, tokens)


def scale_kernel(sel, selw, cot, out):
    for r in range(0, SLOTS * CAP, 512):
        w = jnp.sum(selw[r : r + 512, :], axis=1, keepdims=True)
        picked = jnp.dot(sel[r : r + 512, :], cot[...], preferred_element_type=f32)
        out[r : r + 512, :] = (w * picked).astype(bf16)


def scale_rows(sel, selw, cot):
    rows = SLOTS * CAP
    return pl.pallas_call(
        scale_kernel,
        out_shape=jax.ShapeDtypeStruct((rows, QD), bf16),
        in_specs=[vspec()] * 3,
        out_specs=vspec(),
        cost_estimate=cost(2 * rows * TOK * QD, 4 << 20),
        name="scale_rows",
    )(sel, selw, cot)


def row_block(block, width):
    return pl.BlockSpec((block, width), lambda i: (i, 0))


def piece_specs(block, width):
    half = HALF // block
    low = pl.BlockSpec((block, width), lambda i: (jnp.minimum(i, half - 1), 0))
    high = pl.BlockSpec((block, width), lambda i: (jnp.maximum(i - half, 0), 0))
    return [row_block(block, width)] + [low, high] * 3


def whole(shape):
    return pl.BlockSpec(shape, lambda i: (0,) * len(shape))


def gather_pieces(block, dp, pieces, out):
    width = pieces[0].shape[1]
    first = pl.program_id(0) < HALF // block
    own, la, lb, ra, rb, fa, fb = pieces
    for shift, x in (
        (0, own[...]),
        (3, jnp.where(first, la[...], lb[...])),
        (1, jnp.where(first, ra[...], rb[...])),
        (2, jnp.where(first, fa[...], fb[...])),
    ):
        q = lax.rem(dp[0] + shift, N_DP)
        out[:, pl.ds(pl.multiple_of(q * width, width), width)] = x


HIDDEN_BLOCK = 384


def hidden_kernel(dp, *refs):
    pieces, (wg, wu, g_out, u_out, h_out, x) = refs[:7], refs[7:]
    gather_pieces(HIDDEN_BLOCK, dp, pieces, x)
    g = jnp.dot(x[...], wg[...], preferred_element_type=f32) * scale_in
    u = jnp.dot(x[...], wu[...], preferred_element_type=f32) * scale_in
    g_out[...] = g
    u_out[...] = u
    h_out[...] = (g / (1.0 + jnp.exp(-g)) * u).astype(bf16)


def hidden_of(dp, pieces, wg, wu):
    block = HIDDEN_BLOCK
    return pl.pallas_call(
        hidden_kernel,
        grid=(ROWS // block,),
        out_shape=[
            jax.ShapeDtypeStruct((ROWS, QF), f32),
            jax.ShapeDtypeStruct((ROWS, QF), f32),
            jax.ShapeDtypeStruct((ROWS, QF), bf16),
        ],
        in_specs=[sspec()] + piece_specs(block, QD) + [whole((D, QF)), whole((D, QF))],
        out_specs=[row_block(block, QF)] * 3,
        scratch_shapes=[VMEM((block, D), bf16)],
        cost_estimate=cost(4 * ROWS * D * QF, ROWS * D * 2 + 8 * D * QF),
        name="hidden",
    )(dp, *pieces, wg, wu)


PARTIAL_BLOCK = 384


def partial_kernel(dp, x, wd, *outs):
    for k, out in enumerate(outs):
        q = lax.rem(dp[0] + k, N_DP)
        out[...] = lax.dot_general(
            x[...],
            wd[pl.ds(pl.multiple_of(q * QF, QF), QF), :],
            (((1,), (1,)), ((), ())),
            preferred_element_type=f32,
        ).astype(bf16)


def partial_grads(dp, x, wd):
    block = PARTIAL_BLOCK
    return pl.pallas_call(
        partial_kernel,
        grid=(ROWS // block,),
        out_shape=[jax.ShapeDtypeStruct((ROWS, QF), bf16)] * N_DP,
        in_specs=[sspec(), row_block(block, QD), whole((FF, QD))],
        out_specs=[row_block(block, QF)] * N_DP,
        cost_estimate=cost(2 * ROWS * QD * FF, 6 << 20),
        name="partial_grads",
    )(dp, x, wd)


WEIGHT_BLOCK = 768


def weight_kernel(dp, h0, h1, h2, h3, g_in, u_in, *refs):
    pieces, (out, x, acc) = refs[:7], refs[7:]
    i = pl.program_id(0)
    gather_pieces(WEIGHT_BLOCK, dp, pieces, x)
    grad = h0[...].astype(f32) + h1[...].astype(f32) + h2[...].astype(f32) + h3[...].astype(f32)
    grad = grad * scale_mid
    g = g_in[...]
    s = 1.0 / (1.0 + jnp.exp(-g))
    gg = (grad * u_in[...] * s * (1.0 + g * (1.0 - s))).astype(bf16)
    part = lax.dot_general(gg, x[...], (((0,), (0,)), ((), ())), preferred_element_type=f32)

    @pl.when(i == 0)
    def _():
        acc[...] = part

    @pl.when(i == pl.num_programs(0) - 1)
    def _():
        for r in range(0, D, 512):
            total = (acc[:, r : r + 512] + part[:, r : r + 512]) * scale_in
            out[r : r + 512, :] = total.T.astype(bf16)


def weight_grads(dp, hg, g, u, pieces):
    block = WEIGHT_BLOCK
    assert ROWS // block == 2
    return pl.pallas_call(
        weight_kernel,
        grid=(ROWS // block,),
        out_shape=jax.ShapeDtypeStruct((D, QF), bf16),
        in_specs=[sspec()] + [row_block(block, QF)] * 6 + piece_specs(block, QD),
        out_specs=whole((D, QF)),
        scratch_shapes=[VMEM((block, D), bf16), VMEM((QF, D), f32)],
        cost_estimate=cost(2 * ROWS * D * QF, ROWS * D * 2 + (8 << 20)),
        name="weight_grads",
    )(dp, *hg, g, u, *pieces)


OUTPUT_BLOCK = 384


def output_kernel(dp, *refs):
    pieces, (wd, out, x) = refs[:7], refs[7:]
    gather_pieces(OUTPUT_BLOCK, dp, pieces, x)
    total = jnp.dot(x[...], wd[...], preferred_element_type=f32)
    out[...] = (total * scale_mid).astype(bf16)


def outputs_of(dp, pieces, wd):
    block = OUTPUT_BLOCK
    return pl.pallas_call(
        output_kernel,
        grid=(ROWS // block,),
        out_shape=jax.ShapeDtypeStruct((ROWS, QD), bf16),
        in_specs=[sspec()] + piece_specs(block, QF) + [whole((FF, QD))],
        out_specs=row_block(block, QD),
        scratch_shapes=[VMEM((block, FF), bf16)],
        cost_estimate=cost(2 * ROWS * FF * QD, ROWS * (FF + QD) * 2),
        name="outputs",
    )(dp, *pieces, wd)


def combine_kernel(selw, *refs):
    out = refs[-1]
    total = jnp.zeros(out.shape, f32)
    base = 0
    for ref in refs[:-1]:
        n = ref.shape[0]
        w = selw[base : base + n, :]
        high = w.astype(bf16)
        low = (w - high.astype(f32)).astype(bf16)
        rows = ref[...]
        for part in (high, low):
            total = total + lax.dot_general(
                part, rows, (((0,), (0,)), ((), ())), preferred_element_type=f32
            )
        base += n
    out[...] = total.astype(bf16)


def combine(selw, rows):
    return pl.pallas_call(
        combine_kernel,
        out_shape=jax.ShapeDtypeStruct((TOK, QD), bf16),
        in_specs=[vspec()] * (1 + len(rows)),
        out_specs=vspec(),
        cost_estimate=cost(4 * SLOTS * CAP * TOK * QD, 4 << 20),
        name="combine",
    )(selw, *rows)


def migrate_kernel(plan, x, out):
    for s in range(SLOTS):
        out[s] = x[plan[s]]


def migrate(plan, states):
    return pl.pallas_call(
        migrate_kernel,
        grid_spec=pltpu.PrefetchScalarGridSpec(
            num_scalar_prefetch=1,
            grid=(1,),
            in_specs=[pl.BlockSpec((SLOTS, PART, QF), lambda i, *_: (0, 0, 0))],
            out_specs=pl.BlockSpec((SLOTS, PART, QF), lambda i, *_: (0, 0, 0)),
        ),
        out_shape=jax.ShapeDtypeStruct((SLOTS, PART, QF), bf16),
        cost_estimate=cost(0, 4 << 20),
        name="migrate",
    )(plan, states)


UPDATE_ROWS = 16


def update_kernel(plan, placement, grads, first, second, out, total):
    total[...] = jnp.zeros_like(total)
    for s in range(SLOTS):
        total[placement[s]] += grads[s].astype(f32)

    def body(s, carry):
        p = plan[s]
        g = total[placement[p]]
        one = beta_first * first[p].astype(f32) + (1.0 - beta_first) * g
        two = beta_second * second[p].astype(f32) + (1.0 - beta_second) * g * g
        out[s, 0] = one.astype(bf16)
        out[s, 1] = two.astype(bf16)
        return carry

    lax.fori_loop(0, SLOTS, body, 0, unroll=4)


def update(plan, placement, grads, states):
    steps = PART // UPDATE_ROWS

    def part(n):
        return pl.BlockSpec((SLOTS, UPDATE_ROWS, QF), lambda i, *_: (0, n * steps + i, 0))

    return pl.pallas_call(
        update_kernel,
        grid_spec=pltpu.PrefetchScalarGridSpec(
            num_scalar_prefetch=2,
            grid=(steps,),
            in_specs=[part(0), part(1), part(2)],
            out_specs=pl.BlockSpec((SLOTS, 2, UPDATE_ROWS, QF), lambda i, *_: (0, 0, i, 0)),
            scratch_shapes=[VMEM((SLOTS, UPDATE_ROWS, QF), f32)],
        ),
        out_shape=jax.ShapeDtypeStruct((SLOTS, 2, PART, QF), bf16),
        cost_estimate=cost(20 * D * SLOTS * QF // SLOTS, 10 << 20),
        name="update",
    )(plan, placement, grads, states, states)


def finish_kernel(gate, moments, g_out, one_out, two_out):
    one = moments[:, 0]
    two = moments[:, 1]
    one_out[...] = one
    two_out[...] = two
    w = gate[...].astype(f32) * (1.0 - learn_rate * weight_decay)
    step = learn_rate * one.astype(f32) / (jnp.sqrt(two.astype(f32)) + epsilon)
    g_out[...] = (w - step).astype(bf16)


def finish(gate, moments):
    n = 4
    part = pl.BlockSpec((n, PART, QF), lambda i: (i, 0, 0))
    return pl.pallas_call(
        finish_kernel,
        grid=(SLOTS // n,),
        out_shape=[jax.ShapeDtypeStruct((SLOTS, PART, QF), bf16)] * 3,
        in_specs=[part, pl.BlockSpec((n, 2, PART, QF), lambda i: (i, 0, 0, 0))],
        out_specs=[part] * 3,
        cost_estimate=cost(20 * D * QF, 12 << 20),
        name="finish",
    )(gate, moments)


def exchange(x):
    return lax.all_to_all(x, "expert", split_axis=0, concat_axis=0, tiled=True)


def shift(x, by):
    return lax.ppermute(x, "dp", [(i, (i + by) % N_DP) for i in range(N_DP)])


def ring(x):
    low, high = x[:HALF], x[HALF:]
    la = shift(low, 1)
    rb = shift(high, -1)
    lb = shift(high, 1)
    ra = shift(low, -1)
    fa = shift(la, 1)
    fb = shift(rb, -1)
    return (x, la, lb, ra, rb, fa, fb)


def device_step(
    tokens,
    cotangent,
    routes,
    route_weight,
    gate_weight,
    up_weight,
    down_weight,
    first_moment,
    second_moment,
    placement,
    migration_plan,
):
    index = lax.axis_index("expert").astype(jnp.int32)[None]
    dp = lax.axis_index("dp").astype(jnp.int32)[None]
    wg, wu, wd = gate_weight[0], up_weight[0], down_weight[0]
    rows, sel, selw = select_rows(index, placement, routes, route_weight, tokens)
    got = exchange(rows.reshape(SLOTS, CAP, QD)).reshape(ROWS, QD)
    sent_grads = scale_rows(sel, selw, cotangent)
    got_grads = exchange(sent_grads.reshape(SLOTS, CAP, QD)).reshape(ROWS, QD)
    packed = jnp.concatenate(
        [x[0].reshape(SLOTS, PART, QF) for x in (gate_weight, first_moment, second_moment)],
        axis=1,
    )
    states = exchange(packed)
    new_gate_in = exchange(migrate(migration_plan, states))
    pieces = ring(got)
    g, u, h = hidden_of(dp, pieces, wg, wu)
    partials = partial_grads(dp, got_grads, wd)
    hg = [partials[0]] + [shift(partials[k], k) for k in range(1, N_DP)]
    wgrad = weight_grads(dp, hg, g, u, pieces)
    got_wgrad = exchange(wgrad.reshape(SLOTS, PART, QF))
    moments = exchange(update(migration_plan, placement, got_wgrad, states))
    out = outputs_of(dp, ring(h), wd)
    returned = exchange(out.reshape(SLOTS, CAP, QD)).reshape(ROWS, QD)
    layer_output = combine(selw, [returned])
    results = finish(new_gate_in, moments)
    return (layer_output,) + tuple(r.reshape(1, D, QF) for r in results)


def solution(mesh):
    placed = (
        P("expert", "dp"),
        P("expert", "dp"),
        P("expert", None),
        P("expert", None),
        P("expert", None, "dp"),
        P("expert", None, "dp"),
        P("expert", None, "dp"),
        P("expert", None, "dp"),
        P("expert", None, "dp"),
        P(),
        P(),
    )
    return jax.shard_map(
        device_step,
        mesh=mesh,
        in_specs=placed,
        out_specs=(
            P("expert", "dp"),
            P("expert", None, "dp"),
            P("expert", None, "dp"),
            P("expert", None, "dp"),
        ),
        check_vma=False,
    )
```

profile of v0, /device:TPU:1, one launch (start us, length us, event | category | flops | bytes accessed | tf_op | source)
XLA Modules:
  0.0 427.6 jit_solution(13799128731715525225)
XLA Ops:
  0.6 1.3 copy.15.place_col
  2.0 3.8 select_rows.1
  5.7 8.6 %all-to-all-start = ((bf16[32,48,896]{2,1,0:T(8,128)(2,1)}), bf16[32,48,896]{2,1,0:T(8,128)(2,1)S(1)}, u32[]{:S(2)}, u32[]{:S(2)}) async-start(bf16[32,48,896]{2,1,0:T(8,128)(2,1)} %bitcast.30), calls=%async_computation | async-start | bytes 5505024 | tf_op jit(solution)/shard_map/all_to_all | solution.py:389
  14.3 5.8 %pad_maximum_fusion = bf16[32,336,256]{2,1,0:T(8,128)(2,1)} fusion(bf16[32,112,256]{2,1,0:T(8,128)(2,1)} %bitcast.31, bf16[32,112,256]{2,1,0:T(8,128)(2,1)} %bitcast.32, bf16[32,112,256]{2,1,0:T(8,128)(2,1)} %bitcast.33), kind=kLoop, calls=%fused_computation | loop fusion | flops 16515072 | bytes 11010048 | tf_op jit(solution)/shard_map/concatenate | solution.py:427
  20.1 29.5 %all-to-all-done = bf16[32,48,896]{2,1,0:T(8,128)(2,1)S(1)} async-done(((bf16[32,48,896]{2,1,0:T(8,128)(2,1)}), bf16[32,48,896]{2,1,0:T(8,128)(2,1)S(1)}, u32[]{:S(2)}, u32[]{:S(2)}) %all-to-all-start) | async-done | bytes 2752544 | tf_op jit(solution)/shard_map/all_to_all | solution.py:389
  49.6 5.4 %all-to-all-start.2 = ((bf16[32,336,256]{2,1,0:T(8,128)(2,1)}), bf16[32,336,256]{2,1,0:T(8,128)(2,1)}, u32[]{:S(2)}, u32[]{:S(2)}) async-start(bf16[32,336,256]{2,1,0:T(8,128)(2,1)} %pad_maximum_fusion), calls=%async_computation.2 | async-start | bytes 11010048 | tf_op jit(solution)/shard_map/all_to_all | solution.py:389
  55.0 3.7 scale_rows.1
  58.7 64.2 %all-to-all-done.2.x.first.second = bf16[32,336,256]{2,1,0:T(8,128)(2,1)} async-done(((bf16[32,336,256]{2,1,0:T(8,128)(2,1)}), bf16[32,336,256]{2,1,0:T(8,128)(2,1)}, u32[]{:S(2)}, u32[]{:S(2)}) %all-to-all-start.2) | async-done | bytes 5505056 | tf_op jit(solution)/shard_map/all_to_all | solution.py:389
  122.9 10.4 %all-to-all-start.4 = ((bf16[32,48,896]{2,1,0:T(8,128)(2,1)}), bf16[32,48,896]{2,1,0:T(8,128)(2,1)}, u32[]{:S(2)}, u32[]{:S(2)}) async-start(bf16[32,48,896]{2,1,0:T(8,128)(2,1)} %bitcast.26), calls=%async_computation.4 | async-start | bytes 5505024 | tf_op jit(solution)/shard_map/all_to_all | solution.py:389
  133.3 1.8 fusion
  135.0 1.6 collective-permute-start
  136.6 2.1 collective-permute-start.3
  138.8 1.5 collective-permute-start.2
  140.2 0.0 collective-permute-start.1
  140.2 29.0 %collective-permute-done.refs_1_ = bf16[768,896]{1,0:T(8,128)(2,1)S(1)} collective-permute-done((bf16[768,896]{1,0:T(8,128)(2,1)}, bf16[768,896]{1,0:T(8,128)(2,1)S(1)}, u32[]{:S(2)}, u32[]{:S(2)}) %collective-permute-start) | collective-permute-done | bytes 1376288 | tf_op jit(solution)/shard_map/ppermute | solution.py:393
  169.2 0.0 collective-permute-start.4
  169.2 0.0 collective-permute-done.3.refs_4_
  169.2 2.7 collective-permute-start.5
  171.9 3.5 migrate.1
  175.4 0.0 copy-done.4
  175.4 0.0 all-to-all-done.4
  175.4 9.1 %all-to-all-start.3 = ((bf16[32,112,256]{2,1,0:T(8,128)(2,1)}), bf16[32,112,256]{2,1,0:T(8,128)(2,1)S(1)}, u32[]{:S(2)}, u32[]{:S(2)}) async-start(bf16[32,112,256]{2,1,0:T(8,128)(2,1)} %migrate.1), calls=%async_computation.3 | async-start | bytes 3670016 | tf_op jit(solution)/shard_map/all_to_all | solution.py:389
  184.5 6.9 %partial_grads.1 = (bf16[1536,256]{1,0:T(8,128)(2,1)}, bf16[1536,256]{1,0:T(8,128)(2,1)}, bf16[1536,256]{1,0:T(8,128)(2,1)}, bf16[1536,256]{1,0:T(8,128)(2,1)}) custom-call(s32[1]{0:T(128)} %bitcast.5.dp, bf16[1536,896]{1,0:T(8,128)(2,1)} %bitcast.19.x, bf16[1024,896]{1,0:T(8,128)(2,1)} %bitcast.38), custom_call_target="tpu_custom_call" | custom-call | flops 2818572288 | bytes 6291456 | tf_op jit(solution)/shard_map/partial_grads/pallas_call | solution.py:199
  191.4 0.0 collective-permute-start.12
  191.4 6.5 %collective-permute-done.2.refs_3_ = bf16[768,896]{1,0:T(8,128)(2,1)} collective-permute-done((bf16[768,896]{1,0:T(8,128)(2,1)}, bf16[768,896]{1,0:T(8,128)(2,1)}, u32[]{:S(2)}, u32[]{:S(2)}) %collective-permute-start.2) | collective-permute-done | bytes 1376288 | tf_op jit(solution)/shard_map/ppermute | solution.py:393
  198.0 3.0 collective-permute-start.13
  200.9 0.0 collective-permute-done.1.refs_2_
  200.9 0.7 collective-permute-start.14
  201.6 26.7 %collective-permute-done.4.refs_5_ = bf16[768,896]{1,0:T(8,128)(2,1)} collective-permute-done((bf16[768,896]{1,0:T(8,128)(2,1)S(1)}, bf16[768,896]{1,0:T(8,128)(2,1)}, u32[]{:S(2)}, u32[]{:S(2)}) %collective-permute-start.4) | collective-permute-done | bytes 1376288 | tf_op jit(solution)/shard_map/ppermute | solution.py:393
  228.3 0.0 collective-permute-done.5.refs_6_
  228.3 12.7 %hidden.1 = (f32[1536,256]{1,0:T(8,128)}, f32[1536,256]{1,0:T(8,128)}, bf16[1536,256]{1,0:T(8,128)(2,1)}) custom-call(s32[1]{0:T(128)} %bitcast.5.dp, bf16[1536,896]{1,0:T(8,128)(2,1)} %bitcast.24, bf16[768,896]{1,0:T(8,128)(2,1)} %copy-done.4, bf16[768,896]{1,0:T(8,128)(2,1)} %collective-permute-done.1.refs_2_, ...), custom_call_target="tpu_custom_call" | custom-call | flops 5637144576 | bytes 18350080 | tf_op jit(solution)/shard_map/hidden/pallas_call | solution.py:167
  241.0 4.2 collective-permute-done.12.h1
  245.2 17.8 %collective-permute-done.13.h2 = bf16[1536,256]{1,0:T(8,128)(2,1)} collective-permute-done((bf16[1536,256]{1,0:T(8,128)(2,1)}, bf16[1536,256]{1,0:T(8,128)(2,1)}, u32[]{:S(2)}, u32[]{:S(2)}) %collective-permute-start.13) | collective-permute-done | bytes 786464 | tf_op jit(solution)/shard_map/ppermute | solution.py:393
  262.9 0.0 collective-permute-done.14.h3
  262.9 12.1 %weight_grads.1 = bf16[3584,256]{1,0:T(8,128)(2,1)} custom-call(s32[1]{0:T(128)} %bitcast.5.dp, bf16[1536,256]{1,0:T(8,128)(2,1)} %get-tuple-element.21.h0, bf16[1536,256]{1,0:T(8,128)(2,1)} %collective-permute-done.12.h1, bf16[1536,256]{1,0:T(8,128)(2,1)} %collective-permute-done.13.h2, bf16[1536,256]{1,0:T(8,128)(2,1)} %collective-permute-done.14.h3, ...), custom_call_target="tpu_custom_call" | custom-call | flops 2818572288 | bytes 19398656 | tf_op jit(solution)/shard_map/weight_grads/pallas_call | solution.py:238
  275.0 0.0 all-to-all-done.3.gate
  275.0 1.3 copy-done.3
  276.4 8.1 %all-to-all-start.5 = ((bf16[32,112,256]{2,1,0:T(8,128)(2,1)}), bf16[32,112,256]{2,1,0:T(8,128)(2,1)S(1)}, u32[]{:S(2)}, u32[]{:S(2)}) async-start(bf16[32,112,256]{2,1,0:T(8,128)(2,1)} %bitcast.28), calls=%async_computation.5 | async-start | bytes 3670016 | tf_op jit(solution)/shard_map/all_to_all | solution.py:389
  284.5 0.1 fusion.1
  284.6 1.6 collective-permute-start.9
  286.2 0.0 collective-permute-start.6
  286.2 0.0 collective-permute-start.7
  286.2 2.7 collective-permute-start.8
  288.9 6.2 %collective-permute-done.9.refs_4_ = bf16[768,256]{1,0:T(8,128)(2,1)S(1)} collective-permute-done((bf16[768,256]{1,0:T(8,128)(2,1)S(1)}, bf16[768,256]{1,0:T(8,128)(2,1)S(1)}, u32[]{:S(2)}, u32[]{:S(2)}) %collective-permute-start.9) | collective-permute-done | bytes 393248 | tf_op jit(solution)/shard_map/ppermute | solution.py:393
  295.1 2.7 collective-permute-start.11
  297.8 0.0 collective-permute-done.6.refs_1_
  297.8 0.0 collective-permute-start.10
  297.8 8.1 %collective-permute-done.7.refs_2_ = bf16[768,256]{1,0:T(8,128)(2,1)S(1)} collective-permute-done((bf16[768,256]{1,0:T(8,128)(2,1)S(1)}, bf16[768,256]{1,0:T(8,128)(2,1)S(1)}, u32[]{:S(2)}, u32[]{:S(2)}) %collective-permute-start.7) | collective-permute-done | bytes 393248 | tf_op jit(solution)/shard_map/ppermute | solution.py:393
  306.0 0.0 collective-permute-done.8.refs_3_
  306.0 6.1 %collective-permute-done.11.refs_6_ = bf16[768,256]{1,0:T(8,128)(2,1)S(1)} collective-permute-done((bf16[768,256]{1,0:T(8,128)(2,1)S(1)}, bf16[768,256]{1,0:T(8,128)(2,1)S(1)}, u32[]{:S(2)}, u32[]{:S(2)}) %collective-permute-start.11) | collective-permute-done | bytes 393248 | tf_op jit(solution)/shard_map/ppermute | solution.py:393
  312.0 0.7 copy-done.10
  312.8 1.7 collective-permute-done.10.refs_5_
  314.5 7.7 %outputs.1 = bf16[1536,896]{1,0:T(8,128)(2,1)} custom-call(s32[1]{0:T(128)} %bitcast.5.dp, bf16[1536,256]{1,0:T(8,128)(2,1)} %get-tuple-element.19.refs_0_, bf16[768,256]{1,0:T(8,128)(2,1)} %copy-done.7, bf16[768,256]{1,0:T(8,128)(2,1)} %copy-done.8, bf16[768,256]{1,0:T(8,128)(2,1)} %copy-done.9, bf16[768,256]{1,0:T(8,128)(2,1)} %copy-done.6, ...), custom_call_target="tpu_custom_call" | custom-call | flops 2818572288 | bytes 5898240 | tf_op jit(solution)/shard_map/outputs/pallas_call | solution.py:262
  322.2 0.0 all-to-all-done.5.grads
  322.2 0.0 copy-start.2
  322.2 1.2 copy-done.2
  323.4 8.4 %all-to-all-start.1 = ((bf16[32,48,896]{2,1,0:T(8,128)(2,1)}), bf16[32,48,896]{2,1,0:T(8,128)(2,1)S(1)}, u32[]{:S(2)}, u32[]{:S(2)}) async-start(bf16[32,48,896]{2,1,0:T(8,128)(2,1)} %bitcast.29), calls=%async_computation.1 | async-start | bytes 5505024 | tf_op jit(solution)/shard_map/all_to_all | solution.py:389
  331.8 8.2 %update.1 = bf16[32,2,112,256]{3,2,1,0:T(8,128)(2,1)} custom-call(s32[32]{0:T(128)} %plan.3, s32[32]{0:T(128)} %placement.1, bf16[32,112,256]{2,1,0:T(8,128)(2,1)} %copy-done.2, bf16[32,336,256]{2,1,0:T(8,128)(2,1)} %all-to-all-done.2.x.first.second, bf16[32,336,256]{2,1,0:T(8,128)(2,1)} %all-to-all-done.2.x.first.second), custom_call_target="tpu_custom_call" | custom-call | flops 18350080 | bytes 10485760 | tf_op jit(solution)/shard_map/update/pallas_call | solution.py:349
  340.0 27.1 %all-to-all-done.1 = bf16[32,48,896]{2,1,0:T(8,128)(2,1)S(1)} async-done(((bf16[32,48,896]{2,1,0:T(8,128)(2,1)}), bf16[32,48,896]{2,1,0:T(8,128)(2,1)S(1)}, u32[]{:S(2)}, u32[]{:S(2)}) %all-to-all-start.1) | async-done | bytes 2752544 | tf_op jit(solution)/shard_map/all_to_all | solution.py:389
  367.1 1.5 copy-done.1
  368.6 5.4 %all-to-all-start.6 = ((bf16[32,2,112,256]{3,2,1,0:T(8,128)(2,1)}), bf16[32,2,112,256]{3,2,1,0:T(8,128)(2,1)}, u32[]{:S(2)}, u32[]{:S(2)}) async-start(bf16[32,2,112,256]{3,2,1,0:T(8,128)(2,1)} %update.1), calls=%async_computation.6 | async-start | bytes 7340032 | tf_op jit(solution)/shard_map/all_to_all | solution.py:389
  374.0 3.7 combine.1
  377.7 42.0 %all-to-all-done.6.moments = bf16[32,2,112,256]{3,2,1,0:T(8,128)(2,1)} async-done(((bf16[32,2,112,256]{3,2,1,0:T(8,128)(2,1)}), bf16[32,2,112,256]{3,2,1,0:T(8,128)(2,1)}, u32[]{:S(2)}, u32[]{:S(2)}) %all-to-all-start.6) | async-done | bytes 3670048 | tf_op jit(solution)/shard_map/all_to_all | solution.py:389
  419.8 7.8 %finish.1 = (bf16[32,112,256]{2,1,0:T(8,128)(2,1)}, bf16[32,112,256]{2,1,0:T(8,128)(2,1)}, bf16[32,112,256]{2,1,0:T(8,128)(2,1)}) custom-call(bf16[32,112,256]{2,1,0:T(8,128)(2,1)} %copy-done.3, bf16[32,2,112,256]{3,2,1,0:T(8,128)(2,1)} %all-to-all-done.6.moments), custom_call_target="tpu_custom_call" | custom-call | flops 18350080 | bytes 12582912 | tf_op jit(solution)/shard_map/finish/pallas_call | solution.py:377
  (16 shorter events, 0.0 us)
Async XLA Ops:
  5.7 43.9 %all-to-all-start = ((bf16[32,48,896]{2,1,0:T(8,128)(2,1)}), bf16[32,48,896]{2,1,0:T(8,128)(2,1)S(1)}, u32[]{:S(2)}, u32[]{:S(2)}) async-start(bf16[32,48,896]{2,1,0:T(8,128)(2,1)} %bitcast.30), calls=%async_computation | async-start | bytes 5505024 | tf_op jit(solution)/shard_map/all_to_all | solution.py:389
  49.6 83.6 %copy-start = (bf16[32,48,896]{2,1,0:T(8,128)(2,1)}, bf16[32,48,896]{2,1,0:T(8,128)(2,1)S(1)}, u32[]{:S(2)}) copy-start(bf16[32,48,896]{2,1,0:T(8,128)(2,1)S(1)} %all-to-all-done) | copy-start | bytes 8257540
  49.6 73.3 %all-to-all-start.2 = ((bf16[32,336,256]{2,1,0:T(8,128)(2,1)}), bf16[32,336,256]{2,1,0:T(8,128)(2,1)}, u32[]{:S(2)}, u32[]{:S(2)}) async-start(bf16[32,336,256]{2,1,0:T(8,128)(2,1)} %pad_maximum_fusion), calls=%async_computation.2 | async-start | bytes 11010048 | tf_op jit(solution)/shard_map/all_to_all | solution.py:389
  122.9 52.6 %all-to-all-start.4 = ((bf16[32,48,896]{2,1,0:T(8,128)(2,1)}), bf16[32,48,896]{2,1,0:T(8,128)(2,1)}, u32[]{:S(2)}, u32[]{:S(2)}) async-start(bf16[32,48,896]{2,1,0:T(8,128)(2,1)} %bitcast.26), calls=%async_computation.4 | async-start | bytes 5505024 | tf_op jit(solution)/shard_map/all_to_all | solution.py:389
  135.0 34.2 %collective-permute-start = (bf16[768,896]{1,0:T(8,128)(2,1)}, bf16[768,896]{1,0:T(8,128)(2,1)S(1)}, u32[]{:S(2)}, u32[]{:S(2)}) collective-permute-start(bf16[768,896]{1,0:T(8,128)(2,1)} %bitcast.8), channel_id=1, source_target_pairs={{0,32},{32,64},{64,96},{96,0},{1,33},{33,65},{65,97},{97,1},{2,34}... | collective-permute-start | bytes 4128776 | tf_op jit(solution)/shard_map/ppermute | solution.py:393
  136.6 32.6 %collective-permute-start.3 = (bf16[768,896]{1,0:T(8,128)(2,1)}, bf16[768,896]{1,0:T(8,128)(2,1)}, u32[]{:S(2)}, u32[]{:S(2)}) collective-permute-start(bf16[768,896]{1,0:T(8,128)(2,1)} %bitcast.9), channel_id=1, source_target_pairs={{0,96},{32,0},{64,32},{96,64},{1,97},{33,1},{65,33},{97,65},{2,98}... | collective-permute-start | bytes 4128776 | tf_op jit(solution)/shard_map/ppermute | solution.py:393
  138.8 59.2 %collective-permute-start.2 = (bf16[768,896]{1,0:T(8,128)(2,1)}, bf16[768,896]{1,0:T(8,128)(2,1)}, u32[]{:S(2)}, u32[]{:S(2)}) collective-permute-start(bf16[768,896]{1,0:T(8,128)(2,1)} %bitcast.8), channel_id=1, source_target_pairs={{0,96},{32,0},{64,32},{96,64},{1,97},{33,1},{65,33},{97,65},{2,98}... | collective-permute-start | bytes 4128776 | tf_op jit(solution)/shard_map/ppermute | solution.py:393
  140.2 60.7 %collective-permute-start.1 = (bf16[768,896]{1,0:T(8,128)(2,1)}, bf16[768,896]{1,0:T(8,128)(2,1)}, u32[]{:S(2)}, u32[]{:S(2)}) collective-permute-start(bf16[768,896]{1,0:T(8,128)(2,1)} %bitcast.9), channel_id=1, source_target_pairs={{0,32},{32,64},{64,96},{96,0},{1,33},{33,65},{65,97},{97,1},{2,34}... | collective-permute-start | bytes 4128776 | tf_op jit(solution)/shard_map/ppermute | solution.py:393
  169.2 6.2 %copy-start.4 = (bf16[768,896]{1,0:T(8,128)(2,1)}, bf16[768,896]{1,0:T(8,128)(2,1)S(1)}, u32[]{:S(2)}) copy-start(bf16[768,896]{1,0:T(8,128)(2,1)S(1)} %collective-permute-done.refs_1_) | copy-start | bytes 4128772
  169.2 59.1 %collective-permute-start.4 = (bf16[768,896]{1,0:T(8,128)(2,1)S(1)}, bf16[768,896]{1,0:T(8,128)(2,1)}, u32[]{:S(2)}, u32[]{:S(2)}) collective-permute-start(bf16[768,896]{1,0:T(8,128)(2,1)S(1)} %collective-permute-done.refs_1_), channel_id=1, source_target_pairs={{0,32},{32,64},{64,96},{96,0},{1,33},{33,65},{65,97},{97,1},{2,34}... | collective-permute-start | bytes 4128776 | tf_op jit(solution)/shard_map/ppermute | solution.py:393
  169.2 59.1 %collective-permute-start.5 = (bf16[768,896]{1,0:T(8,128)(2,1)}, bf16[768,896]{1,0:T(8,128)(2,1)}, u32[]{:S(2)}, u32[]{:S(2)}) collective-permute-start(bf16[768,896]{1,0:T(8,128)(2,1)} %collective-permute-done.3.refs_4_), channel_id=1, source_target_pairs={{0,96},{32,0},{64,32},{96,64},{1,97},{33,1},{65,33},{97,65},{2,98}... | collective-permute-start | bytes 4128776 | tf_op jit(solution)/shard_map/ppermute | solution.py:393
  175.4 99.6 %all-to-all-start.3 = ((bf16[32,112,256]{2,1,0:T(8,128)(2,1)}), bf16[32,112,256]{2,1,0:T(8,128)(2,1)S(1)}, u32[]{:S(2)}, u32[]{:S(2)}) async-start(bf16[32,112,256]{2,1,0:T(8,128)(2,1)} %migrate.1), calls=%async_computation.3 | async-start | bytes 3670016 | tf_op jit(solution)/shard_map/all_to_all | solution.py:389
  191.4 53.8 %collective-permute-start.12 = (bf16[1536,256]{1,0:T(8,128)(2,1)}, bf16[1536,256]{1,0:T(8,128)(2,1)}, u32[]{:S(2)}, u32[]{:S(2)}) collective-permute-start(bf16[1536,256]{1,0:T(8,128)(2,1)} %get-tuple-element.22), channel_id=1, source_target_pairs={{0,32},{32,64},{64,96},{96,0},{1,33},{33,65},{65,97},{97,1},{2,34}... | collective-permute-start | bytes 2359304 | tf_op jit(solution)/shard_map/ppermute | solution.py:393
  198.0 65.0 %collective-permute-start.13 = (bf16[1536,256]{1,0:T(8,128)(2,1)}, bf16[1536,256]{1,0:T(8,128)(2,1)}, u32[]{:S(2)}, u32[]{:S(2)}) collective-permute-start(bf16[1536,256]{1,0:T(8,128)(2,1)} %get-tuple-element.23), channel_id=1, source_target_pairs={{0,64},{32,96},{64,0},{96,32},{1,65},{33,97},{65,1},{97,33},{2,66}... | collective-permute-start | bytes 2359304 | tf_op jit(solution)/shard_map/ppermute | solution.py:393
  200.9 62.0 %collective-permute-start.14 = (bf16[1536,256]{1,0:T(8,128)(2,1)}, bf16[1536,256]{1,0:T(8,128)(2,1)}, u32[]{:S(2)}, u32[]{:S(2)}) collective-permute-start(bf16[1536,256]{1,0:T(8,128)(2,1)} %get-tuple-element.24), channel_id=1, source_target_pairs={{0,96},{32,0},{64,32},{96,64},{1,97},{33,1},{65,33},{97,65},{2,98}... | collective-permute-start | bytes 2359304 | tf_op jit(solution)/shard_map/ppermute | solution.py:393
  275.0 1.3 copy-start.3
  275.0 9.5 %copy-start.5 = (bf16[1536,256]{1,0:T(8,128)(2,1)S(1)}, bf16[1536,256]{1,0:T(8,128)(2,1)}, u32[]{:S(2)}) copy-start(bf16[1536,256]{1,0:T(8,128)(2,1)} %get-tuple-element.19.refs_0_) | copy-start | bytes 2359300
  276.4 45.8 %all-to-all-start.5 = ((bf16[32,112,256]{2,1,0:T(8,128)(2,1)}), bf16[32,112,256]{2,1,0:T(8,128)(2,1)S(1)}, u32[]{:S(2)}, u32[]{:S(2)}) async-start(bf16[32,112,256]{2,1,0:T(8,128)(2,1)} %bitcast.28), calls=%async_computation.5 | async-start | bytes 3670016 | tf_op jit(solution)/shard_map/all_to_all | solution.py:389
  284.6 10.5 %collective-permute-start.9 = (bf16[768,256]{1,0:T(8,128)(2,1)S(1)}, bf16[768,256]{1,0:T(8,128)(2,1)S(1)}, u32[]{:S(2)}, u32[]{:S(2)}) collective-permute-start(bf16[768,256]{1,0:T(8,128)(2,1)S(1)} %get-tuple-element.32), channel_id=1, source_target_pairs={{0,96},{32,0},{64,32},{96,64},{1,97},{33,1},{65,33},{97,65},{2,98}... | collective-permute-start | bytes 1179656 | tf_op jit(solution)/shard_map/ppermute | solution.py:393
  286.2 11.7 %collective-permute-start.6 = (bf16[768,256]{1,0:T(8,128)(2,1)S(1)}, bf16[768,256]{1,0:T(8,128)(2,1)S(1)}, u32[]{:S(2)}, u32[]{:S(2)}) collective-permute-start(bf16[768,256]{1,0:T(8,128)(2,1)S(1)} %get-tuple-element.33), channel_id=1, source_target_pairs={{0,32},{32,64},{64,96},{96,0},{1,33},{33,65},{65,97},{97,1},{2,34}... | collective-permute-start | bytes 1179656 | tf_op jit(solution)/shard_map/ppermute | solution.py:393
  286.2 19.8 %collective-permute-start.7 = (bf16[768,256]{1,0:T(8,128)(2,1)S(1)}, bf16[768,256]{1,0:T(8,128)(2,1)S(1)}, u32[]{:S(2)}, u32[]{:S(2)}) collective-permute-start(bf16[768,256]{1,0:T(8,128)(2,1)S(1)} %get-tuple-element.32), channel_id=1, source_target_pairs={{0,32},{32,64},{64,96},{96,0},{1,33},{33,65},{65,97},{97,1},{2,34}... | collective-permute-start | bytes 1179656 | tf_op jit(solution)/shard_map/ppermute | solution.py:393
  286.2 19.8 %collective-permute-start.8 = (bf16[768,256]{1,0:T(8,128)(2,1)S(1)}, bf16[768,256]{1,0:T(8,128)(2,1)S(1)}, u32[]{:S(2)}, u32[]{:S(2)}) collective-permute-start(bf16[768,256]{1,0:T(8,128)(2,1)S(1)} %get-tuple-element.33), channel_id=1, source_target_pairs={{0,96},{32,0},{64,32},{96,64},{1,97},{33,1},{65,33},{97,65},{2,98}... | collective-permute-start | bytes 1179656 | tf_op jit(solution)/shard_map/ppermute | solution.py:393
  295.1 19.4 %copy-start.6 = (bf16[768,256]{1,0:T(8,128)(2,1)}, bf16[768,256]{1,0:T(8,128)(2,1)S(1)}, u32[]{:S(2)}) copy-start(bf16[768,256]{1,0:T(8,128)(2,1)S(1)} %collective-permute-done.9.refs_4_) | copy-start | bytes 1179652
  295.1 17.0 %collective-permute-start.11 = (bf16[768,256]{1,0:T(8,128)(2,1)S(1)}, bf16[768,256]{1,0:T(8,128)(2,1)S(1)}, u32[]{:S(2)}, u32[]{:S(2)}) collective-permute-start(bf16[768,256]{1,0:T(8,128)(2,1)S(1)} %collective-permute-done.9.refs_4_), channel_id=1, source_target_pairs={{0,96},{32,0},{64,32},{96,64},{1,97},{33,1},{65,33},{97,65},{2,98}... | collective-permute-start | bytes 1179656 | tf_op jit(solution)/shard_map/ppermute | solution.py:393
  297.8 16.7 %copy-start.7 = (bf16[768,256]{1,0:T(8,128)(2,1)}, bf16[768,256]{1,0:T(8,128)(2,1)S(1)}, u32[]{:S(2)}) copy-start(bf16[768,256]{1,0:T(8,128)(2,1)S(1)} %collective-permute-done.6.refs_1_) | copy-start | bytes 1179652
  297.8 16.7 %collective-permute-start.10 = (bf16[768,256]{1,0:T(8,128)(2,1)S(1)}, bf16[768,256]{1,0:T(8,128)(2,1)}, u32[]{:S(2)}, u32[]{:S(2)}) collective-permute-start(bf16[768,256]{1,0:T(8,128)(2,1)S(1)} %collective-permute-done.6.refs_1_), channel_id=1, source_target_pairs={{0,32},{32,64},{64,96},{96,0},{1,33},{33,65},{65,97},{97,1},{2,34}... | collective-permute-start | bytes 1179656 | tf_op jit(solution)/shard_map/ppermute | solution.py:393
  306.0 8.5 %copy-start.8 = (bf16[768,256]{1,0:T(8,128)(2,1)}, bf16[768,256]{1,0:T(8,128)(2,1)S(1)}, u32[]{:S(2)}) copy-start(bf16[768,256]{1,0:T(8,128)(2,1)S(1)} %collective-permute-done.7.refs_2_) | copy-start | bytes 1179652
  306.0 8.5 %copy-start.9 = (bf16[768,256]{1,0:T(8,128)(2,1)}, bf16[768,256]{1,0:T(8,128)(2,1)S(1)}, u32[]{:S(2)}) copy-start(bf16[768,256]{1,0:T(8,128)(2,1)S(1)} %collective-permute-done.8.refs_3_) | copy-start | bytes 1179652
  312.0 0.7 copy-start.10
  322.2 1.2 copy-start.2
  323.4 43.7 %all-to-all-start.1 = ((bf16[32,48,896]{2,1,0:T(8,128)(2,1)}), bf16[32,48,896]{2,1,0:T(8,128)(2,1)S(1)}, u32[]{:S(2)}, u32[]{:S(2)}) async-start(bf16[32,48,896]{2,1,0:T(8,128)(2,1)} %bitcast.29), calls=%async_computation.1 | async-start | bytes 5505024 | tf_op jit(solution)/shard_map/all_to_all | solution.py:389
  367.1 1.5 copy-start.1
  368.6 51.2 %all-to-all-start.6 = ((bf16[32,2,112,256]{3,2,1,0:T(8,128)(2,1)}), bf16[32,2,112,256]{3,2,1,0:T(8,128)(2,1)}, u32[]{:S(2)}, u32[]{:S(2)}) async-start(bf16[32,2,112,256]{3,2,1,0:T(8,128)(2,1)} %update.1), calls=%async_computation.6 | async-start | bytes 7340032 | tf_op jit(solution)/shard_map/all_to_all | solution.py:389
where the time goes:
time: 429 us; the launch traced here: 428 us
  waiting for transfers between devices  269 us (63%)
  starting transfers between devices  73.9 us (17%)
  Pallas kernels  70 us (16%)
  local copies, waits for them, and re-layouts  7.94 us (2%)
  other arithmetic  5.79 us (1%)
    all_to_all x7, waiting for transfers between devices, exchange(): return lax.all_to_all(x, 'expert', split_axis=0, concat_axis=0, tiled=True)  163 us
    ppermute x15, waiting for transfers between devices, shift(): return lax.ppermute(x, 'dp', [(i, (i + by) % N_DP) for i in range(N_DP)])  106 us
    all_to_all x7, starting transfers between devices, exchange(): return lax.all_to_all(x, 'expert', split_axis=0, concat_axis=0, tiled=True)  55.3 us
    ppermute x15, starting transfers between devices, shift(): return lax.ppermute(x, 'dp', [(i, (i + by) % N_DP) for i in range(N_DP)])  18.6 us
    pallas_call x1, Pallas kernels, hidden_of(): pl.pallas_call(hidden_kernel, grid=(ROWS // block,), out_shape=[jax.Shape...  12.7 us
    pallas_call x1, Pallas kernels, weight_grads(): pl.pallas_call(weight_kernel, grid=(ROWS // block,), out_shape=jax.ShapeD...  12.1 us
  transfers between devices with their start and end apart: 22, of which 13 were waited for; matrix products, arithmetic and copies ran while one was open for 2% of the time, Pallas kernels for 14%

commit v1 on v0

v1 whole, which is shorter than its diff:
```python
import functools
import math

import jax
import jax.numpy as jnp
from jax import lax
from jax.experimental import pallas as pl
from jax.experimental.pallas import tpu as pltpu
from jax.sharding import PartitionSpec as P


D = 3584
FF = 1024
N_DP = 4
SLOTS = 32
CAP = 48
TOK = 128
QD = D // N_DP
QF = FF // N_DP
PART = D // SLOTS
CHUNKS = ((0, 16), (16, 48))
ROWS = SLOTS * CAP
HALF = SLOTS // 2

beta_first = 0.9
beta_second = 0.95
learn_rate = 0.02
weight_decay = 0.1
epsilon = 1e-08
scale_in = 1.0 / math.sqrt(D)
scale_mid = 1.0 / math.sqrt(FF)


f32 = jnp.float32
bf16 = jnp.bfloat16
VMEM = pltpu.VMEM
SMEM = pltpu.SMEM


def vspec():
    return pl.BlockSpec(memory_space=VMEM)


def sspec():
    return pl.BlockSpec(memory_space=SMEM)


def cost(flops, nbytes):
    return pl.CostEstimate(flops=flops, transcendentals=0, bytes_accessed=nbytes)


def select_kernel(index, place, routes, weights, tokens, *outs):
    rows_out, (sel_out, selw_out) = outs[: len(CHUNKS)], outs[len(CHUNKS) :]
    me = index[0].astype(f32)
    a = lax.broadcasted_iota(jnp.int32, (SLOTS, SLOTS), 0)
    b = lax.broadcasted_iota(jnp.int32, (SLOTS, SLOTS), 1)
    row = place[...].astype(f32)
    col = jnp.sum(jnp.where(a == b, row, 0.0), axis=1, keepdims=True)
    same = jnp.where(jnp.abs(col - row) < 0.5, 1.0, 0.0)
    copies = jnp.sum(same, axis=1, keepdims=True)
    rank = jnp.sum(jnp.where(b < a, same, 0.0), axis=1, keepdims=True)
    turn = me - copies * jnp.floor((me + 0.5) / copies)
    active = jnp.abs(rank - turn) < 0.5
    hit = jnp.zeros((SLOTS, TOK), f32)
    wt = jnp.zeros((SLOTS, TOK), f32)
    for k in range(routes.shape[0]):
        match = (jnp.abs(routes[k : k + 1, :].astype(f32) - col) < 0.5) & active
        hit = hit + jnp.where(match, 1.0, 0.0)
        wt = wt + jnp.where(match, weights[k : k + 1, :], 0.0)
    t0 = lax.broadcasted_iota(jnp.int32, (TOK, TOK), 0)
    t1 = lax.broadcasted_iota(jnp.int32, (TOK, TOK), 1)
    before = jnp.where(t0 < t1, 1.0, 0.0).astype(bf16)
    pos = jnp.dot(hit.astype(bf16), before, preferred_element_type=f32)
    pos = jnp.where(hit > 0.5, pos, -1.0)
    want = lax.broadcasted_iota(jnp.int32, (CAP, TOK), 0).astype(f32)
    for j in range(SLOTS):
        chosen = jnp.abs(pos[j : j + 1, :] - want) < 0.5
        sel_out[j * CAP : (j + 1) * CAP, :] = jnp.where(chosen, 1.0, 0.0).astype(bf16)
        selw_out[j * CAP : (j + 1) * CAP, :] = jnp.where(chosen, wt[j : j + 1, :], 0.0)
    group = 8
    for j in range(0, SLOTS, group):
        sel = sel_out[j * CAP : (j + group) * CAP, :]
        got = jnp.dot(sel, tokens[...], preferred_element_type=f32).astype(bf16)
        got = got.reshape(group, CAP, QD)
        for (lo, hi), out in zip(CHUNKS, rows_out):
            out[j : j + group] = got[:, lo:hi]


def select_rows(index, placement, routes, weights, tokens):
    return pl.pallas_call(
        select_kernel,
        out_shape=[jax.ShapeDtypeStruct((SLOTS, hi - lo, QD), bf16) for lo, hi in CHUNKS]
        + [jax.ShapeDtypeStruct((ROWS, TOK), bf16), jax.ShapeDtypeStruct((ROWS, TOK), f32)],
        in_specs=[sspec()] + [vspec()] * 4,
        out_specs=[vspec()] * (len(CHUNKS) + 2),
        cost_estimate=cost(2 * ROWS * TOK * QD, 4 << 20),
        name="select_rows",
    )(index, placement[None, :], routes.T, weights.T, tokens)


def scale_kernel(sel, selw, cot, out):
    for r in range(0, SLOTS * CAP, 512):
        w = jnp.sum(selw[r : r + 512, :], axis=1, keepdims=True)
        picked = jnp.dot(sel[r : r + 512, :], cot[...], preferred_element_type=f32)
        out[r : r + 512, :] = (w * picked).astype(bf16)


def scale_rows(sel, selw, cot):
    rows = SLOTS * CAP
    return pl.pallas_call(
        scale_kernel,
        out_shape=jax.ShapeDtypeStruct((rows, QD), bf16),
        in_specs=[vspec()] * 3,
        out_specs=vspec(),
        cost_estimate=cost(2 * rows * TOK * QD, 4 << 20),
        name="scale_rows",
    )(sel, selw, cot)


def row_block(block, width):
    return pl.BlockSpec((block, width), lambda i: (i, 0))


def piece_specs(n, pieces):
    half = HALF // n
    specs = []
    for group in pieces:
        shape = (n,) + group[0].shape[1:]
        own = pl.BlockSpec(shape, lambda i: (i, 0, 0))
        low = pl.BlockSpec(shape, lambda i: (jnp.minimum(i, half - 1), 0, 0))
        high = pl.BlockSpec(shape, lambda i: (jnp.maximum(i - half, 0), 0, 0))
        specs += [own] + [low, high] * 3
    return specs


def whole(shape):
    return pl.BlockSpec(shape, lambda i: (0,) * len(shape))


def gather_pieces(n, dp, pieces, out):
    first = pl.program_id(0) < HALF // n
    at = 0
    for j in range(0, len(pieces), 7):
        own, la, lb, ra, rb, fa, fb = pieces[j : j + 7]
        rows, width = own.shape[1:]
        for shift, x in (
            (0, own[...]),
            (3, jnp.where(first, la[...], lb[...])),
            (1, jnp.where(first, ra[...], rb[...])),
            (2, jnp.where(first, fa[...], fb[...])),
        ):
            q = lax.rem(dp[0] + shift, N_DP)
            out[:, at : at + rows, pl.ds(pl.multiple_of(q * width, width), width)] = x
        at += rows


def flat(pieces):
    return [x for group in pieces for x in group]


HIDDEN_SOURCES = 8


def hidden_kernel(count, dp, *refs):
    pieces, (wg, wu, g_out, u_out, h_out, gathered) = refs[:count], refs[count:]
    gather_pieces(HIDDEN_SOURCES, dp, pieces, gathered)
    x = gathered[...].reshape(HIDDEN_SOURCES * CAP, D)
    g = jnp.dot(x, wg[...], preferred_element_type=f32) * scale_in
    u = jnp.dot(x, wu[...], preferred_element_type=f32) * scale_in
    g_out[...] = g
    u_out[...] = u
    h_out[...] = (g / (1.0 + jnp.exp(-g)) * u).astype(bf16)


def hidden_of(dp, pieces, wg, wu):
    n = HIDDEN_SOURCES
    block = n * CAP
    inputs = flat(pieces)
    return pl.pallas_call(
        functools.partial(hidden_kernel, len(inputs)),
        grid=(SLOTS // n,),
        out_shape=[
            jax.ShapeDtypeStruct((ROWS, QF), f32),
            jax.ShapeDtypeStruct((ROWS, QF), f32),
            jax.ShapeDtypeStruct((ROWS, QF), bf16),
        ],
        in_specs=[sspec()] + piece_specs(n, pieces) + [whole((D, QF)), whole((D, QF))],
        out_specs=[row_block(block, QF)] * 3,
        scratch_shapes=[VMEM((n, CAP, D), bf16)],
        cost_estimate=cost(4 * ROWS * D * QF, ROWS * D * 2 + 8 * D * QF),
        name="hidden",
    )(dp, *inputs, wg, wu)


PARTIAL_BLOCK = 384


def partial_kernel(dp, x, wd, *outs):
    for k, out in enumerate(outs):
        q = lax.rem(dp[0] + k, N_DP)
        out[...] = lax.dot_general(
            x[...],
            wd[pl.ds(pl.multiple_of(q * QF, QF), QF), :],
            (((1,), (1,)), ((), ())),
            preferred_element_type=f32,
        ).astype(bf16)


def partial_grads(dp, x, wd):
    block = PARTIAL_BLOCK
    return pl.pallas_call(
        partial_kernel,
        grid=(ROWS // block,),
        out_shape=[jax.ShapeDtypeStruct((ROWS, QF), bf16)] * N_DP,
        in_specs=[sspec(), row_block(block, QD), whole((FF, QD))],
        out_specs=[row_block(block, QF)] * N_DP,
        cost_estimate=cost(2 * ROWS * QD * FF, 6 << 20),
        name="partial_grads",
    )(dp, x, wd)


WEIGHT_SOURCES = 16


def weight_kernel(count, dp, h0, h1, h2, h3, g_in, u_in, *refs):
    pieces, (out, gathered, acc) = refs[:count], refs[count:]
    i = pl.program_id(0)
    gather_pieces(WEIGHT_SOURCES, dp, pieces, gathered)
    x = gathered[...].reshape(WEIGHT_SOURCES * CAP, D)
    grad = h0[...].astype(f32) + h1[...].astype(f32) + h2[...].astype(f32) + h3[...].astype(f32)
    grad = grad * scale_mid
    g = g_in[...]
    s = 1.0 / (1.0 + jnp.exp(-g))
    gg = (grad * u_in[...] * s * (1.0 + g * (1.0 - s))).astype(bf16)
    part = lax.dot_general(gg, x, (((0,), (0,)), ((), ())), preferred_element_type=f32)

    @pl.when(i == 0)
    def _():
        acc[...] = part

    @pl.when(i == pl.num_programs(0) - 1)
    def _():
        for r in range(0, D, 512):
            total = (acc[:, r : r + 512] + part[:, r : r + 512]) * scale_in
            out[r : r + 512, :] = total.T.astype(bf16)


def weight_grads(dp, hg, g, u, pieces):
    n = WEIGHT_SOURCES
    block = n * CAP
    inputs = flat(pieces)
    assert SLOTS // n == 2
    return pl.pallas_call(
        functools.partial(weight_kernel, len(inputs)),
        grid=(SLOTS // n,),
        out_shape=jax.ShapeDtypeStruct((D, QF), bf16),
        in_specs=[sspec()] + [row_block(block, QF)] * 6 + piece_specs(n, pieces),
        out_specs=whole((D, QF)),
        scratch_shapes=[VMEM((n, CAP, D), bf16), VMEM((QF, D), f32)],
        cost_estimate=cost(2 * ROWS * D * QF, ROWS * D * 2 + (8 << 20)),
        name="weight_grads",
    )(dp, *hg, g, u, *inputs)


OUTPUT_SOURCES = 8


def output_kernel(count, dp, *refs):
    pieces, (wd, out, gathered) = refs[:count], refs[count:]
    gather_pieces(OUTPUT_SOURCES, dp, pieces, gathered)
    x = gathered[...].reshape(OUTPUT_SOURCES * CAP, FF)
    total = jnp.dot(x, wd[...], preferred_element_type=f32)
    out[...] = (total * scale_mid).astype(bf16)


def outputs_of(dp, pieces, wd):
    n = OUTPUT_SOURCES
    inputs = flat(pieces)
    return pl.pallas_call(
        functools.partial(output_kernel, len(inputs)),
        grid=(SLOTS // n,),
        out_shape=jax.ShapeDtypeStruct((ROWS, QD), bf16),
        in_specs=[sspec()] + piece_specs(n, pieces) + [whole((FF, QD))],
        out_specs=row_block(n * CAP, QD),
        scratch_shapes=[VMEM((n, CAP, FF), bf16)],
        cost_estimate=cost(2 * ROWS * FF * QD, ROWS * (FF + QD) * 2),
        name="outputs",
    )(dp, *inputs, wd)


def combine_kernel(selw, *refs):
    out = refs[-1]
    total = jnp.zeros(out.shape, f32)
    base = 0
    for ref in refs[:-1]:
        n = ref.shape[0]
        w = selw[base : base + n, :]
        high = w.astype(bf16)
        low = (w - high.astype(f32)).astype(bf16)
        rows = ref[...]
        for part in (high, low):
            total = total + lax.dot_general(
                part, rows, (((0,), (0,)), ((), ())), preferred_element_type=f32
            )
        base += n
    out[...] = total.astype(bf16)


def combine(selw, rows):
    return pl.pallas_call(
        combine_kernel,
        out_shape=jax.ShapeDtypeStruct((TOK, QD), bf16),
        in_specs=[vspec()] * (1 + len(rows)),
        out_specs=vspec(),
        cost_estimate=cost(4 * SLOTS * CAP * TOK * QD, 4 << 20),
        name="combine",
    )(selw, *rows)


UPDATE_ROWS = 16


def update_kernel(plan, placement, grads, gate, first, second, out, total):
    total[...] = jnp.zeros_like(total)
    for s in range(SLOTS):
        total[placement[s]] += grads[s].astype(f32)

    def body(s, carry):
        p = plan[s]
        g = total[placement[p]]
        one = beta_first * first[p].astype(f32) + (1.0 - beta_first) * g
        two = beta_second * second[p].astype(f32) + (1.0 - beta_second) * g * g
        kept = gate[p].astype(f32) * (1.0 - learn_rate * weight_decay)
        out[s, 0] = (kept - learn_rate * one / (jnp.sqrt(two) + epsilon)).astype(bf16)
        out[s, 1] = one.astype(bf16)
        out[s, 2] = two.astype(bf16)
        return carry

    lax.fori_loop(0, SLOTS, body, 0, unroll=4)


def update(plan, placement, grads, states):
    steps = PART // UPDATE_ROWS

    def part(n):
        return pl.BlockSpec((SLOTS, UPDATE_ROWS, QF), lambda i, *_: (0, n * steps + i, 0))

    return pl.pallas_call(
        update_kernel,
        grid_spec=pltpu.PrefetchScalarGridSpec(
            num_scalar_prefetch=2,
            grid=(steps,),
            in_specs=[part(0), part(0), part(1), part(2)],
            out_specs=pl.BlockSpec((SLOTS, 3, UPDATE_ROWS, QF), lambda i, *_: (0, 0, i, 0)),
            scratch_shapes=[VMEM((SLOTS, UPDATE_ROWS, QF), f32)],
        ),
        out_shape=jax.ShapeDtypeStruct((SLOTS, 3, PART, QF), bf16),
        cost_estimate=cost(20 * D * SLOTS * QF // SLOTS, 10 << 20),
        name="update",
    )(plan, placement, grads, states, states, states)


def finish_kernel(moments, *outs):
    for k, out in enumerate(outs):
        out[...] = moments[:, k]


def finish(moments):
    n = 8
    part = pl.BlockSpec((n, PART, QF), lambda i: (i, 0, 0))
    return pl.pallas_call(
        finish_kernel,
        grid=(SLOTS // n,),
        out_shape=[jax.ShapeDtypeStruct((SLOTS, PART, QF), bf16)] * 3,
        in_specs=[pl.BlockSpec((n, 3, PART, QF), lambda i: (i, 0, 0, 0))],
        out_specs=[part] * 3,
        cost_estimate=cost(0, 12 << 20),
        name="finish",
    )(moments)


def exchange(x):
    return lax.all_to_all(x, "expert", split_axis=0, concat_axis=0, tiled=True)


def shift(x, by):
    return lax.ppermute(x, "dp", [(i, (i + by) % N_DP) for i in range(N_DP)])


def ring(x):
    low, high = x[:HALF], x[HALF:]
    la = shift(low, 1)
    rb = shift(high, -1)
    lb = shift(high, 1)
    ra = shift(low, -1)
    fa = shift(la, 1)
    fb = shift(rb, -1)
    return (x, la, lb, ra, rb, fa, fb)


def device_step(
    tokens,
    cotangent,
    routes,
    route_weight,
    gate_weight,
    up_weight,
    down_weight,
    first_moment,
    second_moment,
    placement,
    migration_plan,
):
    index = lax.axis_index("expert").astype(jnp.int32)[None]
    dp = lax.axis_index("dp").astype(jnp.int32)[None]
    wg, wu, wd = gate_weight[0], up_weight[0], down_weight[0]
    *rows, sel, selw = select_rows(index, placement, routes, route_weight, tokens)
    got = [exchange(x) for x in rows]
    sent_grads = scale_rows(sel, selw, cotangent)
    got_grads = exchange(sent_grads.reshape(SLOTS, CAP, QD)).reshape(ROWS, QD)
    packed = jnp.concatenate(
        [x[0].reshape(SLOTS, PART, QF) for x in (gate_weight, first_moment, second_moment)],
        axis=1,
    )
    states = exchange(packed)
    pieces = [ring(x) for x in got]
    g, u, h = hidden_of(dp, pieces, wg, wu)
    partials = partial_grads(dp, got_grads, wd)
    hg = [partials[0]] + [shift(partials[k], k) for k in range(1, N_DP)]
    wgrad = weight_grads(dp, hg, g, u, pieces)
    got_wgrad = exchange(wgrad.reshape(SLOTS, PART, QF))
    moments = exchange(update(migration_plan, placement, got_wgrad, states))
    out = outputs_of(dp, [ring(h.reshape(SLOTS, CAP, QF))], wd)
    returned = exchange(out.reshape(SLOTS, CAP, QD)).reshape(ROWS, QD)
    layer_output = combine(selw, [returned])
    results = finish(moments)
    return (layer_output,) + tuple(r.reshape(1, D, QF) for r in results)


def solution(mesh):
    placed = (
        P("expert", "dp"),
        P("expert", "dp"),
        P("expert", None),
        P("expert", None),
        P("expert", None, "dp"),
        P("expert", None, "dp"),
        P("expert", None, "dp"),
        P("expert", None, "dp"),
        P("expert", None, "dp"),
        P(),
        P(),
    )
    return jax.shard_map(
        device_step,
        mesh=mesh,
        in_specs=placed,
        out_specs=(
            P("expert", "dp"),
            P("expert", None, "dp"),
            P("expert", None, "dp"),
            P("expert", None, "dp"),
        ),
        check_vma=False,
    )
```

time: 429 us -> 429 us (level); the launches traced: 428 us -> 422 us
  blocking collectives: 0 us -> 24.1 us
  starting transfers between devices: 73.9 us -> 57.7 us
  waiting for transfers between devices: 269 us -> 260 us
    all_to_all x0 -> x1, blocking collectives: none -> 24.1 us  [exchange(): return lax.all_to_all(x, 'expert', split_axis=0, concat_axis=0, tiled=True)]
    all_to_all x7 -> x6, waiting for transfers between devices: 163 us -> 141 us  [exchange(): return lax.all_to_all(x, 'expert', split_axis=0, concat_axis=0, tiled=True)]
    all_to_all x7 -> x6, starting transfers between devices: 55.3 us -> 36.7 us  [exchange(): return lax.all_to_all(x, 'expert', split_axis=0, concat_axis=0, tiled=True)]
    ppermute x15 -> x21, waiting for transfers between devices: 106 us -> 120 us  [shift(): return lax.ppermute(x, 'dp', [(i, (i + by) % N_DP) for i in range(N_DP)])]
    pallas_call x5 -> x4, Pallas kernels: 39.7 us -> 36.2 us  [the longest x1 12.4 us: hidden_of(): pl.pallas_call(functools.partial(hidden_kernel, len(inputs)), grid=(SLOTS...]
    ppermute x15 -> x21, starting transfers between devices: 18.6 us -> 21 us  [shift(): return lax.ppermute(x, 'dp', [(i, (i + by) % N_DP) for i in range(N_DP)])]
  transfers between devices with their start and end apart: 22 -> 27, of which waited for: 13 -> 17; matrix products, arithmetic and copies ran while one was open for 2% -> 2% of each run, Pallas kernels for 14% -> 13%
where the time goes in v1:
time: 429 us; the launch traced here: 422 us
  waiting for transfers between devices  260 us (61%)
  Pallas kernels  65.9 us (15%)
  starting transfers between devices  57.7 us (13%)
  blocking collectives  24.1 us (6%)
  local copies, waits for them, and re-layouts  7.22 us (2%)
  other arithmetic  5.78 us (1%)
    all_to_all x6, waiting for transfers between devices, exchange(): return lax.all_to_all(x, 'expert', split_axis=0, concat_axis=0, tiled=True)  141 us
    ppermute x21, waiting for transfers between devices, shift(): return lax.ppermute(x, 'dp', [(i, (i + by) % N_DP) for i in range(N_DP)])  120 us
    all_to_all x6, starting transfers between devices, exchange(): return lax.all_to_all(x, 'expert', split_axis=0, concat_axis=0, tiled=True)  36.7 us
    all_to_all x1, blocking collectives, exchange(): return lax.all_to_all(x, 'expert', split_axis=0, concat_axis=0, tiled=True)  24.1 us
    ppermute x21, starting transfers between devices, shift(): return lax.ppermute(x, 'dp', [(i, (i + by) % N_DP) for i in range(N_DP)])  21 us
    pallas_call x1, Pallas kernels, hidden_of(): pl.pallas_call(functools.partial(hidden_kernel, len(inputs)), grid=(SLOTS...  12.4 us
    pallas_call x1, Pallas kernels, weight_grads(): pl.pallas_call(functools.partial(weight_kernel, len(inputs)), grid=(SLOTS...  12.2 us
    pallas_call x1, Pallas kernels, update(): pl.pallas_call(update_kernel, grid_spec=pltpu.PrefetchScalarGridSpec(num_...  10 us
  transfers between devices with their start and end apart: 27, of which 17 were waited for; matrix products, arithmetic and copies ran while one was open for 2% of the time, Pallas kernels for 13%

profile of v1, /device:TPU:1, one launch (start us, length us, event | category | flops | bytes accessed | tf_op | source)
XLA Modules:
  0.0 422.0 jit_solution(5234131255246408909)
XLA Ops:
  0.6 3.9 select_rows.1
  4.5 24.1 %all_to_all.35.refs_0_ = bf16[32,16,896]{2,1,0:T(8,128)(2,1)S(1)} all-to-all(bf16[32,16,896]{2,1,0:T(8,128)(2,1)} %get-tuple-element.19), channel_id=1, replica_groups=mesh['dp'=4,'expert'=32] {'expert'}, dimensions={0} | all-to-all | bytes 1835008 | tf_op jit(solution)/shard_map/all_to_all | solution.py:383
  28.7 3.9 all-to-all-start.1
  32.6 3.7 scale_rows.1
  36.2 21.8 %all-to-all-done.1.refs_7_ = bf16[32,32,896]{2,1,0:T(8,128)(2,1)S(1)} async-done(((bf16[32,32,896]{2,1,0:T(8,128)(2,1)}), bf16[32,32,896]{2,1,0:T(8,128)(2,1)S(1)}, u32[]{:S(2)}, u32[]{:S(2)}) %all-to-all-start.1) | async-done | bytes 1835040 | tf_op jit(solution)/shard_map/all_to_all | solution.py:383
  58.1 5.1 %all-to-all-start.3 = ((bf16[32,48,896]{2,1,0:T(8,128)(2,1)}), bf16[32,48,896]{2,1,0:T(8,128)(2,1)}, u32[]{:S(2)}, u32[]{:S(2)}) async-start(bf16[32,48,896]{2,1,0:T(8,128)(2,1)} %bitcast.23), calls=%async_computation.3 | async-start | bytes 5505024 | tf_op jit(solution)/shard_map/all_to_all | solution.py:383
  63.2 5.8 %pad_maximum_fusion = bf16[32,336,256]{2,1,0:T(8,128)(2,1)} fusion(bf16[32,112,256]{2,1,0:T(8,128)(2,1)} %bitcast.26, bf16[32,112,256]{2,1,0:T(8,128)(2,1)} %bitcast.27, bf16[32,112,256]{2,1,0:T(8,128)(2,1)} %bitcast.28), kind=kLoop, calls=%fused_computation | loop fusion | flops 16515072 | bytes 11010048 | tf_op jit(solution)/shard_map/concatenate | solution.py:421
  69.0 29.7 %all-to-all-done.3 = bf16[32,48,896]{2,1,0:T(8,128)(2,1)} async-done(((bf16[32,48,896]{2,1,0:T(8,128)(2,1)}), bf16[32,48,896]{2,1,0:T(8,128)(2,1)}, u32[]{:S(2)}, u32[]{:S(2)}) %all-to-all-start.3) | async-done | bytes 2752544 | tf_op jit(solution)/shard_map/all_to_all | solution.py:383
  98.7 5.4 %all-to-all-start.5 = ((bf16[32,336,256]{2,1,0:T(8,128)(2,1)}), bf16[32,336,256]{2,1,0:T(8,128)(2,1)}, u32[]{:S(2)}, u32[]{:S(2)}) async-start(bf16[32,336,256]{2,1,0:T(8,128)(2,1)} %pad_maximum_fusion), calls=%async_computation.5 | async-start | bytes 11010048 | tf_op jit(solution)/shard_map/all_to_all | solution.py:383
  104.1 0.1 fusion.1
  104.2 3.8 collective-permute-start.3
  108.0 1.1 fusion
  109.1 0.1 collective-permute-start.9
  109.2 1.3 collective-permute-start.6
  110.6 0.0 collective-permute-start.1
  110.6 2.7 collective-permute-start.2
  113.2 4.2 %collective-permute-done.3.refs_4_ = bf16[16,16,896]{2,1,0:T(8,128)(2,1)S(1)} collective-permute-done((bf16[16,16,896]{2,1,0:T(8,128)(2,1)S(1)}, bf16[16,16,896]{2,1,0:T(8,128)(2,1)S(1)}, u32[]{:S(2)}, u32[]{:S(2)}) %collective-permute-start.3) | collective-permute-done | bytes 458784 | tf_op jit(solution)/shard_map/ppermute | solution.py:387
  117.5 0.5 collective-permute-start
  118.0 23.3 %collective-permute-done.1.refs_2_ = bf16[16,16,896]{2,1,0:T(8,128)(2,1)S(1)} collective-permute-done((bf16[16,16,896]{2,1,0:T(8,128)(2,1)S(1)}, bf16[16,16,896]{2,1,0:T(8,128)(2,1)S(1)}, u32[]{:S(2)}, u32[]{:S(2)}) %collective-permute-start.1) | collective-permute-done | bytes 458784 | tf_op jit(solution)/shard_map/ppermute | solution.py:387
  141.3 0.0 collective-permute-start.5
  141.3 5.7 %collective-permute-done.2.refs_3_ = bf16[16,16,896]{2,1,0:T(8,128)(2,1)S(1)} collective-permute-done((bf16[16,16,896]{2,1,0:T(8,128)(2,1)S(1)}, bf16[16,16,896]{2,1,0:T(8,128)(2,1)S(1)}, u32[]{:S(2)}, u32[]{:S(2)}) %collective-permute-start.2) | collective-permute-done | bytes 458784 | tf_op jit(solution)/shard_map/ppermute | solution.py:387
  147.0 0.5 collective-permute-start.7
  147.5 3.6 collective-permute-done.refs_1_
  151.1 1.0 collective-permute-start.11
  152.2 0.0 collective-permute-done.6.refs_8_
  152.2 0.6 collective-permute-start.10
  152.8 4.0 collective-permute-done.5.refs_6_
  156.8 0.8 copy-done.13
  157.6 0.5 collective-permute-start.4
  158.1 6.8 %partial_grads.1 = (bf16[1536,256]{1,0:T(8,128)(2,1)}, bf16[1536,256]{1,0:T(8,128)(2,1)}, bf16[1536,256]{1,0:T(8,128)(2,1)}, bf16[1536,256]{1,0:T(8,128)(2,1)}) custom-call(s32[1]{0:T(128)} %bitcast.4.dp, bf16[1536,896]{1,0:T(8,128)(2,1)} %bitcast.14.x, bf16[1024,896]{1,0:T(8,128)(2,1)} %bitcast.37), custom_call_target="tpu_custom_call" | custom-call | flops 2818572288 | bytes 6291456 | tf_op jit(solution)/shard_map/partial_grads/pallas_call | solution.py:211
  165.0 35.1 %collective-permute-done.4.refs_5_ = bf16[16,16,896]{2,1,0:T(8,128)(2,1)} collective-permute-done((bf16[16,16,896]{2,1,0:T(8,128)(2,1)S(1)}, bf16[16,16,896]{2,1,0:T(8,128)(2,1)}, u32[]{:S(2)}, u32[]{:S(2)}) %collective-permute-start.4) | collective-permute-done | bytes 458784 | tf_op jit(solution)/shard_map/ppermute | solution.py:387
  200.0 0.4 collective-permute-start.18
  200.4 0.9 collective-permute-start.19
  201.3 1.6 collective-permute-start.20
  203.0 12.4 %hidden.1 = (f32[1536,256]{1,0:T(8,128)}, f32[1536,256]{1,0:T(8,128)}, bf16[1536,256]{1,0:T(8,128)(2,1)}) custom-call(s32[1]{0:T(128)} %bitcast.4.dp, bf16[32,16,896]{2,1,0:T(8,128)(2,1)} %copy-done.2, bf16[16,16,896]{2,1,0:T(8,128)(2,1)} %copy-done.12, bf16[16,16,896]{2,1,0:T(8,128)(2,1)} %copy-done.10, bf16[16,16,896]{2,1,0:T(8,128)(2,1)} %copy-done.11, ...), custom_call_target="tpu_custom_call" | custom-call | flops 5637144576 | bytes 18350080 | tf_op jit(solution)/shard_map/hidden/pallas_call | solution.py:179
  215.4 5.2 %collective-permute-done.18.h1 = bf16[1536,256]{1,0:T(8,128)(2,1)S(1)} collective-permute-done((bf16[1536,256]{1,0:T(8,128)(2,1)}, bf16[1536,256]{1,0:T(8,128)(2,1)S(1)}, u32[]{:S(2)}, u32[]{:S(2)}) %collective-permute-start.18) | collective-permute-done | bytes 786464 | tf_op jit(solution)/shard_map/ppermute | solution.py:387
  220.6 12.7 %collective-permute-done.19.h2 = bf16[1536,256]{1,0:T(8,128)(2,1)} collective-permute-done((bf16[1536,256]{1,0:T(8,128)(2,1)}, bf16[1536,256]{1,0:T(8,128)(2,1)}, u32[]{:S(2)}, u32[]{:S(2)}) %collective-permute-start.19) | collective-permute-done | bytes 786464 | tf_op jit(solution)/shard_map/ppermute | solution.py:387
  233.3 4.1 collective-permute-done.20.h3
  237.4 0.9 copy-done.7
  238.2 12.2 %weight_grads.1 = bf16[3584,256]{1,0:T(8,128)(2,1)} custom-call(s32[1]{0:T(128)} %bitcast.4.dp, bf16[1536,256]{1,0:T(8,128)(2,1)} %get-tuple-element.23.h0, bf16[1536,256]{1,0:T(8,128)(2,1)} %copy-done.6, bf16[1536,256]{1,0:T(8,128)(2,1)} %collective-permute-done.19.h2, bf16[1536,256]{1,0:T(8,128)(2,1)} %copy-done.7, f32[1536,256]{1,0:T(8,128)} %get-tuple-element.27.g_in, ...), custom_call_target="tpu_custom_call" | custom-call | flops 2818572288 | bytes 19398656 | tf_op jit(solution)/shard_map/weight_grads/pallas_call | solution.py:253
  250.4 8.8 %all-to-all-start.4 = ((bf16[32,112,256]{2,1,0:T(8,128)(2,1)}), bf16[32,112,256]{2,1,0:T(8,128)(2,1)S(1)}, u32[]{:S(2)}, u32[]{:S(2)}) async-start(bf16[32,112,256]{2,1,0:T(8,128)(2,1)} %bitcast.24), calls=%async_computation.4 | async-start | bytes 3670016 | tf_op jit(solution)/shard_map/all_to_all | solution.py:383
  259.2 0.1 fusion.2
  259.3 0.1 collective-permute-start.12
  259.4 2.6 collective-permute-start.15
  262.1 1.1 collective-permute-start.14
  263.2 0.4 collective-permute-start.13
  263.5 7.5 %collective-permute-done.12.refs_1_ = bf16[16,48,256]{2,1,0:T(8,128)(2,1)S(1)} collective-permute-done((bf16[16,48,256]{2,1,0:T(8,128)(2,1)S(1)}, bf16[16,48,256]{2,1,0:T(8,128)(2,1)S(1)}, u32[]{:S(2)}, u32[]{:S(2)}) %collective-permute-start.12) | collective-permute-done | bytes 393248 | tf_op jit(solution)/shard_map/ppermute | solution.py:387
  271.0 2.7 collective-permute-start.17
  273.7 4.7 %collective-permute-done.14.refs_3_ = bf16[16,48,256]{2,1,0:T(8,128)(2,1)S(1)} collective-permute-done((bf16[16,48,256]{2,1,0:T(8,128)(2,1)S(1)}, bf16[16,48,256]{2,1,0:T(8,128)(2,1)S(1)}, u32[]{:S(2)}, u32[]{:S(2)}) %collective-permute-start.14) | collective-permute-done | bytes 393248 | tf_op jit(solution)/shard_map/ppermute | solution.py:387
  278.4 1.0 collective-permute-done.13.refs_2_
  279.5 8.4 %collective-permute-done.16.refs_5_ = bf16[16,48,256]{2,1,0:T(8,128)(2,1)S(1)} collective-permute-done((bf16[16,48,256]{2,1,0:T(8,128)(2,1)S(1)}, bf16[16,48,256]{2,1,0:T(8,128)(2,1)S(1)}, u32[]{:S(2)}, u32[]{:S(2)}) %collective-permute-start.16) | collective-permute-done | bytes 393248 | tf_op jit(solution)/shard_map/ppermute | solution.py:387
  287.9 0.7 copy-done.18
  288.6 0.8 copy-done.19
  289.4 7.7 %outputs.1 = bf16[1536,896]{1,0:T(8,128)(2,1)} custom-call(s32[1]{0:T(128)} %bitcast.4.dp, bf16[32,48,256]{2,1,0:T(8,128)(2,1)} %bitcast.30, bf16[16,48,256]{2,1,0:T(8,128)(2,1)} %copy-done.14, bf16[16,48,256]{2,1,0:T(8,128)(2,1)} %copy-done.17, bf16[16,48,256]{2,1,0:T(8,128)(2,1)} %copy-done.16, bf16[16,48,256]{2,1,0:T(8,128)(2,1)} %copy-done.15, ...), custom_call_target="tpu_custom_call" | custom-call | flops 2818572288 | bytes 5898240 | tf_op jit(solution)/shard_map/outputs/pallas_call | solution.py:279
  297.1 0.0 copy-start.3
  297.1 1.2 copy-done.3
  298.3 8.1 %all-to-all-start.2 = ((bf16[32,48,896]{2,1,0:T(8,128)(2,1)}), bf16[32,48,896]{2,1,0:T(8,128)(2,1)S(1)}, u32[]{:S(2)}, u32[]{:S(2)}) async-start(bf16[32,48,896]{2,1,0:T(8,128)(2,1)} %bitcast.25), calls=%async_computation.2 | async-start | bytes 5505024 | tf_op jit(solution)/shard_map/all_to_all | solution.py:383
  306.4 10.0 %update.1 = bf16[32,3,112,256]{3,2,1,0:T(8,128)(2,1)} custom-call(s32[32]{0:T(128)} %plan.1, s32[32]{0:T(128)} %placement.1, bf16[32,112,256]{2,1,0:T(8,128)(2,1)} %copy-done.3, bf16[32,336,256]{2,1,0:T(8,128)(2,1)} %all-to-all-done.5.gate.first.second, bf16[32,336,256]{2,1,0:T(8,128)(2,1)} %all-to-all-done.5.gate.first.second, ...), custom_call_target="tpu_custom_call" | custom-call | flops 18350080 | bytes 10485760 | tf_op jit(solution)/shard_map/update/pallas_call | solution.py:348
  316.4 25.3 %all-to-all-done.2 = bf16[32,48,896]{2,1,0:T(8,128)(2,1)S(1)} async-done(((bf16[32,48,896]{2,1,0:T(8,128)(2,1)}), bf16[32,48,896]{2,1,0:T(8,128)(2,1)S(1)}, u32[]{:S(2)}, u32[]{:S(2)}) %all-to-all-start.2) | async-done | bytes 2752544 | tf_op jit(solution)/shard_map/all_to_all | solution.py:383
  341.7 1.6 copy-done.1
  343.3 5.4 %all-to-all-start.6 = ((bf16[32,3,112,256]{3,2,1,0:T(8,128)(2,1)}), bf16[32,3,112,256]{3,2,1,0:T(8,128)(2,1)}, u32[]{:S(2)}, u32[]{:S(2)}) async-start(bf16[32,3,112,256]{3,2,1,0:T(8,128)(2,1)} %update.1), calls=%async_computation.6 | async-start | bytes 11010048 | tf_op jit(solution)/shard_map/all_to_all | solution.py:383
  348.7 3.7 combine.1
  352.4 64.1 %all-to-all-done.6.moments = bf16[32,3,112,256]{3,2,1,0:T(8,128)(2,1)} async-done(((bf16[32,3,112,256]{3,2,1,0:T(8,128)(2,1)}), bf16[32,3,112,256]{3,2,1,0:T(8,128)(2,1)}, u32[]{:S(2)}, u32[]{:S(2)}) %all-to-all-start.6) | async-done | bytes 5505056 | tf_op jit(solution)/shard_map/all_to_all | solution.py:383
  416.5 5.5 %finish.1 = (bf16[32,112,256]{2,1,0:T(8,128)(2,1)}, bf16[32,112,256]{2,1,0:T(8,128)(2,1)}, bf16[32,112,256]{2,1,0:T(8,128)(2,1)}) custom-call(bf16[32,3,112,256]{3,2,1,0:T(8,128)(2,1)} %all-to-all-done.6.moments), custom_call_target="tpu_custom_call" | custom-call | bytes 12582912 | tf_op jit(solution)/shard_map/finish/pallas_call | solution.py:371
  (44 shorter events, 0.1 us)
Async XLA Ops:
  28.7 75.4 %copy-start.2 = (bf16[32,16,896]{2,1,0:T(8,128)(2,1)}, bf16[32,16,896]{2,1,0:T(8,128)(2,1)S(1)}, u32[]{:S(2)}) copy-start(bf16[32,16,896]{2,1,0:T(8,128)(2,1)S(1)} %all_to_all.35.refs_0_) | copy-start | bytes 2752516
  28.7 29.4 %all-to-all-start.1 = ((bf16[32,32,896]{2,1,0:T(8,128)(2,1)}), bf16[32,32,896]{2,1,0:T(8,128)(2,1)S(1)}, u32[]{:S(2)}, u32[]{:S(2)}) async-start(bf16[32,32,896]{2,1,0:T(8,128)(2,1)} %get-tuple-element.20), calls=%async_computation.1 | async-start | bytes 3670016 | tf_op jit(solution)/shard_map/all_to_all | solution.py:383
  58.1 49.9 %copy-start = (bf16[32,32,896]{2,1,0:T(8,128)(2,1)}, bf16[32,32,896]{2,1,0:T(8,128)(2,1)S(1)}, u32[]{:S(2)}) copy-start(bf16[32,32,896]{2,1,0:T(8,128)(2,1)S(1)} %all-to-all-done.1.refs_7_) | copy-start | bytes 5505028
  58.1 40.6 %all-to-all-start.3 = ((bf16[32,48,896]{2,1,0:T(8,128)(2,1)}), bf16[32,48,896]{2,1,0:T(8,128)(2,1)}, u32[]{:S(2)}, u32[]{:S(2)}) async-start(bf16[32,48,896]{2,1,0:T(8,128)(2,1)} %bitcast.23), calls=%async_computation.3 | async-start | bytes 5505024 | tf_op jit(solution)/shard_map/all_to_all | solution.py:383
  98.7 151.8 %all-to-all-start.5 = ((bf16[32,336,256]{2,1,0:T(8,128)(2,1)}), bf16[32,336,256]{2,1,0:T(8,128)(2,1)}, u32[]{:S(2)}, u32[]{:S(2)}) async-start(bf16[32,336,256]{2,1,0:T(8,128)(2,1)} %pad_maximum_fusion), calls=%async_computation.5 | async-start | bytes 11010048 | tf_op jit(solution)/shard_map/all_to_all | solution.py:383
  104.2 13.3 %collective-permute-start.3 = (bf16[16,16,896]{2,1,0:T(8,128)(2,1)S(1)}, bf16[16,16,896]{2,1,0:T(8,128)(2,1)S(1)}, u32[]{:S(2)}, u32[]{:S(2)}) collective-permute-start(bf16[16,16,896]{2,1,0:T(8,128)(2,1)S(1)} %get-tuple-element.34), channel_id=1, source_target_pairs={{0,96},{32,0},{64,32},{96,64},{1,97},{33,1},{65,33},{97,65},{2,98}... | collective-permute-start | bytes 1376264 | tf_op jit(solution)/shard_map/ppermute | solution.py:387
  109.1 42.0 %collective-permute-start.9 = (bf16[16,32,896]{2,1,0:T(8,128)(2,1)}, bf16[16,32,896]{2,1,0:T(8,128)(2,1)S(1)}, u32[]{:S(2)}, u32[]{:S(2)}) collective-permute-start(bf16[16,32,896]{2,1,0:T(8,128)(2,1)} %get-tuple-element.32), channel_id=1, source_target_pairs={{0,96},{32,0},{64,32},{96,64},{1,97},{33,1},{65,33},{97,65},{2,98}... | collective-permute-start | bytes 2752520 | tf_op jit(solution)/shard_map/ppermute | solution.py:387
  109.2 42.9 %collective-permute-start.6 = (bf16[16,32,896]{2,1,0:T(8,128)(2,1)S(1)}, bf16[16,32,896]{2,1,0:T(8,128)(2,1)S(1)}, u32[]{:S(2)}, u32[]{:S(2)}) collective-permute-start(bf16[16,32,896]{2,1,0:T(8,128)(2,1)S(1)} %get-tuple-element.33), channel_id=1, source_target_pairs={{0,32},{32,64},{64,96},{96,0},{1,33},{33,65},{65,97},{97,1},{2,34}... | collective-permute-start | bytes 2752520 | tf_op jit(solution)/shard_map/ppermute | solution.py:387
  110.6 30.7 %collective-permute-start.1 = (bf16[16,16,896]{2,1,0:T(8,128)(2,1)S(1)}, bf16[16,16,896]{2,1,0:T(8,128)(2,1)S(1)}, u32[]{:S(2)}, u32[]{:S(2)}) collective-permute-start(bf16[16,16,896]{2,1,0:T(8,128)(2,1)S(1)} %get-tuple-element.34), channel_id=1, source_target_pairs={{0,32},{32,64},{64,96},{96,0},{1,33},{33,65},{65,97},{97,1},{2,34}... | collective-permute-start | bytes 1376264 | tf_op jit(solution)/shard_map/ppermute | solution.py:387
  110.6 36.4 %collective-permute-start.2 = (bf16[16,16,896]{2,1,0:T(8,128)(2,1)S(1)}, bf16[16,16,896]{2,1,0:T(8,128)(2,1)S(1)}, u32[]{:S(2)}, u32[]{:S(2)}) collective-permute-start(bf16[16,16,896]{2,1,0:T(8,128)(2,1)S(1)} %get-tuple-element.35), channel_id=1, source_target_pairs={{0,96},{32,0},{64,32},{96,64},{1,97},{33,1},{65,33},{97,65},{2,98}... | collective-permute-start | bytes 1376264 | tf_op jit(solution)/shard_map/ppermute | solution.py:387
  117.5 34.7 %copy-start.9 = (bf16[16,16,896]{2,1,0:T(8,128)(2,1)}, bf16[16,16,896]{2,1,0:T(8,128)(2,1)S(1)}, u32[]{:S(2)}) copy-start(bf16[16,16,896]{2,1,0:T(8,128)(2,1)S(1)} %collective-permute-done.3.refs_4_) | copy-start | bytes 1376260
  117.5 33.7 %collective-permute-start = (bf16[16,16,896]{2,1,0:T(8,128)(2,1)S(1)}, bf16[16,16,896]{2,1,0:T(8,128)(2,1)S(1)}, u32[]{:S(2)}, u32[]{:S(2)}) collective-permute-start(bf16[16,16,896]{2,1,0:T(8,128)(2,1)S(1)} %get-tuple-element.35), channel_id=1, source_target_pairs={{0,32},{32,64},{64,96},{96,0},{1,33},{33,65},{65,97},{97,1},{2,34}... | collective-permute-start | bytes 1376264 | tf_op jit(solution)/shard_map/ppermute | solution.py:387
  141.3 15.5 %copy-start.10 = (bf16[16,16,896]{2,1,0:T(8,128)(2,1)}, bf16[16,16,896]{2,1,0:T(8,128)(2,1)S(1)}, u32[]{:S(2)}) copy-start(bf16[16,16,896]{2,1,0:T(8,128)(2,1)S(1)} %collective-permute-done.1.refs_2_) | copy-start | bytes 1376260
  141.3 15.5 %collective-permute-start.5 = (bf16[16,16,896]{2,1,0:T(8,128)(2,1)S(1)}, bf16[16,16,896]{2,1,0:T(8,128)(2,1)S(1)}, u32[]{:S(2)}, u32[]{:S(2)}) collective-permute-start(bf16[16,16,896]{2,1,0:T(8,128)(2,1)S(1)} %collective-permute-done.3.refs_4_), channel_id=1, source_target_pairs={{0,96},{32,0},{64,32},{96,64},{1,97},{33,1},{65,33},{97,65},{2,98}... | collective-permute-start | bytes 1376264 | tf_op jit(solution)/shard_map/ppermute | solution.py:387
  147.0 9.8 %copy-start.11 = (bf16[16,16,896]{2,1,0:T(8,128)(2,1)}, bf16[16,16,896]{2,1,0:T(8,128)(2,1)S(1)}, u32[]{:S(2)}) copy-start(bf16[16,16,896]{2,1,0:T(8,128)(2,1)S(1)} %collective-permute-done.2.refs_3_) | copy-start | bytes 1376260
  147.0 53.5 %collective-permute-start.7 = (bf16[16,32,896]{2,1,0:T(8,128)(2,1)}, bf16[16,32,896]{2,1,0:T(8,128)(2,1)}, u32[]{:S(2)}, u32[]{:S(2)}) collective-permute-start(bf16[16,32,896]{2,1,0:T(8,128)(2,1)} %get-tuple-element.32), channel_id=1, source_target_pairs={{0,32},{32,64},{64,96},{96,0},{1,33},{33,65},{65,97},{97,1},{2,34}... | collective-permute-start | bytes 2752520 | tf_op jit(solution)/shard_map/ppermute | solution.py:387
  151.1 13.8 %copy-start.12 = (bf16[16,16,896]{2,1,0:T(8,128)(2,1)}, bf16[16,16,896]{2,1,0:T(8,128)(2,1)S(1)}, u32[]{:S(2)}) copy-start(bf16[16,16,896]{2,1,0:T(8,128)(2,1)S(1)} %collective-permute-done.refs_1_) | copy-start | bytes 1376260
  151.1 50.2 %collective-permute-start.8 = (bf16[16,32,896]{2,1,0:T(8,128)(2,1)S(1)}, bf16[16,32,896]{2,1,0:T(8,128)(2,1)}, u32[]{:S(2)}, u32[]{:S(2)}) collective-permute-start(bf16[16,32,896]{2,1,0:T(8,128)(2,1)S(1)} %get-tuple-element.33), channel_id=1, source_target_pairs={{0,96},{32,0},{64,32},{96,64},{1,97},{33,1},{65,33},{97,65},{2,98}... | collective-permute-start | bytes 2752520 | tf_op jit(solution)/shard_map/ppermute | solution.py:387
  151.1 13.8 %copy-start.4 = (bf16[16,32,896]{2,1,0:T(8,128)(2,1)}, bf16[16,32,896]{2,1,0:T(8,128)(2,1)S(1)}, u32[]{:S(2)}) copy-start(bf16[16,32,896]{2,1,0:T(8,128)(2,1)S(1)} %collective-permute-done.9.refs_11_) | copy-start | bytes 2752516
  151.1 51.8 %collective-permute-start.11 = (bf16[16,32,896]{2,1,0:T(8,128)(2,1)S(1)}, bf16[16,32,896]{2,1,0:T(8,128)(2,1)}, u32[]{:S(2)}, u32[]{:S(2)}) collective-permute-start(bf16[16,32,896]{2,1,0:T(8,128)(2,1)S(1)} %collective-permute-done.9.refs_11_), channel_id=1, source_target_pairs={{0,96},{32,0},{64,32},{96,64},{1,97},{33,1},{65,33},{97,65},{2,98}... | collective-permute-start | bytes 2752520 | tf_op jit(solution)/shard_map/ppermute | solution.py:387
  152.2 12.8 %copy-start.5 = (bf16[16,32,896]{2,1,0:T(8,128)(2,1)}, bf16[16,32,896]{2,1,0:T(8,128)(2,1)S(1)}, u32[]{:S(2)}) copy-start(bf16[16,32,896]{2,1,0:T(8,128)(2,1)S(1)} %collective-permute-done.6.refs_8_) | copy-start | bytes 2752516
  152.2 50.8 %collective-permute-start.10 = (bf16[16,32,896]{2,1,0:T(8,128)(2,1)S(1)}, bf16[16,32,896]{2,1,0:T(8,128)(2,1)}, u32[]{:S(2)}, u32[]{:S(2)}) collective-permute-start(bf16[16,32,896]{2,1,0:T(8,128)(2,1)S(1)} %collective-permute-done.6.refs_8_), channel_id=1, source_target_pairs={{0,32},{32,64},{64,96},{96,0},{1,33},{33,65},{65,97},{97,1},{2,34}... | collective-permute-start | bytes 2752520 | tf_op jit(solution)/shard_map/ppermute | solution.py:387
  156.8 0.8 copy-start.13
  157.6 42.5 %collective-permute-start.4 = (bf16[16,16,896]{2,1,0:T(8,128)(2,1)S(1)}, bf16[16,16,896]{2,1,0:T(8,128)(2,1)}, u32[]{:S(2)}, u32[]{:S(2)}) collective-permute-start(bf16[16,16,896]{2,1,0:T(8,128)(2,1)S(1)} %collective-permute-done.refs_1_), channel_id=1, source_target_pairs={{0,32},{32,64},{64,96},{96,0},{1,33},{33,65},{65,97},{97,1},{2,34}... | collective-permute-start | bytes 1376264 | tf_op jit(solution)/shard_map/ppermute | solution.py:387
  200.0 20.6 %collective-permute-start.18 = (bf16[1536,256]{1,0:T(8,128)(2,1)}, bf16[1536,256]{1,0:T(8,128)(2,1)S(1)}, u32[]{:S(2)}, u32[]{:S(2)}) collective-permute-start(bf16[1536,256]{1,0:T(8,128)(2,1)} %get-tuple-element.24), channel_id=1, source_target_pairs={{0,32},{32,64},{64,96},{96,0},{1,33},{33,65},{65,97},{97,1},{2,34}... | collective-permute-start | bytes 2359304 | tf_op jit(solution)/shard_map/ppermute | solution.py:387
  200.4 32.9 %collective-permute-start.19 = (bf16[1536,256]{1,0:T(8,128)(2,1)}, bf16[1536,256]{1,0:T(8,128)(2,1)}, u32[]{:S(2)}, u32[]{:S(2)}) collective-permute-start(bf16[1536,256]{1,0:T(8,128)(2,1)} %get-tuple-element.25), channel_id=1, source_target_pairs={{0,64},{32,96},{64,0},{96,32},{1,65},{33,97},{65,1},{97,33},{2,66}... | collective-permute-start | bytes 2359304 | tf_op jit(solution)/shard_map/ppermute | solution.py:387
  201.3 36.0 %collective-permute-start.20 = (bf16[1536,256]{1,0:T(8,128)(2,1)}, bf16[1536,256]{1,0:T(8,128)(2,1)S(1)}, u32[]{:S(2)}, u32[]{:S(2)}) collective-permute-start(bf16[1536,256]{1,0:T(8,128)(2,1)} %get-tuple-element.26), channel_id=1, source_target_pairs={{0,96},{32,0},{64,32},{96,64},{1,97},{33,1},{65,33},{97,65},{2,98}... | collective-permute-start | bytes 2359304 | tf_op jit(solution)/shard_map/ppermute | solution.py:387
  220.6 16.7 %copy-start.6 = (bf16[1536,256]{1,0:T(8,128)(2,1)}, bf16[1536,256]{1,0:T(8,128)(2,1)S(1)}, u32[]{:S(2)}) copy-start(bf16[1536,256]{1,0:T(8,128)(2,1)S(1)} %collective-permute-done.18.h1) | copy-start | bytes 2359300
  237.4 0.9 copy-start.7
  250.4 8.8 %copy-start.8 = (bf16[1536,256]{1,0:T(8,128)(2,1)S(1)}, bf16[1536,256]{1,0:T(8,128)(2,1)}, u32[]{:S(2)}) copy-start(bf16[1536,256]{1,0:T(8,128)(2,1)} %get-tuple-element.21) | copy-start | bytes 2359300
  250.4 46.6 %all-to-all-start.4 = ((bf16[32,112,256]{2,1,0:T(8,128)(2,1)}), bf16[32,112,256]{2,1,0:T(8,128)(2,1)S(1)}, u32[]{:S(2)}, u32[]{:S(2)}) async-start(bf16[32,112,256]{2,1,0:T(8,128)(2,1)} %bitcast.24), calls=%async_computation.4 | async-start | bytes 3670016 | tf_op jit(solution)/shard_map/all_to_all | solution.py:383
  259.3 11.7 %collective-permute-start.12 = (bf16[16,48,256]{2,1,0:T(8,128)(2,1)S(1)}, bf16[16,48,256]{2,1,0:T(8,128)(2,1)S(1)}, u32[]{:S(2)}, u32[]{:S(2)}) collective-permute-start(bf16[16,48,256]{2,1,0:T(8,128)(2,1)S(1)} %bitcast.33), channel_id=1, source_target_pairs={{0,32},{32,64},{64,96},{96,0},{1,33},{33,65},{65,97},{97,1},{2,34}... | collective-permute-start | bytes 1179656 | tf_op jit(solution)/shard_map/ppermute | solution.py:387
  259.4 11.6 %collective-permute-start.15 = (bf16[16,48,256]{2,1,0:T(8,128)(2,1)S(1)}, bf16[16,48,256]{2,1,0:T(8,128)(2,1)S(1)}, u32[]{:S(2)}, u32[]{:S(2)}) collective-permute-start(bf16[16,48,256]{2,1,0:T(8,128)(2,1)S(1)} %bitcast.31), channel_id=1, source_target_pairs={{0,96},{32,0},{64,32},{96,64},{1,97},{33,1},{65,33},{97,65},{2,98}... | collective-permute-start | bytes 1179656 | tf_op jit(solution)/shard_map/ppermute | solution.py:387
  262.1 16.4 %collective-permute-start.14 = (bf16[16,48,256]{2,1,0:T(8,128)(2,1)S(1)}, bf16[16,48,256]{2,1,0:T(8,128)(2,1)S(1)}, u32[]{:S(2)}, u32[]{:S(2)}) collective-permute-start(bf16[16,48,256]{2,1,0:T(8,128)(2,1)S(1)} %bitcast.34), channel_id=1, source_target_pairs={{0,96},{32,0},{64,32},{96,64},{1,97},{33,1},{65,33},{97,65},{2,98}... | collective-permute-start | bytes 1179656 | tf_op jit(solution)/shard_map/ppermute | solution.py:387
  263.2 16.3 %collective-permute-start.13 = (bf16[16,48,256]{2,1,0:T(8,128)(2,1)S(1)}, bf16[16,48,256]{2,1,0:T(8,128)(2,1)S(1)}, u32[]{:S(2)}, u32[]{:S(2)}) collective-permute-start(bf16[16,48,256]{2,1,0:T(8,128)(2,1)S(1)} %bitcast.32), channel_id=1, source_target_pairs={{0,32},{32,64},{64,96},{96,0},{1,33},{33,65},{65,97},{97,1},{2,34}... | collective-permute-start | bytes 1179656 | tf_op jit(solution)/shard_map/ppermute | solution.py:387
  271.0 18.4 %copy-start.14 = (bf16[16,48,256]{2,1,0:T(8,128)(2,1)}, bf16[16,48,256]{2,1,0:T(8,128)(2,1)S(1)}, u32[]{:S(2)}) copy-start(bf16[16,48,256]{2,1,0:T(8,128)(2,1)S(1)} %collective-permute-done.12.refs_1_) | copy-start | bytes 1179652
  271.0 16.9 %collective-permute-start.16 = (bf16[16,48,256]{2,1,0:T(8,128)(2,1)S(1)}, bf16[16,48,256]{2,1,0:T(8,128)(2,1)S(1)}, u32[]{:S(2)}, u32[]{:S(2)}) collective-permute-start(bf16[16,48,256]{2,1,0:T(8,128)(2,1)S(1)} %collective-permute-done.12.refs_1_), channel_id=1, source_target_pairs={{0,32},{32,64},{64,96},{96,0},{1,33},{33,65},{65,97},{97,1},{2,34}... | collective-permute-start | bytes 1179656 | tf_op jit(solution)/shard_map/ppermute | solution.py:387
  271.0 18.4 %copy-start.15 = (bf16[16,48,256]{2,1,0:T(8,128)(2,1)}, bf16[16,48,256]{2,1,0:T(8,128)(2,1)S(1)}, u32[]{:S(2)}) copy-start(bf16[16,48,256]{2,1,0:T(8,128)(2,1)S(1)} %collective-permute-done.15.refs_4_) | copy-start | bytes 1179652
  271.0 16.8 %collective-permute-start.17 = (bf16[16,48,256]{2,1,0:T(8,128)(2,1)S(1)}, bf16[16,48,256]{2,1,0:T(8,128)(2,1)S(1)}, u32[]{:S(2)}, u32[]{:S(2)}) collective-permute-start(bf16[16,48,256]{2,1,0:T(8,128)(2,1)S(1)} %collective-permute-done.15.refs_4_), channel_id=1, source_target_pairs={{0,96},{32,0},{64,32},{96,64},{1,97},{33,1},{65,33},{97,65},{2,98}... | collective-permute-start | bytes 1179656 | tf_op jit(solution)/shard_map/ppermute | solution.py:387
  278.4 11.0 %copy-start.16 = (bf16[16,48,256]{2,1,0:T(8,128)(2,1)}, bf16[16,48,256]{2,1,0:T(8,128)(2,1)S(1)}, u32[]{:S(2)}) copy-start(bf16[16,48,256]{2,1,0:T(8,128)(2,1)S(1)} %collective-permute-done.14.refs_3_) | copy-start | bytes 1179652
  279.4 9.9 %copy-start.17 = (bf16[16,48,256]{2,1,0:T(8,128)(2,1)}, bf16[16,48,256]{2,1,0:T(8,128)(2,1)S(1)}, u32[]{:S(2)}) copy-start(bf16[16,48,256]{2,1,0:T(8,128)(2,1)S(1)} %collective-permute-done.13.refs_2_) | copy-start | bytes 1179652
  287.9 0.8 copy-start.18
  288.6 0.8 copy-start.19
  297.1 1.2 copy-start.3
  298.3 43.4 %all-to-all-start.2 = ((bf16[32,48,896]{2,1,0:T(8,128)(2,1)}), bf16[32,48,896]{2,1,0:T(8,128)(2,1)S(1)}, u32[]{:S(2)}, u32[]{:S(2)}) async-start(bf16[32,48,896]{2,1,0:T(8,128)(2,1)} %bitcast.25), calls=%async_computation.2 | async-start | bytes 5505024 | tf_op jit(solution)/shard_map/all_to_all | solution.py:383
  341.7 1.6 copy-start.1
  343.3 73.3 %all-to-all-start.6 = ((bf16[32,3,112,256]{3,2,1,0:T(8,128)(2,1)}), bf16[32,3,112,256]{3,2,1,0:T(8,128)(2,1)}, u32[]{:S(2)}, u32[]{:S(2)}) async-start(bf16[32,3,112,256]{3,2,1,0:T(8,128)(2,1)} %update.1), calls=%async_computation.6 | async-start | bytes 11010048 | tf_op jit(solution)/shard_map/all_to_all | solution.py:383

commit v2 on v1

--- a/solution.py
+++ b/solution.py
@@ -206,60 +206,96 @@
         ).astype(bf16)
 
 
-def partial_grads(dp, x, wd):
+def partial_grads(dp, x, wd, part):
     block = PARTIAL_BLOCK
+    rows = ROWS // 2
+    steps = rows // block
     return pl.pallas_call(
         partial_kernel,
-        grid=(ROWS // block,),
-        out_shape=[jax.ShapeDtypeStruct((ROWS, QF), bf16)] * N_DP,
-        in_specs=[sspec(), row_block(block, QD), whole((FF, QD))],
+        grid=(steps,),
+        out_shape=[jax.ShapeDtypeStruct((rows, QF), bf16)] * N_DP,
+        in_specs=[
+            sspec(),
+            pl.BlockSpec((block, QD), lambda i: (part * steps + i, 0)),
+            whole((FF, QD)),
+        ],
         out_specs=[row_block(block, QF)] * N_DP,
-        cost_estimate=cost(2 * ROWS * QD * FF, 6 << 20),
-        name="partial_grads",
+        cost_estimate=cost(2 * rows * QD * FF, 4 << 20),
     )(dp, x, wd)
 
 
-WEIGHT_SOURCES = 16
-
-
-def weight_kernel(count, dp, h0, h1, h2, h3, g_in, u_in, *refs):
-    pieces, (out, gathered, acc) = refs[:count], refs[count:]
+WEIGHT_SOURCES = 8
+WEIGHT_STEPS = HALF // WEIGHT_SOURCES
+
+
+def weight_kernel(part, count, dp, h0, h1, h2, h3, g_in, u_in, *refs):
+    pieces, rest = refs[:count], refs[count:]
     i = pl.program_id(0)
-    gather_pieces(WEIGHT_SOURCES, dp, pieces, gathered)
+    out, gathered, acc = rest[-3:]
+    at = 0
+    for j in range(0, count, 4):
+        rows = pieces[j].shape[1]
+        for shift, ref in zip((0, 3, 1, 2), pieces[j : j + 4]):
+            q = lax.rem(dp[0] + shift, N_DP)
+            gathered[:, at : at + rows, pl.ds(pl.multiple_of(q * QD, QD), QD)] = ref[...]
+        at += rows
     x = gathered[...].reshape(WEIGHT_SOURCES * CAP, D)
     grad = h0[...].astype(f32) + h1[...].astype(f32) + h2[...].astype(f32) + h3[...].astype(f32)
     grad = grad * scale_mid
     g = g_in[...]
     s = 1.0 / (1.0 + jnp.exp(-g))
     gg = (grad * u_in[...] * s * (1.0 + g * (1.0 - s))).astype(bf16)
-    part = lax.dot_general(gg, x, (((0,), (0,)), ((), ())), preferred_element_type=f32)
-
-    @pl.when(i == 0)
-    def _():
-        acc[...] = part
-
-    @pl.when(i == pl.num_programs(0) - 1)
-    def _():
-        for r in range(0, D, 512):
-            total = (acc[:, r : r + 512] + part[:, r : r + 512]) * scale_in
-            out[r : r + 512, :] = total.T.astype(bf16)
-
-
-def weight_grads(dp, hg, g, u, pieces):
+    product = lax.dot_general(gg, x, (((0,), (0,)), ((), ())), preferred_element_type=f32)
+    last = i == pl.num_programs(0) - 1
+    if part == 0:
+
+        @pl.when(i == 0)
+        def _():
+            out[...] = product
+
+        @pl.when(i > 0)
+        def _():
+            out[...] += product
+
+    else:
+
+        @pl.when(i == 0)
+        def _():
+            acc[...] = rest[0][...] + product
+
+        @pl.when(last)
+        def _():
+            for r in range(0, D, 512):
+                total = (acc[:, r : r + 512] + product[:, r : r + 512]) * scale_in
+                out[r : r + 512, :] = total.T.astype(bf16)
+
+
+def weight_grads(dp, hg, g, u, pieces, part, carry=()):
     n = WEIGHT_SOURCES
     block = n * CAP
-    inputs = flat(pieces)
-    assert SLOTS // n == 2
-    return pl.pallas_call(
-        functools.partial(weight_kernel, len(inputs)),
-        grid=(SLOTS // n,),
-        out_shape=jax.ShapeDtypeStruct((D, QF), bf16),
-        in_specs=[sspec()] + [row_block(block, QF)] * 6 + piece_specs(n, pieces),
-        out_specs=whole((D, QF)),
-        scratch_shapes=[VMEM((n, CAP, D), bf16), VMEM((QF, D), f32)],
-        cost_estimate=cost(2 * ROWS * D * QF, ROWS * D * 2 + (8 << 20)),
-        name="weight_grads",
-    )(dp, *hg, g, u, *inputs)
+    steps = WEIGHT_STEPS
+    assert steps == 2
+    inputs, specs = [], []
+    for own, la, lb, ra, rb, fa, fb in pieces:
+        shape = (n,) + own.shape[1:]
+        inputs += [own] + ([la, ra, fa] if part == 0 else [lb, rb, fb])
+        specs += [pl.BlockSpec(shape, lambda i: (part * steps + i, 0, 0))]
+        specs += [pl.BlockSpec(shape, lambda i: (i, 0, 0))] * 3
+    values = pl.BlockSpec((block, QF), lambda i: (part * steps + i, 0))
+    shape = jax.ShapeDtypeStruct((QF, D), f32) if part == 0 else jax.ShapeDtypeStruct((D, QF), bf16)
+    return pl.pallas_call(
+        functools.partial(weight_kernel, part, len(inputs)),
+        grid=(steps,),
+        out_shape=shape,
+        in_specs=[sspec()]
+        + [row_block(block, QF)] * 4
+        + [values] * 2
+        + specs
+        + [whole((QF, D))] * len(carry),
+        out_specs=whole(shape.shape),
+        scratch_shapes=[VMEM((n, CAP, D), bf16), VMEM((QF, D) if part else (8, 128), f32)],
+        cost_estimate=cost(ROWS * D * QF, ROWS * D + (8 << 20)),
+    )(dp, *hg, g, u, *inputs, *carry)
 
 
 OUTPUT_SOURCES = 8
@@ -425,9 +461,14 @@
     states = exchange(packed)
     pieces = [ring(x) for x in got]
     g, u, h = hidden_of(dp, pieces, wg, wu)
-    partials = partial_grads(dp, got_grads, wd)
-    hg = [partials[0]] + [shift(partials[k], k) for k in range(1, N_DP)]
-    wgrad = weight_grads(dp, hg, g, u, pieces)
+    carry = ()
+    hg = []
+    for part in range(2):
+        partials = partial_grads(dp, got_grads, wd, part)
+        hg.append([partials[0]] + [shift(partials[k], k) for k in range(1, N_DP)])
+    for part in range(2):
+        carry = (weight_grads(dp, hg[part], g, u, pieces, part, carry),)
+    wgrad = carry[0]
     got_wgrad = exchange(wgrad.reshape(SLOTS, PART, QF))
     moments = exchange(update(migration_plan, placement, got_wgrad, states))
     out = outputs_of(dp, [ring(h.reshape(SLOTS, CAP, QF))], wd)

time: 429 us -> 440 us (1.026)
  starting transfers between devices: 57.7 us -> 69.9 us
  waiting for transfers between devices: 260 us -> 252 us
  Pallas kernels: 65.9 us -> 72.6 us
    ppermute x21 -> x24, starting transfers between devices: 21 us -> 30.6 us  [shift(): return lax.ppermute(x, 'dp', [(i, (i + by) % N_DP) for i in range(N_DP)])]
    ppermute x21 -> x24, waiting for transfers between devices: 120 us -> 111 us  [shift(): return lax.ppermute(x, 'dp', [(i, (i + by) % N_DP) for i in range(N_DP)])]
    pallas_call x2 -> x4, Pallas kernels: 19 us -> 25.7 us  [the longest x2 16.6 us: weight_grads(): pl.pallas_call(functools.partial(weight_kernel, part, len(inputs)), grid=...]
  transfers between devices with their start and end apart: 27 -> 30, of which waited for: 17 -> 17; matrix products, arithmetic and copies ran while one was open for 2% -> 2% of each run, Pallas kernels for 13% -> 15%
where the time goes in v2:
time: 440 us; the launch traced here: 433 us
  waiting for transfers between devices  252 us (57%)
  Pallas kernels  72.6 us (16%)
  starting transfers between devices  69.9 us (16%)
  blocking collectives  24.1 us (5%)
  local copies, waits for them, and re-layouts  7.74 us (2%)
  other arithmetic  5.78 us (1%)
    all_to_all x6, waiting for transfers between devices, exchange(): return lax.all_to_all(x, 'expert', split_axis=0, concat_axis=0, tiled=True)  141 us
    ppermute x24, waiting for transfers between devices, shift(): return lax.ppermute(x, 'dp', [(i, (i + by) % N_DP) for i in range(N_DP)])  111 us
    all_to_all x6, starting transfers between devices, exchange(): return lax.all_to_all(x, 'expert', split_axis=0, concat_axis=0, tiled=True)  39.3 us
    ppermute x24, starting transfers between devices, shift(): return lax.ppermute(x, 'dp', [(i, (i + by) % N_DP) for i in range(N_DP)])  30.6 us
    all_to_all x1, blocking collectives, exchange(): return lax.all_to_all(x, 'expert', split_axis=0, concat_axis=0, tiled=True)  24.1 us
    pallas_call x2, Pallas kernels, weight_grads(): pl.pallas_call(functools.partial(weight_kernel, part, len(inputs)), grid=...  16.6 us
    pallas_call x1, Pallas kernels, hidden_of(): pl.pallas_call(functools.partial(hidden_kernel, len(inputs)), grid=(SLOTS...  12.4 us
    pallas_call x1, Pallas kernels, update(): pl.pallas_call(update_kernel, grid_spec=pltpu.PrefetchScalarGridSpec(num_...  10 us
  transfers between devices with their start and end apart: 30, of which 17 were waited for; matrix products, arithmetic and copies ran while one was open for 2% of the time, Pallas kernels for 15%

profile of v2, /device:TPU:1, one launch (start us, length us, event | category | flops | bytes accessed | tf_op | source)
XLA Modules:
  0.0 432.6 jit_solution(6402039608019496588)
XLA Ops:
  0.6 3.9 select_rows.1
  4.5 24.1 %all_to_all.35.refs_0_ = bf16[32,16,896]{2,1,0:T(8,128)(2,1)S(1)} all-to-all(bf16[32,16,896]{2,1,0:T(8,128)(2,1)} %get-tuple-element.23), channel_id=1, replica_groups=mesh['dp'=4,'expert'=32] {'expert'}, dimensions={0} | all-to-all | bytes 1835008 | tf_op jit(solution)/shard_map/all_to_all | solution.py:419
  28.7 3.9 all-to-all-start.1
  32.6 3.7 scale_rows.1
  36.2 21.8 %all-to-all-done.1.refs_7_.refs_4_ = bf16[32,32,896]{2,1,0:T(8,128)(2,1)S(1)} async-done(((bf16[32,32,896]{2,1,0:T(8,128)(2,1)}), bf16[32,32,896]{2,1,0:T(8,128)(2,1)S(1)}, u32[]{:S(2)}, u32[]{:S(2)}) %all-to-all-start.1) | async-done | bytes 1835040 | tf_op jit(solution)/shard_map/all_to_all | solution.py:419
  58.1 5.1 %all-to-all-start.3 = ((bf16[32,48,896]{2,1,0:T(8,128)(2,1)}), bf16[32,48,896]{2,1,0:T(8,128)(2,1)}, u32[]{:S(2)}, u32[]{:S(2)}) async-start(bf16[32,48,896]{2,1,0:T(8,128)(2,1)} %bitcast.23), calls=%async_computation.3 | async-start | bytes 5505024 | tf_op jit(solution)/shard_map/all_to_all | solution.py:419
  63.2 5.8 %pad_maximum_fusion = bf16[32,336,256]{2,1,0:T(8,128)(2,1)} fusion(bf16[32,112,256]{2,1,0:T(8,128)(2,1)} %bitcast.26, bf16[32,112,256]{2,1,0:T(8,128)(2,1)} %bitcast.27, bf16[32,112,256]{2,1,0:T(8,128)(2,1)} %bitcast.28), kind=kLoop, calls=%fused_computation | loop fusion | flops 16515072 | bytes 11010048 | tf_op jit(solution)/shard_map/concatenate | solution.py:457
  69.0 29.7 %all-to-all-done.3 = bf16[32,48,896]{2,1,0:T(8,128)(2,1)} async-done(((bf16[32,48,896]{2,1,0:T(8,128)(2,1)}), bf16[32,48,896]{2,1,0:T(8,128)(2,1)}, u32[]{:S(2)}, u32[]{:S(2)}) %all-to-all-start.3) | async-done | bytes 2752544 | tf_op jit(solution)/shard_map/all_to_all | solution.py:419
  98.7 5.4 %all-to-all-start.5 = ((bf16[32,336,256]{2,1,0:T(8,128)(2,1)}), bf16[32,336,256]{2,1,0:T(8,128)(2,1)}, u32[]{:S(2)}, u32[]{:S(2)}) async-start(bf16[32,336,256]{2,1,0:T(8,128)(2,1)} %pad_maximum_fusion), calls=%async_computation.5 | async-start | bytes 11010048 | tf_op jit(solution)/shard_map/all_to_all | solution.py:419
  104.2 1.7 collective-permute-start
  105.9 1.1 fusion
  107.0 1.6 collective-permute-start.6
  108.6 1.0 collective-permute-start.9
  109.7 0.4 collective-permute-start.1
  110.1 2.2 collective-permute-start.2
  112.3 6.3 %collective-permute-done.refs_1_ = bf16[16,16,896]{2,1,0:T(8,128)(2,1)S(1)} collective-permute-done((bf16[16,16,896]{2,1,0:T(8,128)(2,1)S(1)}, bf16[16,16,896]{2,1,0:T(8,128)(2,1)S(1)}, u32[]{:S(2)}, u32[]{:S(2)}) %collective-permute-start) | collective-permute-done | bytes 458784 | tf_op jit(solution)/shard_map/ppermute | solution.py:423
  118.6 1.2 collective-permute-start.3
  119.8 28.3 %collective-permute-done.1.refs_2_.refs_1_ = bf16[16,16,896]{2,1,0:T(8,128)(2,1)S(1)} collective-permute-done((bf16[16,16,896]{2,1,0:T(8,128)(2,1)S(1)}, bf16[16,16,896]{2,1,0:T(8,128)(2,1)S(1)}, u32[]{:S(2)}, u32[]{:S(2)}) %collective-permute-start.1) | collective-permute-done | bytes 458784 | tf_op jit(solution)/shard_map/ppermute | solution.py:423
  148.1 0.7 collective-permute-start.7
  148.8 0.7 collective-permute-done.3.refs_4_.refs_2_
  149.5 2.2 collective-permute-start.8
  151.8 2.7 collective-permute-start.11
  154.5 6.1 %collective-permute-done.4.refs_5_.refs_3_ = bf16[16,16,896]{2,1,0:T(8,128)(2,1)S(1)} collective-permute-done((bf16[16,16,896]{2,1,0:T(8,128)(2,1)S(1)}, bf16[16,16,896]{2,1,0:T(8,128)(2,1)S(1)}, u32[]{:S(2)}, u32[]{:S(2)}) %collective-permute-start.4) | collective-permute-done | bytes 458784 | tf_op jit(solution)/shard_map/ppermute | solution.py:423
  160.6 0.8 copy-done.10
  161.4 4.5 %shard_map.139 = (bf16[768,256]{1,0:T(8,128)(2,1)}, bf16[768,256]{1,0:T(8,128)(2,1)}, bf16[768,256]{1,0:T(8,128)(2,1)}, bf16[768,256]{1,0:T(8,128)(2,1)}) custom-call(s32[1]{0:T(128)} %bitcast.4.dp, bf16[1536,896]{1,0:T(8,128)(2,1)} %bitcast.14.x, bf16[1024,896]{1,0:T(8,128)(2,1)} %bitcast.37), custom_call_target="tpu_custom_call" | custom-call | flops 1409286144 | bytes 4194304 | tf_op jit(solution)/shard_map/pallas_call | solution.py:213
  165.9 33.3 %collective-permute-done.5.refs_6_.refs_3_ = bf16[16,16,896]{2,1,0:T(8,128)(2,1)} collective-permute-done((bf16[16,16,896]{2,1,0:T(8,128)(2,1)}, bf16[16,16,896]{2,1,0:T(8,128)(2,1)}, u32[]{:S(2)}, u32[]{:S(2)}) %collective-permute-start.5) | collective-permute-done | bytes 458784 | tf_op jit(solution)/shard_map/ppermute | solution.py:423
  199.3 1.3 collective-permute-start.21
  200.6 4.5 %shard_map.138 = (bf16[768,256]{1,0:T(8,128)(2,1)}, bf16[768,256]{1,0:T(8,128)(2,1)}, bf16[768,256]{1,0:T(8,128)(2,1)}, bf16[768,256]{1,0:T(8,128)(2,1)}) custom-call(s32[1]{0:T(128)} %bitcast.4.dp, bf16[1536,896]{1,0:T(8,128)(2,1)} %bitcast.14.x, bf16[1024,896]{1,0:T(8,128)(2,1)} %bitcast.38), custom_call_target="tpu_custom_call" | custom-call | flops 1409286144 | bytes 4194304 | tf_op jit(solution)/shard_map/pallas_call | solution.py:213
  205.1 1.2 collective-permute-start.18
  206.3 2.3 collective-permute-start.19
  208.6 1.2 collective-permute-done.21.h1
  209.8 1.2 collective-permute-start.20
  211.0 2.7 collective-permute-start.23
  213.7 12.4 %hidden.1 = (f32[1536,256]{1,0:T(8,128)}, f32[1536,256]{1,0:T(8,128)}, bf16[1536,256]{1,0:T(8,128)(2,1)}) custom-call(s32[1]{0:T(128)} %bitcast.4.dp, bf16[32,16,896]{2,1,0:T(8,128)(2,1)} %copy-done.1, bf16[16,16,896]{2,1,0:T(8,128)(2,1)} %copy-done.8, bf16[16,16,896]{2,1,0:T(8,128)(2,1)} %copy-done.7, bf16[16,16,896]{2,1,0:T(8,128)(2,1)} %copy-done.9, ...), custom_call_target="tpu_custom_call" | custom-call | flops 5637144576 | bytes 18350080 | tf_op jit(solution)/shard_map/hidden/pallas_call | solution.py:179
  226.1 9.8 %collective-permute-done.22.h2 = bf16[768,256]{1,0:T(8,128)(2,1)S(1)} collective-permute-done((bf16[768,256]{1,0:T(8,128)(2,1)}, bf16[768,256]{1,0:T(8,128)(2,1)S(1)}, u32[]{:S(2)}, u32[]{:S(2)}) %collective-permute-start.22) | collective-permute-done | bytes 393248 | tf_op jit(solution)/shard_map/ppermute | solution.py:423
  235.9 4.2 collective-permute-done.23.h3
  240.1 0.7 copy-done.15
  240.8 7.8 %shard_map.140.refs_8_ = f32[256,3584]{1,0:T(8,128)} custom-call(s32[1]{0:T(128)} %bitcast.4.dp, bf16[768,256]{1,0:T(8,128)(2,1)} %get-tuple-element.33.h0, bf16[768,256]{1,0:T(8,128)(2,1)} %collective-permute-done.21.h1, bf16[768,256]{1,0:T(8,128)(2,1)} %copy-done.14, bf16[768,256]{1,0:T(8,128)(2,1)} %copy-done.15, f32[1536,256]{1,0:T(8,128)} %get-tuple-element.31.g_in, ...), custom_call_target="tpu_custom_call" | custom-call | flops 1409286144 | bytes 13893632 | tf_op jit(solution)/shard_map/pallas_call | solution.py:286
  248.7 0.7 copy-done.11
  249.7 8.8 %shard_map.141 = bf16[3584,256]{1,0:T(8,128)(2,1)} custom-call(s32[1]{0:T(128)} %bitcast.4.dp, bf16[768,256]{1,0:T(8,128)(2,1)} %get-tuple-element.27.h0, bf16[768,256]{1,0:T(8,128)(2,1)} %copy-done.11, bf16[768,256]{1,0:T(8,128)(2,1)} %copy-done.12, bf16[768,256]{1,0:T(8,128)(2,1)} %copy-done.13, f32[1536,256]{1,0:T(8,128)} %get-tuple-element.31.g_in, ...), custom_call_target="tpu_custom_call" | custom-call | flops 1409286144 | bytes 13893632 | tf_op jit(solution)/shard_map/pallas_call | solution.py:286
  258.5 11.3 %all-to-all-start.4 = ((bf16[32,112,256]{2,1,0:T(8,128)(2,1)}), bf16[32,112,256]{2,1,0:T(8,128)(2,1)S(1)}, u32[]{:S(2)}, u32[]{:S(2)}) async-start(bf16[32,112,256]{2,1,0:T(8,128)(2,1)} %bitcast.24), calls=%async_computation.4 | async-start | bytes 3670016 | tf_op jit(solution)/shard_map/all_to_all | solution.py:419
  269.9 1.9 collective-permute-start.12
  271.8 0.9 collective-permute-start.15
  272.7 0.6 collective-permute-start.13
  273.3 2.1 collective-permute-start.14
  275.3 6.3 %collective-permute-done.12.refs_1_ = bf16[16,48,256]{2,1,0:T(8,128)(2,1)S(1)} collective-permute-done((bf16[16,48,256]{2,1,0:T(8,128)(2,1)S(1)}, bf16[16,48,256]{2,1,0:T(8,128)(2,1)S(1)}, u32[]{:S(2)}, u32[]{:S(2)}) %collective-permute-start.12) | collective-permute-done | bytes 393248 | tf_op jit(solution)/shard_map/ppermute | solution.py:423
  281.6 0.6 collective-permute-start.16
  282.3 2.1 collective-permute-start.17
  284.3 5.7 %collective-permute-done.13.refs_2_ = bf16[16,48,256]{2,1,0:T(8,128)(2,1)S(1)} collective-permute-done((bf16[16,48,256]{2,1,0:T(8,128)(2,1)S(1)}, bf16[16,48,256]{2,1,0:T(8,128)(2,1)S(1)}, u32[]{:S(2)}, u32[]{:S(2)}) %collective-permute-start.13) | collective-permute-done | bytes 393248 | tf_op jit(solution)/shard_map/ppermute | solution.py:423
  290.1 0.3 collective-permute-done.14.refs_3_
  290.4 8.1 %collective-permute-done.16.refs_5_ = bf16[16,48,256]{2,1,0:T(8,128)(2,1)S(1)} collective-permute-done((bf16[16,48,256]{2,1,0:T(8,128)(2,1)S(1)}, bf16[16,48,256]{2,1,0:T(8,128)(2,1)S(1)}, u32[]{:S(2)}, u32[]{:S(2)}) %collective-permute-start.16) | collective-permute-done | bytes 393248 | tf_op jit(solution)/shard_map/ppermute | solution.py:423
  298.5 0.3 collective-permute-done.17.refs_6_
  298.8 0.4 copy-done.20
  299.2 0.7 copy-done.21
  300.0 7.6 %outputs.1 = bf16[1536,896]{1,0:T(8,128)(2,1)} custom-call(s32[1]{0:T(128)} %bitcast.4.dp, bf16[32,48,256]{2,1,0:T(8,128)(2,1)} %bitcast.30, bf16[16,48,256]{2,1,0:T(8,128)(2,1)} %copy-done.16, bf16[16,48,256]{2,1,0:T(8,128)(2,1)} %copy-done.18, bf16[16,48,256]{2,1,0:T(8,128)(2,1)} %copy-done.19, bf16[16,48,256]{2,1,0:T(8,128)(2,1)} %copy-done.17, ...), custom_call_target="tpu_custom_call" | custom-call | flops 2818572288 | bytes 5898240 | tf_op jit(solution)/shard_map/outputs/pallas_call | solution.py:315
  307.7 1.2 copy-done.3
  308.9 8.1 %all-to-all-start.2 = ((bf16[32,48,896]{2,1,0:T(8,128)(2,1)}), bf16[32,48,896]{2,1,0:T(8,128)(2,1)S(1)}, u32[]{:S(2)}, u32[]{:S(2)}) async-start(bf16[32,48,896]{2,1,0:T(8,128)(2,1)} %bitcast.25), calls=%async_computation.2 | async-start | bytes 5505024 | tf_op jit(solution)/shard_map/all_to_all | solution.py:419
  317.0 10.0 %update.1 = bf16[32,3,112,256]{3,2,1,0:T(8,128)(2,1)} custom-call(s32[32]{0:T(128)} %plan.1, s32[32]{0:T(128)} %placement.1, bf16[32,112,256]{2,1,0:T(8,128)(2,1)} %copy-done.3, bf16[32,336,256]{2,1,0:T(8,128)(2,1)} %all-to-all-done.5.gate.first.second, bf16[32,336,256]{2,1,0:T(8,128)(2,1)} %all-to-all-done.5.gate.first.second, ...), custom_call_target="tpu_custom_call" | custom-call | flops 18350080 | bytes 10485760 | tf_op jit(solution)/shard_map/update/pallas_call | solution.py:384
  327.0 25.3 %all-to-all-done.2 = bf16[32,48,896]{2,1,0:T(8,128)(2,1)S(1)} async-done(((bf16[32,48,896]{2,1,0:T(8,128)(2,1)}), bf16[32,48,896]{2,1,0:T(8,128)(2,1)S(1)}, u32[]{:S(2)}, u32[]{:S(2)}) %all-to-all-start.2) | async-done | bytes 2752544 | tf_op jit(solution)/shard_map/all_to_all | solution.py:419
  352.3 1.6 copy-done.2
  353.8 5.4 %all-to-all-start.6 = ((bf16[32,3,112,256]{3,2,1,0:T(8,128)(2,1)}), bf16[32,3,112,256]{3,2,1,0:T(8,128)(2,1)}, u32[]{:S(2)}, u32[]{:S(2)}) async-start(bf16[32,3,112,256]{3,2,1,0:T(8,128)(2,1)} %update.1), calls=%async_computation.6 | async-start | bytes 11010048 | tf_op jit(solution)/shard_map/all_to_all | solution.py:419
  359.2 3.7 combine.1
  363.0 64.1 %all-to-all-done.6.moments = bf16[32,3,112,256]{3,2,1,0:T(8,128)(2,1)} async-done(((bf16[32,3,112,256]{3,2,1,0:T(8,128)(2,1)}), bf16[32,3,112,256]{3,2,1,0:T(8,128)(2,1)}, u32[]{:S(2)}, u32[]{:S(2)}) %all-to-all-start.6) | async-done | bytes 5505056 | tf_op jit(solution)/shard_map/all_to_all | solution.py:419
  427.1 5.5 %finish.1 = (bf16[32,112,256]{2,1,0:T(8,128)(2,1)}, bf16[32,112,256]{2,1,0:T(8,128)(2,1)}, bf16[32,112,256]{2,1,0:T(8,128)(2,1)}) custom-call(bf16[32,3,112,256]{3,2,1,0:T(8,128)(2,1)} %all-to-all-done.6.moments), custom_call_target="tpu_custom_call" | custom-call | bytes 12582912 | tf_op jit(solution)/shard_map/finish/pallas_call | solution.py:407
  (56 shorter events, 0.5 us)
Async XLA Ops:
  28.7 75.4 %copy-start.1 = (bf16[32,16,896]{2,1,0:T(8,128)(2,1)}, bf16[32,16,896]{2,1,0:T(8,128)(2,1)S(1)}, u32[]{:S(2)}) copy-start(bf16[32,16,896]{2,1,0:T(8,128)(2,1)S(1)} %all_to_all.35.refs_0_) | copy-start | bytes 2752516
  28.7 29.4 %all-to-all-start.1 = ((bf16[32,32,896]{2,1,0:T(8,128)(2,1)}), bf16[32,32,896]{2,1,0:T(8,128)(2,1)S(1)}, u32[]{:S(2)}, u32[]{:S(2)}) async-start(bf16[32,32,896]{2,1,0:T(8,128)(2,1)} %get-tuple-element.24), calls=%async_computation.1 | async-start | bytes 3670016 | tf_op jit(solution)/shard_map/all_to_all | solution.py:419
  58.1 47.8 %copy-start = (bf16[32,32,896]{2,1,0:T(8,128)(2,1)}, bf16[32,32,896]{2,1,0:T(8,128)(2,1)S(1)}, u32[]{:S(2)}) copy-start(bf16[32,32,896]{2,1,0:T(8,128)(2,1)S(1)} %all-to-all-done.1.refs_7_.refs_4_) | copy-start | bytes 5505028
  58.1 40.6 %all-to-all-start.3 = ((bf16[32,48,896]{2,1,0:T(8,128)(2,1)}), bf16[32,48,896]{2,1,0:T(8,128)(2,1)}, u32[]{:S(2)}, u32[]{:S(2)}) async-start(bf16[32,48,896]{2,1,0:T(8,128)(2,1)} %bitcast.23), calls=%async_computation.3 | async-start | bytes 5505024 | tf_op jit(solution)/shard_map/all_to_all | solution.py:419
  98.7 159.8 %all-to-all-start.5 = ((bf16[32,336,256]{2,1,0:T(8,128)(2,1)}), bf16[32,336,256]{2,1,0:T(8,128)(2,1)}, u32[]{:S(2)}, u32[]{:S(2)}) async-start(bf16[32,336,256]{2,1,0:T(8,128)(2,1)} %pad_maximum_fusion), calls=%async_computation.5 | async-start | bytes 11010048 | tf_op jit(solution)/shard_map/all_to_all | solution.py:419
  104.2 14.4 %collective-permute-start = (bf16[16,16,896]{2,1,0:T(8,128)(2,1)S(1)}, bf16[16,16,896]{2,1,0:T(8,128)(2,1)S(1)}, u32[]{:S(2)}, u32[]{:S(2)}) collective-permute-start(bf16[16,16,896]{2,1,0:T(8,128)(2,1)S(1)} %get-tuple-element.43), channel_id=1, source_target_pairs={{0,32},{32,64},{64,96},{96,0},{1,33},{33,65},{65,97},{97,1},{2,34}... | collective-permute-start | bytes 1376264 | tf_op jit(solution)/shard_map/ppermute | solution.py:423
  107.0 44.8 %collective-permute-start.6 = (bf16[16,32,896]{2,1,0:T(8,128)(2,1)S(1)}, bf16[16,32,896]{2,1,0:T(8,128)(2,1)S(1)}, u32[]{:S(2)}, u32[]{:S(2)}) collective-permute-start(bf16[16,32,896]{2,1,0:T(8,128)(2,1)S(1)} %get-tuple-element.41), channel_id=1, source_target_pairs={{0,32},{32,64},{64,96},{96,0},{1,33},{33,65},{65,97},{97,1},{2,34}... | collective-permute-start | bytes 2752520 | tf_op jit(solution)/shard_map/ppermute | solution.py:423
  108.6 43.2 %collective-permute-start.9 = (bf16[16,32,896]{2,1,0:T(8,128)(2,1)}, bf16[16,32,896]{2,1,0:T(8,128)(2,1)S(1)}, u32[]{:S(2)}, u32[]{:S(2)}) collective-permute-start(bf16[16,32,896]{2,1,0:T(8,128)(2,1)} %get-tuple-element.40), channel_id=1, source_target_pairs={{0,96},{32,0},{64,32},{96,64},{1,97},{33,1},{65,33},{97,65},{2,98}... | collective-permute-start | bytes 2752520 | tf_op jit(solution)/shard_map/ppermute | solution.py:423
  109.7 38.4 %collective-permute-start.1 = (bf16[16,16,896]{2,1,0:T(8,128)(2,1)S(1)}, bf16[16,16,896]{2,1,0:T(8,128)(2,1)S(1)}, u32[]{:S(2)}, u32[]{:S(2)}) collective-permute-start(bf16[16,16,896]{2,1,0:T(8,128)(2,1)S(1)} %get-tuple-element.42), channel_id=1, source_target_pairs={{0,32},{32,64},{64,96},{96,0},{1,33},{33,65},{65,97},{97,1},{2,34}... | collective-permute-start | bytes 1376264 | tf_op jit(solution)/shard_map/ppermute | solution.py:423
  110.1 38.0 %collective-permute-start.2 = (bf16[16,16,896]{2,1,0:T(8,128)(2,1)S(1)}, bf16[16,16,896]{2,1,0:T(8,128)(2,1)S(1)}, u32[]{:S(2)}, u32[]{:S(2)}) collective-permute-start(bf16[16,16,896]{2,1,0:T(8,128)(2,1)S(1)} %get-tuple-element.43), channel_id=1, source_target_pairs={{0,96},{32,0},{64,32},{96,64},{1,97},{33,1},{65,33},{97,65},{2,98}... | collective-permute-start | bytes 1376264 | tf_op jit(solution)/shard_map/ppermute | solution.py:423
  118.6 33.2 %copy-start.8 = (bf16[16,16,896]{2,1,0:T(8,128)(2,1)}, bf16[16,16,896]{2,1,0:T(8,128)(2,1)S(1)}, u32[]{:S(2)}) copy-start(bf16[16,16,896]{2,1,0:T(8,128)(2,1)S(1)} %collective-permute-done.refs_1_) | copy-start | bytes 1376260
  118.6 30.9 %collective-permute-start.3 = (bf16[16,16,896]{2,1,0:T(8,128)(2,1)S(1)}, bf16[16,16,896]{2,1,0:T(8,128)(2,1)}, u32[]{:S(2)}, u32[]{:S(2)}) collective-permute-start(bf16[16,16,896]{2,1,0:T(8,128)(2,1)S(1)} %get-tuple-element.42), channel_id=1, source_target_pairs={{0,96},{32,0},{64,32},{96,64},{1,97},{33,1},{65,33},{97,65},{2,98}... | collective-permute-start | bytes 1376264 | tf_op jit(solution)/shard_map/ppermute | solution.py:423
  148.1 57.0 %copy-start.7 = (bf16[16,16,896]{2,1,0:T(8,128)(2,1)}, bf16[16,16,896]{2,1,0:T(8,128)(2,1)S(1)}, u32[]{:S(2)}) copy-start(bf16[16,16,896]{2,1,0:T(8,128)(2,1)S(1)} %collective-permute-done.1.refs_2_.refs_1_) | copy-start | bytes 1376260
  148.1 12.5 %collective-permute-start.4 = (bf16[16,16,896]{2,1,0:T(8,128)(2,1)S(1)}, bf16[16,16,896]{2,1,0:T(8,128)(2,1)S(1)}, u32[]{:S(2)}, u32[]{:S(2)}) collective-permute-start(bf16[16,16,896]{2,1,0:T(8,128)(2,1)S(1)} %collective-permute-done.refs_1_), channel_id=1, source_target_pairs={{0,32},{32,64},{64,96},{96,0},{1,33},{33,65},{65,97},{97,1},{2,34}... | collective-permute-start | bytes 1376264 | tf_op jit(solution)/shard_map/ppermute | solution.py:423
  148.1 12.5 %copy-start.9 = (bf16[16,16,896]{2,1,0:T(8,128)(2,1)}, bf16[16,16,896]{2,1,0:T(8,128)(2,1)S(1)}, u32[]{:S(2)}) copy-start(bf16[16,16,896]{2,1,0:T(8,128)(2,1)S(1)} %collective-permute-done.2.refs_3_.refs_2_) | copy-start | bytes 1376260
  148.1 57.0 %collective-permute-start.7 = (bf16[16,32,896]{2,1,0:T(8,128)(2,1)}, bf16[16,32,896]{2,1,0:T(8,128)(2,1)}, u32[]{:S(2)}, u32[]{:S(2)}) collective-permute-start(bf16[16,32,896]{2,1,0:T(8,128)(2,1)} %get-tuple-element.40), channel_id=1, source_target_pairs={{0,32},{32,64},{64,96},{96,0},{1,33},{33,65},{65,97},{97,1},{2,34}... | collective-permute-start | bytes 2752520 | tf_op jit(solution)/shard_map/ppermute | solution.py:423
  149.5 56.8 %collective-permute-start.8 = (bf16[16,32,896]{2,1,0:T(8,128)(2,1)S(1)}, bf16[16,32,896]{2,1,0:T(8,128)(2,1)}, u32[]{:S(2)}, u32[]{:S(2)}) collective-permute-start(bf16[16,32,896]{2,1,0:T(8,128)(2,1)S(1)} %get-tuple-element.41), channel_id=1, source_target_pairs={{0,96},{32,0},{64,32},{96,64},{1,97},{33,1},{65,33},{97,65},{2,98}... | collective-permute-start | bytes 2752520 | tf_op jit(solution)/shard_map/ppermute | solution.py:423
  151.8 53.3 %copy-start.5 = (bf16[16,32,896]{2,1,0:T(8,128)(2,1)}, bf16[16,32,896]{2,1,0:T(8,128)(2,1)S(1)}, u32[]{:S(2)}) copy-start(bf16[16,32,896]{2,1,0:T(8,128)(2,1)S(1)} %collective-permute-done.6.refs_8_.refs_5_) | copy-start | bytes 2752516
  151.8 59.2 %collective-permute-start.10 = (bf16[16,32,896]{2,1,0:T(8,128)(2,1)S(1)}, bf16[16,32,896]{2,1,0:T(8,128)(2,1)}, u32[]{:S(2)}, u32[]{:S(2)}) collective-permute-start(bf16[16,32,896]{2,1,0:T(8,128)(2,1)S(1)} %collective-permute-done.6.refs_8_.refs_5_), channel_id=1, source_target_pairs={{0,32},{32,64},{64,96},{96,0},{1,33},{33,65},{65,97},{97,1},{2,34}... | collective-permute-start | bytes 2752520 | tf_op jit(solution)/shard_map/ppermute | solution.py:423
  151.8 53.3 %copy-start.4 = (bf16[16,32,896]{2,1,0:T(8,128)(2,1)}, bf16[16,32,896]{2,1,0:T(8,128)(2,1)S(1)}, u32[]{:S(2)}) copy-start(bf16[16,32,896]{2,1,0:T(8,128)(2,1)S(1)} %collective-permute-done.9.refs_11_.refs_6_) | copy-start | bytes 2752516
  151.8 59.2 %collective-permute-start.11 = (bf16[16,32,896]{2,1,0:T(8,128)(2,1)S(1)}, bf16[16,32,896]{2,1,0:T(8,128)(2,1)}, u32[]{:S(2)}, u32[]{:S(2)}) collective-permute-start(bf16[16,32,896]{2,1,0:T(8,128)(2,1)S(1)} %collective-permute-done.9.refs_11_.refs_6_), channel_id=1, source_target_pairs={{0,96},{32,0},{64,32},{96,64},{1,97},{33,1},{65,33},{97,65},{2,98}... | collective-permute-start | bytes 2752520 | tf_op jit(solution)/shard_map/ppermute | solution.py:423
  160.6 0.8 copy-start.10
  161.4 37.9 %collective-permute-start.5 = (bf16[16,16,896]{2,1,0:T(8,128)(2,1)}, bf16[16,16,896]{2,1,0:T(8,128)(2,1)}, u32[]{:S(2)}, u32[]{:S(2)}) collective-permute-start(bf16[16,16,896]{2,1,0:T(8,128)(2,1)} %collective-permute-done.3.refs_4_.refs_2_), channel_id=1, source_target_pairs={{0,96},{32,0},{64,32},{96,64},{1,97},{33,1},{65,33},{97,65},{2,98}... | collective-permute-start | bytes 1376264 | tf_op jit(solution)/shard_map/ppermute | solution.py:423
  199.3 10.5 %collective-permute-start.21 = (bf16[768,256]{1,0:T(8,128)(2,1)}, bf16[768,256]{1,0:T(8,128)(2,1)}, u32[]{:S(2)}, u32[]{:S(2)}) collective-permute-start(bf16[768,256]{1,0:T(8,128)(2,1)} %get-tuple-element.34), channel_id=1, source_target_pairs={{0,32},{32,64},{64,96},{96,0},{1,33},{33,65},{65,97},{97,1},{2,34}... | collective-permute-start | bytes 1179656 | tf_op jit(solution)/shard_map/ppermute | solution.py:423
  205.1 43.5 %collective-permute-start.18 = (bf16[768,256]{1,0:T(8,128)(2,1)}, bf16[768,256]{1,0:T(8,128)(2,1)S(1)}, u32[]{:S(2)}, u32[]{:S(2)}) collective-permute-start(bf16[768,256]{1,0:T(8,128)(2,1)} %get-tuple-element.28), channel_id=1, source_target_pairs={{0,32},{32,64},{64,96},{96,0},{1,33},{33,65},{65,97},{97,1},{2,34}... | collective-permute-start | bytes 1179656 | tf_op jit(solution)/shard_map/ppermute | solution.py:423
  206.3 42.3 %collective-permute-start.19 = (bf16[768,256]{1,0:T(8,128)(2,1)}, bf16[768,256]{1,0:T(8,128)(2,1)S(1)}, u32[]{:S(2)}, u32[]{:S(2)}) collective-permute-start(bf16[768,256]{1,0:T(8,128)(2,1)} %get-tuple-element.29), channel_id=1, source_target_pairs={{0,64},{32,96},{64,0},{96,32},{1,65},{33,97},{65,1},{97,33},{2,66}... | collective-permute-start | bytes 1179656 | tf_op jit(solution)/shard_map/ppermute | solution.py:423
  209.8 38.9 %collective-permute-start.20 = (bf16[768,256]{1,0:T(8,128)(2,1)}, bf16[768,256]{1,0:T(8,128)(2,1)S(1)}, u32[]{:S(2)}, u32[]{:S(2)}) collective-permute-start(bf16[768,256]{1,0:T(8,128)(2,1)} %get-tuple-element.30), channel_id=1, source_target_pairs={{0,96},{32,0},{64,32},{96,64},{1,97},{33,1},{65,33},{97,65},{2,98}... | collective-permute-start | bytes 1179656 | tf_op jit(solution)/shard_map/ppermute | solution.py:423
  211.0 24.9 %collective-permute-start.22 = (bf16[768,256]{1,0:T(8,128)(2,1)}, bf16[768,256]{1,0:T(8,128)(2,1)S(1)}, u32[]{:S(2)}, u32[]{:S(2)}) collective-permute-start(bf16[768,256]{1,0:T(8,128)(2,1)} %get-tuple-element.35), channel_id=1, source_target_pairs={{0,64},{32,96},{64,0},{96,32},{1,65},{33,97},{65,1},{97,33},{2,66}... | collective-permute-start | bytes 1179656 | tf_op jit(solution)/shard_map/ppermute | solution.py:423
  211.0 29.1 %collective-permute-start.23 = (bf16[768,256]{1,0:T(8,128)(2,1)}, bf16[768,256]{1,0:T(8,128)(2,1)S(1)}, u32[]{:S(2)}, u32[]{:S(2)}) collective-permute-start(bf16[768,256]{1,0:T(8,128)(2,1)} %get-tuple-element.36), channel_id=1, source_target_pairs={{0,96},{32,0},{64,32},{96,64},{1,97},{33,1},{65,33},{97,65},{2,98}... | collective-permute-start | bytes 1179656 | tf_op jit(solution)/shard_map/ppermute | solution.py:423
  235.9 4.2 copy-start.14
  240.0 0.7 copy-start.15
  248.6 0.7 copy-start.11
  248.6 0.9 copy-start.12
  248.7 1.0 copy-start.13
  258.5 11.4 %copy-start.6 = (bf16[1536,256]{1,0:T(8,128)(2,1)S(1)}, bf16[1536,256]{1,0:T(8,128)(2,1)}, u32[]{:S(2)}) copy-start(bf16[1536,256]{1,0:T(8,128)(2,1)} %get-tuple-element.25) | copy-start | bytes 2359300
  258.5 49.1 %all-to-all-start.4 = ((bf16[32,112,256]{2,1,0:T(8,128)(2,1)}), bf16[32,112,256]{2,1,0:T(8,128)(2,1)S(1)}, u32[]{:S(2)}, u32[]{:S(2)}) async-start(bf16[32,112,256]{2,1,0:T(8,128)(2,1)} %bitcast.24), calls=%async_computation.4 | async-start | bytes 3670016 | tf_op jit(solution)/shard_map/all_to_all | solution.py:419
  269.9 11.7 %collective-permute-start.12 = (bf16[16,48,256]{2,1,0:T(8,128)(2,1)S(1)}, bf16[16,48,256]{2,1,0:T(8,128)(2,1)S(1)}, u32[]{:S(2)}, u32[]{:S(2)}) collective-permute-start(bf16[16,48,256]{2,1,0:T(8,128)(2,1)S(1)} %bitcast.31), channel_id=1, source_target_pairs={{0,32},{32,64},{64,96},{96,0},{1,33},{33,65},{65,97},{97,1},{2,34}... | collective-permute-start | bytes 1179656 | tf_op jit(solution)/shard_map/ppermute | solution.py:423
  271.8 10.4 %collective-permute-start.15 = (bf16[16,48,256]{2,1,0:T(8,128)(2,1)S(1)}, bf16[16,48,256]{2,1,0:T(8,128)(2,1)S(1)}, u32[]{:S(2)}, u32[]{:S(2)}) collective-permute-start(bf16[16,48,256]{2,1,0:T(8,128)(2,1)S(1)} %bitcast.33), channel_id=1, source_target_pairs={{0,96},{32,0},{64,32},{96,64},{1,97},{33,1},{65,33},{97,65},{2,98}... | collective-permute-start | bytes 1179656 | tf_op jit(solution)/shard_map/ppermute | solution.py:423
  272.7 17.4 %collective-permute-start.13 = (bf16[16,48,256]{2,1,0:T(8,128)(2,1)S(1)}, bf16[16,48,256]{2,1,0:T(8,128)(2,1)S(1)}, u32[]{:S(2)}, u32[]{:S(2)}) collective-permute-start(bf16[16,48,256]{2,1,0:T(8,128)(2,1)S(1)} %bitcast.34), channel_id=1, source_target_pairs={{0,32},{32,64},{64,96},{96,0},{1,33},{33,65},{65,97},{97,1},{2,34}... | collective-permute-start | bytes 1179656 | tf_op jit(solution)/shard_map/ppermute | solution.py:423
  273.3 17.1 %collective-permute-start.14 = (bf16[16,48,256]{2,1,0:T(8,128)(2,1)S(1)}, bf16[16,48,256]{2,1,0:T(8,128)(2,1)S(1)}, u32[]{:S(2)}, u32[]{:S(2)}) collective-permute-start(bf16[16,48,256]{2,1,0:T(8,128)(2,1)S(1)} %bitcast.32), channel_id=1, source_target_pairs={{0,96},{32,0},{64,32},{96,64},{1,97},{33,1},{65,33},{97,65},{2,98}... | collective-permute-start | bytes 1179656 | tf_op jit(solution)/shard_map/ppermute | solution.py:423
  281.6 18.3 %copy-start.16 = (bf16[16,48,256]{2,1,0:T(8,128)(2,1)}, bf16[16,48,256]{2,1,0:T(8,128)(2,1)S(1)}, u32[]{:S(2)}) copy-start(bf16[16,48,256]{2,1,0:T(8,128)(2,1)S(1)} %collective-permute-done.12.refs_1_) | copy-start | bytes 1179652
  281.6 16.9 %collective-permute-start.16 = (bf16[16,48,256]{2,1,0:T(8,128)(2,1)S(1)}, bf16[16,48,256]{2,1,0:T(8,128)(2,1)S(1)}, u32[]{:S(2)}, u32[]{:S(2)}) collective-permute-start(bf16[16,48,256]{2,1,0:T(8,128)(2,1)S(1)} %collective-permute-done.12.refs_1_), channel_id=1, source_target_pairs={{0,32},{32,64},{64,96},{96,0},{1,33},{33,65},{65,97},{97,1},{2,34}... | collective-permute-start | bytes 1179656 | tf_op jit(solution)/shard_map/ppermute | solution.py:423
  282.3 17.7 %copy-start.17 = (bf16[16,48,256]{2,1,0:T(8,128)(2,1)}, bf16[16,48,256]{2,1,0:T(8,128)(2,1)S(1)}, u32[]{:S(2)}) copy-start(bf16[16,48,256]{2,1,0:T(8,128)(2,1)S(1)} %collective-permute-done.15.refs_4_) | copy-start | bytes 1179652
  282.3 16.6 %collective-permute-start.17 = (bf16[16,48,256]{2,1,0:T(8,128)(2,1)S(1)}, bf16[16,48,256]{2,1,0:T(8,128)(2,1)S(1)}, u32[]{:S(2)}, u32[]{:S(2)}) collective-permute-start(bf16[16,48,256]{2,1,0:T(8,128)(2,1)S(1)} %collective-permute-done.15.refs_4_), channel_id=1, source_target_pairs={{0,96},{32,0},{64,32},{96,64},{1,97},{33,1},{65,33},{97,65},{2,98}... | collective-permute-start | bytes 1179656 | tf_op jit(solution)/shard_map/ppermute | solution.py:423
  290.1 9.9 %copy-start.18 = (bf16[16,48,256]{2,1,0:T(8,128)(2,1)}, bf16[16,48,256]{2,1,0:T(8,128)(2,1)S(1)}, u32[]{:S(2)}) copy-start(bf16[16,48,256]{2,1,0:T(8,128)(2,1)S(1)} %collective-permute-done.13.refs_2_) | copy-start | bytes 1179652
  290.4 9.6 %copy-start.19 = (bf16[16,48,256]{2,1,0:T(8,128)(2,1)}, bf16[16,48,256]{2,1,0:T(8,128)(2,1)S(1)}, u32[]{:S(2)}) copy-start(bf16[16,48,256]{2,1,0:T(8,128)(2,1)S(1)} %collective-permute-done.14.refs_3_) | copy-start | bytes 1179652
  298.5 0.7 copy-start.20
  299.2 0.7 copy-start.21
  307.6 1.2 copy-start.3
  308.9 43.4 %all-to-all-start.2 = ((bf16[32,48,896]{2,1,0:T(8,128)(2,1)}), bf16[32,48,896]{2,1,0:T(8,128)(2,1)S(1)}, u32[]{:S(2)}, u32[]{:S(2)}) async-start(bf16[32,48,896]{2,1,0:T(8,128)(2,1)} %bitcast.25), calls=%async_computation.2 | async-start | bytes 5505024 | tf_op jit(solution)/shard_map/all_to_all | solution.py:419
  352.3 1.6 copy-start.2
  353.8 73.3 %all-to-all-start.6 = ((bf16[32,3,112,256]{3,2,1,0:T(8,128)(2,1)}), bf16[32,3,112,256]{3,2,1,0:T(8,128)(2,1)}, u32[]{:S(2)}, u32[]{:S(2)}) async-start(bf16[32,3,112,256]{3,2,1,0:T(8,128)(2,1)} %update.1), calls=%async_computation.6 | async-start | bytes 11010048 | tf_op jit(solution)/shard_map/all_to_all | solution.py:419

commit v3 on v2

--- a/solution.py
+++ b/solution.py
@@ -49,8 +49,7 @@
     return pl.CostEstimate(flops=flops, transcendentals=0, bytes_accessed=nbytes)
 
 
-def select_kernel(index, place, routes, weights, tokens, *outs):
-    rows_out, (sel_out, selw_out) = outs[: len(CHUNKS)], outs[len(CHUNKS) :]
+def select_kernel(index, place, routes, weights, tokens, out, pos_out, wt_out, sel):
     me = index[0].astype(f32)
     a = lax.broadcasted_iota(jnp.int32, (SLOTS, SLOTS), 0)
     b = lax.broadcasted_iota(jnp.int32, (SLOTS, SLOTS), 1)
@@ -72,49 +71,96 @@
     before = jnp.where(t0 < t1, 1.0, 0.0).astype(bf16)
     pos = jnp.dot(hit.astype(bf16), before, preferred_element_type=f32)
     pos = jnp.where(hit > 0.5, pos, -1.0)
-    want = lax.broadcasted_iota(jnp.int32, (CAP, TOK), 0).astype(f32)
+    pos_out[...] = pos
+    wt_out[...] = wt
+    mark_rows(pos, wt, CHUNKS[0], sel, None)
+    spread_rows(CHUNKS[0], sel, tokens, out)
+
+
+def mark_rows(pos, wt, chunk, sel, selw):
+    lo, hi = chunk
+    want = (lax.broadcasted_iota(jnp.int32, (hi - lo, TOK), 0) + lo).astype(f32)
     for j in range(SLOTS):
         chosen = jnp.abs(pos[j : j + 1, :] - want) < 0.5
-        sel_out[j * CAP : (j + 1) * CAP, :] = jnp.where(chosen, 1.0, 0.0).astype(bf16)
-        selw_out[j * CAP : (j + 1) * CAP, :] = jnp.where(chosen, wt[j : j + 1, :], 0.0)
+        if sel is not None:
+            sel[j] = jnp.where(chosen, 1.0, 0.0).astype(bf16)
+        if selw is not None:
+            selw[j] = jnp.where(chosen, wt[j : j + 1, :], 0.0)
+
+
+def spread_rows(chunk, sel, values, out):
+    rows = chunk[1] - chunk[0]
+    group = 256 // rows
+    for j in range(0, SLOTS, group):
+        picks = sel[j : j + group].reshape(group * rows, TOK)
+        got = jnp.dot(picks, values[...], preferred_element_type=f32).astype(bf16)
+        out[j : j + group] = got.reshape(group, rows, QD)
+
+
+def select_rows(index, placement, routes, weights, tokens):
+    rows = CHUNKS[0][1]
+    return pl.pallas_call(
+        select_kernel,
+        out_shape=[
+            jax.ShapeDtypeStruct((SLOTS, rows, QD), bf16),
+            jax.ShapeDtypeStruct((SLOTS, TOK), f32),
+            jax.ShapeDtypeStruct((SLOTS, TOK), f32),
+        ],
+        in_specs=[sspec()] + [vspec()] * 4,
+        out_specs=[vspec()] * 3,
+        scratch_shapes=[VMEM((SLOTS, rows, TOK), bf16)],
+        cost_estimate=cost(2 * ROWS * TOK * QD // 3, 2 << 20),
+        name="select_rows",
+    )(index, placement[None, :], routes.T, weights.T, tokens)
+
+
+def rest_kernel(pos_in, tokens, out, sel):
+    pos = pos_in[...]
+    mark_rows(pos, None, CHUNKS[1], sel, None)
+    spread_rows(CHUNKS[1], sel, tokens, out)
+
+
+def rest_rows(pos, tokens):
+    lo, hi = CHUNKS[1]
+    return pl.pallas_call(
+        rest_kernel,
+        out_shape=jax.ShapeDtypeStruct((SLOTS, hi - lo, QD), bf16),
+        in_specs=[vspec()] * 2,
+        out_specs=vspec(),
+        scratch_shapes=[VMEM((SLOTS, hi - lo, TOK), bf16)],
+        cost_estimate=cost(2 * ROWS * TOK * QD, 4 << 20),
+        name="rest_rows",
+    )(pos, tokens)
+
+
+def scale_kernel(pos_in, wt_in, cot, out, high_out, low_out, selw):
+    mark_rows(pos_in[...], wt_in[...], (0, CAP), None, selw)
     group = 8
     for j in range(0, SLOTS, group):
-        sel = sel_out[j * CAP : (j + group) * CAP, :]
-        got = jnp.dot(sel, tokens[...], preferred_element_type=f32).astype(bf16)
-        got = got.reshape(group, CAP, QD)
-        for (lo, hi), out in zip(CHUNKS, rows_out):
-            out[j : j + group] = got[:, lo:hi]
-
-
-def select_rows(index, placement, routes, weights, tokens):
-    return pl.pallas_call(
-        select_kernel,
-        out_shape=[jax.ShapeDtypeStruct((SLOTS, hi - lo, QD), bf16) for lo, hi in CHUNKS]
-        + [jax.ShapeDtypeStruct((ROWS, TOK), bf16), jax.ShapeDtypeStruct((ROWS, TOK), f32)],
-        in_specs=[sspec()] + [vspec()] * 4,
-        out_specs=[vspec()] * (len(CHUNKS) + 2),
+        w = selw[j : j + group].reshape(group * CAP, TOK)
+        picks = jnp.where(w != 0.0, 1.0, 0.0).astype(bf16)
+        picked = jnp.dot(picks, cot[...], preferred_element_type=f32)
+        rows = pl.ds(j * CAP, group * CAP)
+        out[rows, :] = (jnp.sum(w, axis=1, keepdims=True) * picked).astype(bf16)
+        high = w.astype(bf16)
+        high_out[rows, :] = high
+        low_out[rows, :] = (w - high.astype(f32)).astype(bf16)
+
+
+def scale_rows(pos, wt, cot):
+    return pl.pallas_call(
+        scale_kernel,
+        out_shape=[
+            jax.ShapeDtypeStruct((ROWS, QD), bf16),
+            jax.ShapeDtypeStruct((ROWS, TOK), bf16),
+            jax.ShapeDtypeStruct((ROWS, TOK), bf16),
+        ],
+        in_specs=[vspec()] * 3,
+        out_specs=[vspec()] * 3,
+        scratch_shapes=[VMEM((SLOTS, CAP, TOK), f32)],
         cost_estimate=cost(2 * ROWS * TOK * QD, 4 << 20),
-        name="select_rows",
-    )(index, placement[None, :], routes.T, weights.T, tokens)
-
-
-def scale_kernel(sel, selw, cot, out):
-    for r in range(0, SLOTS * CAP, 512):
-        w = jnp.sum(selw[r : r + 512, :], axis=1, keepdims=True)
-        picked = jnp.dot(sel[r : r + 512, :], cot[...], preferred_element_type=f32)
-        out[r : r + 512, :] = (w * picked).astype(bf16)
-
-
-def scale_rows(sel, selw, cot):
-    rows = SLOTS * CAP
-    return pl.pallas_call(
-        scale_kernel,
-        out_shape=jax.ShapeDtypeStruct((rows, QD), bf16),
-        in_specs=[vspec()] * 3,
-        out_specs=vspec(),
-        cost_estimate=cost(2 * rows * TOK * QD, 4 << 20),
         name="scale_rows",
-    )(sel, selw, cot)
+    )(pos, wt, cot)
 
 
 def row_block(block, width):
@@ -162,14 +208,14 @@
 
 
 def hidden_kernel(count, dp, *refs):
-    pieces, (wg, wu, g_out, u_out, h_out, gathered) = refs[:count], refs[count:]
+    pieces, (wg, wu, slope_out, h_out, gathered) = refs[:count], refs[count:]
     gather_pieces(HIDDEN_SOURCES, dp, pieces, gathered)
     x = gathered[...].reshape(HIDDEN_SOURCES * CAP, D)
     g = jnp.dot(x, wg[...], preferred_element_type=f32) * scale_in
     u = jnp.dot(x, wu[...], preferred_element_type=f32) * scale_in
-    g_out[...] = g
-    u_out[...] = u
-    h_out[...] = (g / (1.0 + jnp.exp(-g)) * u).astype(bf16)
+    s = 1.0 / (1.0 + jnp.exp(-g))
+    slope_out[...] = u * s * (1.0 + g * (1.0 - s))
+    h_out[...] = (g * s * u).astype(bf16)
 
 
 def hidden_of(dp, pieces, wg, wu):
@@ -181,11 +227,10 @@
         grid=(SLOTS // n,),
         out_shape=[
             jax.ShapeDtypeStruct((ROWS, QF), f32),
-            jax.ShapeDtypeStruct((ROWS, QF), f32),
             jax.ShapeDtypeStruct((ROWS, QF), bf16),
         ],
         in_specs=[sspec()] + piece_specs(n, pieces) + [whole((D, QF)), whole((D, QF))],
-        out_specs=[row_block(block, QF)] * 3,
+        out_specs=[row_block(block, QF)] * 2,
         scratch_shapes=[VMEM((n, CAP, D), bf16)],
         cost_estimate=cost(4 * ROWS * D * QF, ROWS * D * 2 + 8 * D * QF),
         name="hidden",
@@ -228,49 +273,41 @@
 WEIGHT_STEPS = HALF // WEIGHT_SOURCES
 
 
-def weight_kernel(part, count, dp, h0, h1, h2, h3, g_in, u_in, *refs):
+def weight_kernel(part, count, dp, h0, h1, h2, h3, slope, *refs):
     pieces, rest = refs[:count], refs[count:]
     i = pl.program_id(0)
-    out, gathered, acc = rest[-3:]
+    out, acc = rest[-2:]
+    grad = h0[...].astype(f32) + h1[...].astype(f32) + h2[...].astype(f32) + h3[...].astype(f32)
+    gg = (grad * scale_mid * slope[...]).astype(bf16).reshape(WEIGHT_SOURCES, CAP, QF)
     at = 0
+    groups = []
     for j in range(0, count, 4):
         rows = pieces[j].shape[1]
-        for shift, ref in zip((0, 3, 1, 2), pieces[j : j + 4]):
-            q = lax.rem(dp[0] + shift, N_DP)
-            gathered[:, at : at + rows, pl.ds(pl.multiple_of(q * QD, QD), QD)] = ref[...]
+        groups.append(gg[:, at : at + rows].reshape(WEIGHT_SOURCES * rows, QF).T)
         at += rows
-    x = gathered[...].reshape(WEIGHT_SOURCES * CAP, D)
-    grad = h0[...].astype(f32) + h1[...].astype(f32) + h2[...].astype(f32) + h3[...].astype(f32)
-    grad = grad * scale_mid
-    g = g_in[...]
-    s = 1.0 / (1.0 + jnp.exp(-g))
-    gg = (grad * u_in[...] * s * (1.0 + g * (1.0 - s))).astype(bf16)
-    product = lax.dot_general(gg, x, (((0,), (0,)), ((), ())), preferred_element_type=f32)
-    last = i == pl.num_programs(0) - 1
-    if part == 0:
+    for k, shift in enumerate((0, 3, 1, 2)):
+        q = lax.rem(dp[0] + shift, N_DP)
+        to = pl.ds(pl.multiple_of(q * QD, QD), QD)
+        product = None
+        for left, ref in zip(groups, pieces[k::4]):
+            x = ref[...].reshape(-1, QD)
+            one = jnp.dot(left, x, preferred_element_type=f32)
+            product = one if product is None else product + one
 
         @pl.when(i == 0)
         def _():
-            out[...] = product
+            acc[:, to] = product if part == 0 else rest[0][:, to] + product
 
         @pl.when(i > 0)
         def _():
-            out[...] += product
-
-    else:
-
-        @pl.when(i == 0)
-        def _():
-            acc[...] = rest[0][...] + product
-
-        @pl.when(last)
-        def _():
-            for r in range(0, D, 512):
-                total = (acc[:, r : r + 512] + product[:, r : r + 512]) * scale_in
-                out[r : r + 512, :] = total.T.astype(bf16)
-
-
-def weight_grads(dp, hg, g, u, pieces, part, carry=()):
+            if part == 0:
+                out[:, to] = acc[:, to] + product
+            else:
+                total = ((acc[:, to] + product) * scale_in).astype(bf16)
+                out[to, :] = total.T
+
+
+def weight_grads(dp, hg, slope, pieces, part, carry=()):
     n = WEIGHT_SOURCES
     block = n * CAP
     steps = WEIGHT_STEPS
@@ -289,13 +326,13 @@
         out_shape=shape,
         in_specs=[sspec()]
         + [row_block(block, QF)] * 4
-        + [values] * 2
+        + [values]
         + specs
         + [whole((QF, D))] * len(carry),
         out_specs=whole(shape.shape),
-        scratch_shapes=[VMEM((n, CAP, D), bf16), VMEM((QF, D) if part else (8, 128), f32)],
+        scratch_shapes=[VMEM((QF, D), f32)],
         cost_estimate=cost(ROWS * D * QF, ROWS * D + (8 << 20)),
-    )(dp, *hg, g, u, *inputs, *carry)
+    )(dp, *hg, slope, *inputs, *carry)
 
 
 OUTPUT_SOURCES = 8
@@ -324,33 +361,24 @@
     )(dp, *inputs, wd)
 
 
-def combine_kernel(selw, *refs):
-    out = refs[-1]
+def combine_kernel(high, low, rows, out):
     total = jnp.zeros(out.shape, f32)
-    base = 0
-    for ref in refs[:-1]:
-        n = ref.shape[0]
-        w = selw[base : base + n, :]
-        high = w.astype(bf16)
-        low = (w - high.astype(f32)).astype(bf16)
-        rows = ref[...]
-        for part in (high, low):
-            total = total + lax.dot_general(
-                part, rows, (((0,), (0,)), ((), ())), preferred_element_type=f32
-            )
-        base += n
+    for part in (high, low):
+        total = total + lax.dot_general(
+            part[...], rows[...], (((0,), (0,)), ((), ())), preferred_element_type=f32
+        )
     out[...] = total.astype(bf16)
 
 
-def combine(selw, rows):
+def combine(high, low, rows):
     return pl.pallas_call(
         combine_kernel,
         out_shape=jax.ShapeDtypeStruct((TOK, QD), bf16),
-        in_specs=[vspec()] * (1 + len(rows)),
+        in_specs=[vspec()] * 3,
         out_specs=vspec(),
-        cost_estimate=cost(4 * SLOTS * CAP * TOK * QD, 4 << 20),
+        cost_estimate=cost(4 * ROWS * TOK * QD, 4 << 20),
         name="combine",
-    )(selw, *rows)
+    )(high, low, rows)
 
 
 UPDATE_ROWS = 16
@@ -450,9 +478,10 @@
     index = lax.axis_index("expert").astype(jnp.int32)[None]
     dp = lax.axis_index("dp").astype(jnp.int32)[None]
     wg, wu, wd = gate_weight[0], up_weight[0], down_weight[0]
-    *rows, sel, selw = select_rows(index, placement, routes, route_weight, tokens)
+    first_rows, pos, wt = select_rows(index, placement, routes, route_weight, tokens)
+    rows = (first_rows, rest_rows(pos, tokens))
     got = [exchange(x) for x in rows]
-    sent_grads = scale_rows(sel, selw, cotangent)
+    sent_grads, high, low = scale_rows(pos, wt, cotangent)
     got_grads = exchange(sent_grads.reshape(SLOTS, CAP, QD)).reshape(ROWS, QD)
     packed = jnp.concatenate(
         [x[0].reshape(SLOTS, PART, QF) for x in (gate_weight, first_moment, second_moment)],
@@ -460,20 +489,20 @@
     )
     states = exchange(packed)
     pieces = [ring(x) for x in got]
-    g, u, h = hidden_of(dp, pieces, wg, wu)
+    slope, h = hidden_of(dp, pieces, wg, wu)
     carry = ()
     hg = []
     for part in range(2):
         partials = partial_grads(dp, got_grads, wd, part)
         hg.append([partials[0]] + [shift(partials[k], k) for k in range(1, N_DP)])
     for part in range(2):
-        carry = (weight_grads(dp, hg[part], g, u, pieces, part, carry),)
+        carry = (weight_grads(dp, hg[part], slope, pieces, part, carry),)
     wgrad = carry[0]
     got_wgrad = exchange(wgrad.reshape(SLOTS, PART, QF))
     moments = exchange(update(migration_plan, placement, got_wgrad, states))
     out = outputs_of(dp, [ring(h.reshape(SLOTS, CAP, QF))], wd)
     returned = exchange(out.reshape(SLOTS, CAP, QD)).reshape(ROWS, QD)
-    layer_output = combine(selw, [returned])
+    layer_output = combine(high, low, returned)
     results = finish(moments)
     return (layer_output,) + tuple(r.reshape(1, D, QF) for r in results)
 

time: 440 us -> 434 us (0.986)
  blocking collectives: 24.1 us -> 0 us
  waiting for transfers between devices: 252 us -> 264 us
    all_to_all x1 -> x0, blocking collectives: 24.1 us -> none  [exchange(): return lax.all_to_all(x, 'expert', split_axis=0, concat_axis=0, tiled=True)]
    all_to_all x6 -> x7, waiting for transfers between devices: 141 us -> 154 us  [exchange(): return lax.all_to_all(x, 'expert', split_axis=0, concat_axis=0, tiled=True)]
    all_to_all x6 -> x7, starting transfers between devices: 39.3 us -> 50 us  [exchange(): return lax.all_to_all(x, 'expert', split_axis=0, concat_axis=0, tiled=True)]
    ppermute x24, starting transfers between devices: 30.6 us -> 23.7 us  [shift(): return lax.ppermute(x, 'dp', [(i, (i + by) % N_DP) for i in range(N_DP)])]
  transfers between devices with their start and end apart: 30 -> 31, of which waited for: 17 -> 18; matrix products, arithmetic and copies ran while one was open for 2% -> 2% of each run, Pallas kernels for 15% -> 16%
where the time goes in v3:
time: 434 us; the launch traced here: 427 us
  waiting for transfers between devices  264 us (61%)
  Pallas kernels  75.1 us (17%)
  starting transfers between devices  73.7 us (17%)
  local copies, waits for them, and re-layouts  7.87 us (2%)
  other arithmetic  5.78 us (1%)
    all_to_all x7, waiting for transfers between devices, exchange(): return lax.all_to_all(x, 'expert', split_axis=0, concat_axis=0, tiled=True)  154 us
    ppermute x24, waiting for transfers between devices, shift(): return lax.ppermute(x, 'dp', [(i, (i + by) % N_DP) for i in range(N_DP)])  110 us
    all_to_all x7, starting transfers between devices, exchange(): return lax.all_to_all(x, 'expert', split_axis=0, concat_axis=0, tiled=True)  50 us
    ppermute x24, starting transfers between devices, shift(): return lax.ppermute(x, 'dp', [(i, (i + by) % N_DP) for i in range(N_DP)])  23.7 us
    pallas_call x2, Pallas kernels, weight_grads(): pl.pallas_call(functools.partial(weight_kernel, part, len(inputs)), grid=...  17.8 us
    pallas_call x1, Pallas kernels, hidden_of(): pl.pallas_call(functools.partial(hidden_kernel, len(inputs)), grid=(SLOTS...  12.5 us
    pallas_call x1, Pallas kernels, update(): pl.pallas_call(update_kernel, grid_spec=pltpu.PrefetchScalarGridSpec(num_...  10 us
    pallas_call x2, Pallas kernels, partial_grads(): pl.pallas_call(partial_kernel, grid=(steps,), out_shape=[jax.ShapeDtypeSt...  9.09 us
  transfers between devices with their start and end apart: 31, of which 18 were waited for; matrix products, arithmetic and copies ran while one was open for 2% of the time, Pallas kernels for 16%

profile of v3, /device:TPU:1, one launch (start us, length us, event | category | flops | bytes accessed | tf_op | source)
XLA Modules:
  0.0 427.1 jit_solution(5358625925297537037)
XLA Ops:
  0.6 2.6 select_rows.1
  3.2 8.6 %all-to-all-start = ((bf16[32,16,896]{2,1,0:T(8,128)(2,1)}), bf16[32,16,896]{2,1,0:T(8,128)(2,1)S(1)}, u32[]{:S(2)}, u32[]{:S(2)}) async-start(bf16[32,16,896]{2,1,0:T(8,128)(2,1)} %get-tuple-element.27), calls=%async_computation | async-start | bytes 1835008 | tf_op jit(solution)/shard_map/all_to_all | solution.py:447
  11.8 2.8 rest_rows.1
  14.6 12.7 %all-to-all-done.refs_0_ = bf16[32,16,896]{2,1,0:T(8,128)(2,1)S(1)} async-done(((bf16[32,16,896]{2,1,0:T(8,128)(2,1)}), bf16[32,16,896]{2,1,0:T(8,128)(2,1)S(1)}, u32[]{:S(2)}, u32[]{:S(2)}) %all-to-all-start) | async-done | bytes 917536 | tf_op jit(solution)/shard_map/all_to_all | solution.py:447
  27.4 3.9 all-to-all-start.1
  31.3 3.4 scale_rows.1
  34.6 22.2 %all-to-all-done.1.refs_7_.refs_4_ = bf16[32,32,896]{2,1,0:T(8,128)(2,1)S(1)} async-done(((bf16[32,32,896]{2,1,0:T(8,128)(2,1)}), bf16[32,32,896]{2,1,0:T(8,128)(2,1)S(1)}, u32[]{:S(2)}, u32[]{:S(2)}) %all-to-all-start.1) | async-done | bytes 1835040 | tf_op jit(solution)/shard_map/all_to_all | solution.py:447
  56.8 5.1 %all-to-all-start.3 = ((bf16[32,48,896]{2,1,0:T(8,128)(2,1)}), bf16[32,48,896]{2,1,0:T(8,128)(2,1)}, u32[]{:S(2)}, u32[]{:S(2)}) async-start(bf16[32,48,896]{2,1,0:T(8,128)(2,1)} %bitcast.25), calls=%async_computation.3 | async-start | bytes 5505024 | tf_op jit(solution)/shard_map/all_to_all | solution.py:447
  61.9 5.8 %pad_maximum_fusion = bf16[32,336,256]{2,1,0:T(8,128)(2,1)} fusion(bf16[32,112,256]{2,1,0:T(8,128)(2,1)} %bitcast.26, bf16[32,112,256]{2,1,0:T(8,128)(2,1)} %bitcast.27, bf16[32,112,256]{2,1,0:T(8,128)(2,1)} %bitcast.28), kind=kLoop, calls=%fused_computation | loop fusion | flops 16515072 | bytes 11010048 | tf_op jit(solution)/shard_map/concatenate | solution.py:486
  67.7 29.7 %all-to-all-done.3 = bf16[32,48,896]{2,1,0:T(8,128)(2,1)} async-done(((bf16[32,48,896]{2,1,0:T(8,128)(2,1)}), bf16[32,48,896]{2,1,0:T(8,128)(2,1)}, u32[]{:S(2)}, u32[]{:S(2)}) %all-to-all-start.3) | async-done | bytes 2752544 | tf_op jit(solution)/shard_map/all_to_all | solution.py:447
  97.4 5.4 %all-to-all-start.5 = ((bf16[32,336,256]{2,1,0:T(8,128)(2,1)}), bf16[32,336,256]{2,1,0:T(8,128)(2,1)}, u32[]{:S(2)}, u32[]{:S(2)}) async-start(bf16[32,336,256]{2,1,0:T(8,128)(2,1)} %pad_maximum_fusion), calls=%async_computation.5 | async-start | bytes 11010048 | tf_op jit(solution)/shard_map/all_to_all | solution.py:447
  102.9 3.8 collective-permute-start.3
  106.7 1.1 fusion
  107.8 0.1 collective-permute-start.9
  107.9 1.3 collective-permute-start.6
  109.3 2.7 collective-permute-start.2
  111.9 4.2 collective-permute-done.3.refs_4_.refs_2_
  116.2 0.5 collective-permute-start
  116.7 23.3 %collective-permute-done.1.refs_2_.refs_1_ = bf16[16,16,896]{2,1,0:T(8,128)(2,1)S(1)} collective-permute-done((bf16[16,16,896]{2,1,0:T(8,128)(2,1)S(1)}, bf16[16,16,896]{2,1,0:T(8,128)(2,1)S(1)}, u32[]{:S(2)}, u32[]{:S(2)}) %collective-permute-start.1) | collective-permute-done | bytes 458784 | tf_op jit(solution)/shard_map/ppermute | solution.py:451
  140.0 5.7 %collective-permute-done.2.refs_3_.refs_2_ = bf16[16,16,896]{2,1,0:T(8,128)(2,1)S(1)} collective-permute-done((bf16[16,16,896]{2,1,0:T(8,128)(2,1)S(1)}, bf16[16,16,896]{2,1,0:T(8,128)(2,1)S(1)}, u32[]{:S(2)}, u32[]{:S(2)}) %collective-permute-start.2) | collective-permute-done | bytes 458784 | tf_op jit(solution)/shard_map/ppermute | solution.py:451
  145.7 0.5 collective-permute-start.7
  146.2 3.6 collective-permute-done.refs_1_
  149.8 1.0 collective-permute-start.11
  150.9 0.5 collective-permute-start.10
  151.4 4.1 collective-permute-done.5.refs_6_.refs_3_
  155.5 0.8 copy-done.9
  156.3 0.5 collective-permute-start.4
  156.8 4.5 %shard_map.139 = (bf16[768,256]{1,0:T(8,128)(2,1)}, bf16[768,256]{1,0:T(8,128)(2,1)}, bf16[768,256]{1,0:T(8,128)(2,1)}, bf16[768,256]{1,0:T(8,128)(2,1)}) custom-call(s32[1]{0:T(128)} %bitcast.4.dp, bf16[1536,896]{1,0:T(8,128)(2,1)} %bitcast.14.x, bf16[1024,896]{1,0:T(8,128)(2,1)} %bitcast.37), custom_call_target="tpu_custom_call" | custom-call | flops 1409286144 | bytes 4194304 | tf_op jit(solution)/shard_map/pallas_call | solution.py:258
  161.3 37.4 %collective-permute-done.4.refs_5_.refs_3_ = bf16[16,16,896]{2,1,0:T(8,128)(2,1)} collective-permute-done((bf16[16,16,896]{2,1,0:T(8,128)(2,1)}, bf16[16,16,896]{2,1,0:T(8,128)(2,1)}, u32[]{:S(2)}, u32[]{:S(2)}) %collective-permute-start.4) | collective-permute-done | bytes 458784 | tf_op jit(solution)/shard_map/ppermute | solution.py:451
  198.7 0.4 collective-permute-start.21
  199.1 4.6 %shard_map.138 = (bf16[768,256]{1,0:T(8,128)(2,1)}, bf16[768,256]{1,0:T(8,128)(2,1)}, bf16[768,256]{1,0:T(8,128)(2,1)}, bf16[768,256]{1,0:T(8,128)(2,1)}) custom-call(s32[1]{0:T(128)} %bitcast.4.dp, bf16[1536,896]{1,0:T(8,128)(2,1)} %bitcast.14.x, bf16[1024,896]{1,0:T(8,128)(2,1)} %bitcast.38), custom_call_target="tpu_custom_call" | custom-call | flops 1409286144 | bytes 4194304 | tf_op jit(solution)/shard_map/pallas_call | solution.py:258
  203.7 1.0 collective-permute-start.22
  204.7 1.5 collective-permute-start.23
  206.2 3.2 collective-permute-done.21.h1
  209.4 2.7 collective-permute-start.20
  212.1 12.5 %hidden.1 = (f32[1536,256]{1,0:T(8,128)}, bf16[1536,256]{1,0:T(8,128)(2,1)}) custom-call(s32[1]{0:T(128)} %bitcast.4.dp, bf16[32,16,896]{2,1,0:T(8,128)(2,1)} %copy-done.1, bf16[16,16,896]{2,1,0:T(8,128)(2,1)} %collective-permute-done.refs_1_, bf16[16,16,896]{2,1,0:T(8,128)(2,1)} %copy-done.8, bf16[16,16,896]{2,1,0:T(8,128)(2,1)} %copy-done.10, ...), custom_call_target="tpu_custom_call" | custom-call | flops 5637144576 | bytes 18350080 | tf_op jit(solution)/shard_map/hidden/pallas_call | solution.py:225
  224.7 0.8 collective-permute-done.23.h3
  225.5 0.8 copy-done.15
  226.2 8.2 %shard_map.140.refs_8_ = f32[256,3584]{1,0:T(8,128)} custom-call(s32[1]{0:T(128)} %bitcast.4.dp, bf16[768,256]{1,0:T(8,128)(2,1)} %get-tuple-element.35.h0, bf16[768,256]{1,0:T(8,128)(2,1)} %collective-permute-done.21.h1, bf16[768,256]{1,0:T(8,128)(2,1)} %copy-done.13, bf16[768,256]{1,0:T(8,128)(2,1)} %copy-done.15, f32[1536,256]{1,0:T(8,128)} %get-tuple-element.34.slope, ...), custom_call_target="tpu_custom_call" | custom-call | flops 1409286144 | bytes 13893632 | tf_op jit(solution)/shard_map/pallas_call | solution.py:323
  234.5 6.0 %collective-permute-done.20.h3 = bf16[768,256]{1,0:T(8,128)(2,1)S(1)} collective-permute-done((bf16[768,256]{1,0:T(8,128)(2,1)}, bf16[768,256]{1,0:T(8,128)(2,1)S(1)}, u32[]{:S(2)}, u32[]{:S(2)}) %collective-permute-start.20) | collective-permute-done | bytes 393248 | tf_op jit(solution)/shard_map/ppermute | solution.py:451
  240.5 0.8 copy-done.14
  241.3 9.5 %shard_map.141 = bf16[3584,256]{1,0:T(8,128)(2,1)} custom-call(s32[1]{0:T(128)} %bitcast.4.dp, bf16[768,256]{1,0:T(8,128)(2,1)} %get-tuple-element.30.h0, bf16[768,256]{1,0:T(8,128)(2,1)} %copy-done.11, bf16[768,256]{1,0:T(8,128)(2,1)} %copy-done.12, bf16[768,256]{1,0:T(8,128)(2,1)} %copy-done.14, f32[1536,256]{1,0:T(8,128)} %get-tuple-element.34.slope, ...), custom_call_target="tpu_custom_call" | custom-call | flops 1409286144 | bytes 13893632 | tf_op jit(solution)/shard_map/pallas_call | solution.py:323
  250.8 13.5 %all-to-all-start.4 = ((bf16[32,112,256]{2,1,0:T(8,128)(2,1)}), bf16[32,112,256]{2,1,0:T(8,128)(2,1)S(1)}, u32[]{:S(2)}, u32[]{:S(2)}) async-start(bf16[32,112,256]{2,1,0:T(8,128)(2,1)} %bitcast.23), calls=%async_computation.4 | async-start | bytes 3670016 | tf_op jit(solution)/shard_map/all_to_all | solution.py:447
  264.4 0.6 collective-permute-start.12
  265.0 2.2 collective-permute-start.15
  267.2 0.3 collective-permute-start.14
  267.4 1.2 collective-permute-start.13
  268.6 7.5 %collective-permute-done.12.refs_1_ = bf16[16,48,256]{2,1,0:T(8,128)(2,1)S(1)} collective-permute-done((bf16[16,48,256]{2,1,0:T(8,128)(2,1)S(1)}, bf16[16,48,256]{2,1,0:T(8,128)(2,1)S(1)}, u32[]{:S(2)}, u32[]{:S(2)}) %collective-permute-start.12) | collective-permute-done | bytes 393248 | tf_op jit(solution)/shard_map/ppermute | solution.py:451
  276.2 2.7 collective-permute-start.17
  278.8 5.3 %collective-permute-done.14.refs_3_ = bf16[16,48,256]{2,1,0:T(8,128)(2,1)S(1)} collective-permute-done((bf16[16,48,256]{2,1,0:T(8,128)(2,1)S(1)}, bf16[16,48,256]{2,1,0:T(8,128)(2,1)S(1)}, u32[]{:S(2)}, u32[]{:S(2)}) %collective-permute-start.14) | collective-permute-done | bytes 393248 | tf_op jit(solution)/shard_map/ppermute | solution.py:451
  284.1 0.4 collective-permute-done.13.refs_2_
  284.6 8.4 %collective-permute-done.16.refs_5_ = bf16[16,48,256]{2,1,0:T(8,128)(2,1)S(1)} collective-permute-done((bf16[16,48,256]{2,1,0:T(8,128)(2,1)S(1)}, bf16[16,48,256]{2,1,0:T(8,128)(2,1)S(1)}, u32[]{:S(2)}, u32[]{:S(2)}) %collective-permute-start.16) | collective-permute-done | bytes 393248 | tf_op jit(solution)/shard_map/ppermute | solution.py:451
  293.0 0.8 copy-done.20
  293.8 0.7 copy-done.21
  294.5 7.7 %outputs.1 = bf16[1536,896]{1,0:T(8,128)(2,1)} custom-call(s32[1]{0:T(128)} %bitcast.4.dp, bf16[32,48,256]{2,1,0:T(8,128)(2,1)} %bitcast.30, bf16[16,48,256]{2,1,0:T(8,128)(2,1)} %copy-done.16, bf16[16,48,256]{2,1,0:T(8,128)(2,1)} %copy-done.19, bf16[16,48,256]{2,1,0:T(8,128)(2,1)} %copy-done.18, bf16[16,48,256]{2,1,0:T(8,128)(2,1)} %copy-done.17, ...), custom_call_target="tpu_custom_call" | custom-call | flops 2818572288 | bytes 5898240 | tf_op jit(solution)/shard_map/outputs/pallas_call | solution.py:352
  302.2 1.2 copy-done.3
  303.4 8.1 %all-to-all-start.2 = ((bf16[32,48,896]{2,1,0:T(8,128)(2,1)}), bf16[32,48,896]{2,1,0:T(8,128)(2,1)S(1)}, u32[]{:S(2)}, u32[]{:S(2)}) async-start(bf16[32,48,896]{2,1,0:T(8,128)(2,1)} %bitcast.24), calls=%async_computation.2 | async-start | bytes 5505024 | tf_op jit(solution)/shard_map/all_to_all | solution.py:447
  311.5 10.0 %update.1 = bf16[32,3,112,256]{3,2,1,0:T(8,128)(2,1)} custom-call(s32[32]{0:T(128)} %plan.1, s32[32]{0:T(128)} %placement.1, bf16[32,112,256]{2,1,0:T(8,128)(2,1)} %copy-done.3, bf16[32,336,256]{2,1,0:T(8,128)(2,1)} %all-to-all-done.5.gate.first.second, bf16[32,336,256]{2,1,0:T(8,128)(2,1)} %all-to-all-done.5.gate.first.second, ...), custom_call_target="tpu_custom_call" | custom-call | flops 18350080 | bytes 10485760 | tf_op jit(solution)/shard_map/update/pallas_call | solution.py:412
  321.5 25.2 %all-to-all-done.2 = bf16[32,48,896]{2,1,0:T(8,128)(2,1)S(1)} async-done(((bf16[32,48,896]{2,1,0:T(8,128)(2,1)}), bf16[32,48,896]{2,1,0:T(8,128)(2,1)S(1)}, u32[]{:S(2)}, u32[]{:S(2)}) %all-to-all-start.2) | async-done | bytes 2752544 | tf_op jit(solution)/shard_map/all_to_all | solution.py:447
  346.8 1.6 copy-done.2
  348.3 5.4 %all-to-all-start.6 = ((bf16[32,3,112,256]{3,2,1,0:T(8,128)(2,1)}), bf16[32,3,112,256]{3,2,1,0:T(8,128)(2,1)}, u32[]{:S(2)}, u32[]{:S(2)}) async-start(bf16[32,3,112,256]{3,2,1,0:T(8,128)(2,1)} %update.1), calls=%async_computation.6 | async-start | bytes 11010048 | tf_op jit(solution)/shard_map/all_to_all | solution.py:447
  353.7 3.7 combine.1
  357.5 64.1 %all-to-all-done.6.moments = bf16[32,3,112,256]{3,2,1,0:T(8,128)(2,1)} async-done(((bf16[32,3,112,256]{3,2,1,0:T(8,128)(2,1)}), bf16[32,3,112,256]{3,2,1,0:T(8,128)(2,1)}, u32[]{:S(2)}, u32[]{:S(2)}) %all-to-all-start.6) | async-done | bytes 5505056 | tf_op jit(solution)/shard_map/all_to_all | solution.py:447
  421.6 5.5 %finish.1 = (bf16[32,112,256]{2,1,0:T(8,128)(2,1)}, bf16[32,112,256]{2,1,0:T(8,128)(2,1)}, bf16[32,112,256]{2,1,0:T(8,128)(2,1)}) custom-call(bf16[32,3,112,256]{3,2,1,0:T(8,128)(2,1)} %all-to-all-done.6.moments), custom_call_target="tpu_custom_call" | custom-call | bytes 12582912 | tf_op jit(solution)/shard_map/finish/pallas_call | solution.py:435
  (58 shorter events, 0.3 us)
Async XLA Ops:
  3.2 24.1 %all-to-all-start = ((bf16[32,16,896]{2,1,0:T(8,128)(2,1)}), bf16[32,16,896]{2,1,0:T(8,128)(2,1)S(1)}, u32[]{:S(2)}, u32[]{:S(2)}) async-start(bf16[32,16,896]{2,1,0:T(8,128)(2,1)} %get-tuple-element.27), calls=%async_computation | async-start | bytes 1835008 | tf_op jit(solution)/shard_map/all_to_all | solution.py:447
  27.4 75.4 %copy-start.1 = (bf16[32,16,896]{2,1,0:T(8,128)(2,1)}, bf16[32,16,896]{2,1,0:T(8,128)(2,1)S(1)}, u32[]{:S(2)}) copy-start(bf16[32,16,896]{2,1,0:T(8,128)(2,1)S(1)} %all-to-all-done.refs_0_) | copy-start | bytes 2752516
  27.4 29.4 %all-to-all-start.1 = ((bf16[32,32,896]{2,1,0:T(8,128)(2,1)}), bf16[32,32,896]{2,1,0:T(8,128)(2,1)S(1)}, u32[]{:S(2)}, u32[]{:S(2)}) async-start(bf16[32,32,896]{2,1,0:T(8,128)(2,1)} %rest_rows.1), calls=%async_computation.1 | async-start | bytes 3670016 | tf_op jit(solution)/shard_map/all_to_all | solution.py:447
  56.8 49.9 %copy-start = (bf16[32,32,896]{2,1,0:T(8,128)(2,1)}, bf16[32,32,896]{2,1,0:T(8,128)(2,1)S(1)}, u32[]{:S(2)}) copy-start(bf16[32,32,896]{2,1,0:T(8,128)(2,1)S(1)} %all-to-all-done.1.refs_7_.refs_4_) | copy-start | bytes 5505028
  56.8 40.6 %all-to-all-start.3 = ((bf16[32,48,896]{2,1,0:T(8,128)(2,1)}), bf16[32,48,896]{2,1,0:T(8,128)(2,1)}, u32[]{:S(2)}, u32[]{:S(2)}) async-start(bf16[32,48,896]{2,1,0:T(8,128)(2,1)} %bitcast.25), calls=%async_computation.3 | async-start | bytes 5505024 | tf_op jit(solution)/shard_map/all_to_all | solution.py:447
  97.4 153.4 %all-to-all-start.5 = ((bf16[32,336,256]{2,1,0:T(8,128)(2,1)}), bf16[32,336,256]{2,1,0:T(8,128)(2,1)}, u32[]{:S(2)}, u32[]{:S(2)}) async-start(bf16[32,336,256]{2,1,0:T(8,128)(2,1)} %pad_maximum_fusion), calls=%async_computation.5 | async-start | bytes 11010048 | tf_op jit(solution)/shard_map/all_to_all | solution.py:447
  102.9 13.3 %collective-permute-start.3 = (bf16[16,16,896]{2,1,0:T(8,128)(2,1)S(1)}, bf16[16,16,896]{2,1,0:T(8,128)(2,1)S(1)}, u32[]{:S(2)}, u32[]{:S(2)}) collective-permute-start(bf16[16,16,896]{2,1,0:T(8,128)(2,1)S(1)} %get-tuple-element.44), channel_id=1, source_target_pairs={{0,96},{32,0},{64,32},{96,64},{1,97},{33,1},{65,33},{97,65},{2,98}... | collective-permute-start | bytes 1376264 | tf_op jit(solution)/shard_map/ppermute | solution.py:451
  107.8 42.0 %collective-permute-start.9 = (bf16[16,32,896]{2,1,0:T(8,128)(2,1)}, bf16[16,32,896]{2,1,0:T(8,128)(2,1)S(1)}, u32[]{:S(2)}, u32[]{:S(2)}) collective-permute-start(bf16[16,32,896]{2,1,0:T(8,128)(2,1)} %get-tuple-element.42), channel_id=1, source_target_pairs={{0,96},{32,0},{64,32},{96,64},{1,97},{33,1},{65,33},{97,65},{2,98}... | collective-permute-start | bytes 2752520 | tf_op jit(solution)/shard_map/ppermute | solution.py:451
  107.9 42.9 %collective-permute-start.6 = (bf16[16,32,896]{2,1,0:T(8,128)(2,1)S(1)}, bf16[16,32,896]{2,1,0:T(8,128)(2,1)S(1)}, u32[]{:S(2)}, u32[]{:S(2)}) collective-permute-start(bf16[16,32,896]{2,1,0:T(8,128)(2,1)S(1)} %get-tuple-element.43), channel_id=1, source_target_pairs={{0,32},{32,64},{64,96},{96,0},{1,33},{33,65},{65,97},{97,1},{2,34}... | collective-permute-start | bytes 2752520 | tf_op jit(solution)/shard_map/ppermute | solution.py:451
  109.3 30.7 %collective-permute-start.1 = (bf16[16,16,896]{2,1,0:T(8,128)(2,1)S(1)}, bf16[16,16,896]{2,1,0:T(8,128)(2,1)S(1)}, u32[]{:S(2)}, u32[]{:S(2)}) collective-permute-start(bf16[16,16,896]{2,1,0:T(8,128)(2,1)S(1)} %get-tuple-element.44), channel_id=1, source_target_pairs={{0,32},{32,64},{64,96},{96,0},{1,33},{33,65},{65,97},{97,1},{2,34}... | collective-permute-start | bytes 1376264 | tf_op jit(solution)/shard_map/ppermute | solution.py:451
  109.3 36.4 %collective-permute-start.2 = (bf16[16,16,896]{2,1,0:T(8,128)(2,1)S(1)}, bf16[16,16,896]{2,1,0:T(8,128)(2,1)S(1)}, u32[]{:S(2)}, u32[]{:S(2)}) collective-permute-start(bf16[16,16,896]{2,1,0:T(8,128)(2,1)S(1)} %get-tuple-element.45), channel_id=1, source_target_pairs={{0,96},{32,0},{64,32},{96,64},{1,97},{33,1},{65,33},{97,65},{2,98}... | collective-permute-start | bytes 1376264 | tf_op jit(solution)/shard_map/ppermute | solution.py:451
  116.2 87.5 %copy-start.7 = (bf16[16,16,896]{2,1,0:T(8,128)(2,1)}, bf16[16,16,896]{2,1,0:T(8,128)(2,1)S(1)}, u32[]{:S(2)}) copy-start(bf16[16,16,896]{2,1,0:T(8,128)(2,1)S(1)} %collective-permute-done.3.refs_4_.refs_2_) | copy-start | bytes 1376260
  116.2 33.7 %collective-permute-start = (bf16[16,16,896]{2,1,0:T(8,128)(2,1)S(1)}, bf16[16,16,896]{2,1,0:T(8,128)(2,1)}, u32[]{:S(2)}, u32[]{:S(2)}) collective-permute-start(bf16[16,16,896]{2,1,0:T(8,128)(2,1)S(1)} %get-tuple-element.45), channel_id=1, source_target_pairs={{0,32},{32,64},{64,96},{96,0},{1,33},{33,65},{65,97},{97,1},{2,34}... | collective-permute-start | bytes 1376264 | tf_op jit(solution)/shard_map/ppermute | solution.py:451
  140.0 15.5 %copy-start.8 = (bf16[16,16,896]{2,1,0:T(8,128)(2,1)}, bf16[16,16,896]{2,1,0:T(8,128)(2,1)S(1)}, u32[]{:S(2)}) copy-start(bf16[16,16,896]{2,1,0:T(8,128)(2,1)S(1)} %collective-permute-done.1.refs_2_.refs_1_) | copy-start | bytes 1376260
  140.0 15.5 %collective-permute-start.5 = (bf16[16,16,896]{2,1,0:T(8,128)(2,1)S(1)}, bf16[16,16,896]{2,1,0:T(8,128)(2,1)S(1)}, u32[]{:S(2)}, u32[]{:S(2)}) collective-permute-start(bf16[16,16,896]{2,1,0:T(8,128)(2,1)S(1)} %collective-permute-done.3.refs_4_.refs_2_), channel_id=1, source_target_pairs={{0,96},{32,0},{64,32},{96,64},{1,97},{33,1},{65,33},{97,65},{2,98}... | collective-permute-start | bytes 1376264 | tf_op jit(solution)/shard_map/ppermute | solution.py:451
  145.7 9.8 %copy-start.10 = (bf16[16,16,896]{2,1,0:T(8,128)(2,1)}, bf16[16,16,896]{2,1,0:T(8,128)(2,1)S(1)}, u32[]{:S(2)}) copy-start(bf16[16,16,896]{2,1,0:T(8,128)(2,1)S(1)} %collective-permute-done.2.refs_3_.refs_2_) | copy-start | bytes 1376260
  145.7 58.0 %collective-permute-start.7 = (bf16[16,32,896]{2,1,0:T(8,128)(2,1)}, bf16[16,32,896]{2,1,0:T(8,128)(2,1)}, u32[]{:S(2)}, u32[]{:S(2)}) collective-permute-start(bf16[16,32,896]{2,1,0:T(8,128)(2,1)} %get-tuple-element.42), channel_id=1, source_target_pairs={{0,32},{32,64},{64,96},{96,0},{1,33},{33,65},{65,97},{97,1},{2,34}... | collective-permute-start | bytes 2752520 | tf_op jit(solution)/shard_map/ppermute | solution.py:451
  149.8 54.9 %collective-permute-start.8 = (bf16[16,32,896]{2,1,0:T(8,128)(2,1)S(1)}, bf16[16,32,896]{2,1,0:T(8,128)(2,1)}, u32[]{:S(2)}, u32[]{:S(2)}) collective-permute-start(bf16[16,32,896]{2,1,0:T(8,128)(2,1)S(1)} %get-tuple-element.43), channel_id=1, source_target_pairs={{0,96},{32,0},{64,32},{96,64},{1,97},{33,1},{65,33},{97,65},{2,98}... | collective-permute-start | bytes 2752520 | tf_op jit(solution)/shard_map/ppermute | solution.py:451
  149.8 53.8 %copy-start.4 = (bf16[16,32,896]{2,1,0:T(8,128)(2,1)}, bf16[16,32,896]{2,1,0:T(8,128)(2,1)S(1)}, u32[]{:S(2)}) copy-start(bf16[16,32,896]{2,1,0:T(8,128)(2,1)S(1)} %collective-permute-done.9.refs_11_.refs_6_) | copy-start | bytes 2752516
  149.8 59.5 %collective-permute-start.11 = (bf16[16,32,896]{2,1,0:T(8,128)(2,1)S(1)}, bf16[16,32,896]{2,1,0:T(8,128)(2,1)}, u32[]{:S(2)}, u32[]{:S(2)}) collective-permute-start(bf16[16,32,896]{2,1,0:T(8,128)(2,1)S(1)} %collective-permute-done.9.refs_11_.refs_6_), channel_id=1, source_target_pairs={{0,96},{32,0},{64,32},{96,64},{1,97},{33,1},{65,33},{97,65},{2,98}... | collective-permute-start | bytes 2752520 | tf_op jit(solution)/shard_map/ppermute | solution.py:451
  150.9 52.8 %copy-start.5 = (bf16[16,32,896]{2,1,0:T(8,128)(2,1)}, bf16[16,32,896]{2,1,0:T(8,128)(2,1)S(1)}, u32[]{:S(2)}) copy-start(bf16[16,32,896]{2,1,0:T(8,128)(2,1)S(1)} %collective-permute-done.6.refs_8_.refs_5_) | copy-start | bytes 2752516
  150.9 58.5 %collective-permute-start.10 = (bf16[16,32,896]{2,1,0:T(8,128)(2,1)S(1)}, bf16[16,32,896]{2,1,0:T(8,128)(2,1)}, u32[]{:S(2)}, u32[]{:S(2)}) collective-permute-start(bf16[16,32,896]{2,1,0:T(8,128)(2,1)S(1)} %collective-permute-done.6.refs_8_.refs_5_), channel_id=1, source_target_pairs={{0,32},{32,64},{64,96},{96,0},{1,33},{33,65},{65,97},{97,1},{2,34}... | collective-permute-start | bytes 2752520 | tf_op jit(solution)/shard_map/ppermute | solution.py:451
  155.5 0.8 copy-start.9
  156.3 42.5 %collective-permute-start.4 = (bf16[16,16,896]{2,1,0:T(8,128)(2,1)}, bf16[16,16,896]{2,1,0:T(8,128)(2,1)}, u32[]{:S(2)}, u32[]{:S(2)}) collective-permute-start(bf16[16,16,896]{2,1,0:T(8,128)(2,1)} %collective-permute-done.refs_1_), channel_id=1, source_target_pairs={{0,32},{32,64},{64,96},{96,0},{1,33},{33,65},{65,97},{97,1},{2,34}... | collective-permute-start | bytes 1376264 | tf_op jit(solution)/shard_map/ppermute | solution.py:451
  198.7 10.6 %collective-permute-start.21 = (bf16[768,256]{1,0:T(8,128)(2,1)}, bf16[768,256]{1,0:T(8,128)(2,1)}, u32[]{:S(2)}, u32[]{:S(2)}) collective-permute-start(bf16[768,256]{1,0:T(8,128)(2,1)} %get-tuple-element.36), channel_id=1, source_target_pairs={{0,32},{32,64},{64,96},{96,0},{1,33},{33,65},{65,97},{97,1},{2,34}... | collective-permute-start | bytes 1179656 | tf_op jit(solution)/shard_map/ppermute | solution.py:451
  203.7 21.0 %collective-permute-start.22 = (bf16[768,256]{1,0:T(8,128)(2,1)}, bf16[768,256]{1,0:T(8,128)(2,1)S(1)}, u32[]{:S(2)}, u32[]{:S(2)}) collective-permute-start(bf16[768,256]{1,0:T(8,128)(2,1)} %get-tuple-element.37), channel_id=1, source_target_pairs={{0,64},{32,96},{64,0},{96,32},{1,65},{33,97},{65,1},{97,33},{2,66}... | collective-permute-start | bytes 1179656 | tf_op jit(solution)/shard_map/ppermute | solution.py:451
  204.7 20.7 %collective-permute-start.23 = (bf16[768,256]{1,0:T(8,128)(2,1)}, bf16[768,256]{1,0:T(8,128)(2,1)S(1)}, u32[]{:S(2)}, u32[]{:S(2)}) collective-permute-start(bf16[768,256]{1,0:T(8,128)(2,1)} %get-tuple-element.38), channel_id=1, source_target_pairs={{0,96},{32,0},{64,32},{96,64},{1,97},{33,1},{65,33},{97,65},{2,98}... | collective-permute-start | bytes 1179656 | tf_op jit(solution)/shard_map/ppermute | solution.py:451
  209.4 25.1 %collective-permute-start.18 = (bf16[768,256]{1,0:T(8,128)(2,1)}, bf16[768,256]{1,0:T(8,128)(2,1)S(1)}, u32[]{:S(2)}, u32[]{:S(2)}) collective-permute-start(bf16[768,256]{1,0:T(8,128)(2,1)} %get-tuple-element.31), channel_id=1, source_target_pairs={{0,32},{32,64},{64,96},{96,0},{1,33},{33,65},{65,97},{97,1},{2,34}... | collective-permute-start | bytes 1179656 | tf_op jit(solution)/shard_map/ppermute | solution.py:451
  209.4 25.1 %collective-permute-start.19 = (bf16[768,256]{1,0:T(8,128)(2,1)}, bf16[768,256]{1,0:T(8,128)(2,1)S(1)}, u32[]{:S(2)}, u32[]{:S(2)}) collective-permute-start(bf16[768,256]{1,0:T(8,128)(2,1)} %get-tuple-element.32), channel_id=1, source_target_pairs={{0,64},{32,96},{64,0},{96,32},{1,65},{33,97},{65,1},{97,33},{2,66}... | collective-permute-start | bytes 1179656 | tf_op jit(solution)/shard_map/ppermute | solution.py:451
  209.4 31.1 %collective-permute-start.20 = (bf16[768,256]{1,0:T(8,128)(2,1)}, bf16[768,256]{1,0:T(8,128)(2,1)S(1)}, u32[]{:S(2)}, u32[]{:S(2)}) collective-permute-start(bf16[768,256]{1,0:T(8,128)(2,1)} %get-tuple-element.33), channel_id=1, source_target_pairs={{0,96},{32,0},{64,32},{96,64},{1,97},{33,1},{65,33},{97,65},{2,98}... | collective-permute-start | bytes 1179656 | tf_op jit(solution)/shard_map/ppermute | solution.py:451
  224.7 0.8 copy-start.13
  225.5 0.8 copy-start.15
  234.5 6.0 %copy-start.11 = (bf16[768,256]{1,0:T(8,128)(2,1)}, bf16[768,256]{1,0:T(8,128)(2,1)S(1)}, u32[]{:S(2)}) copy-start(bf16[768,256]{1,0:T(8,128)(2,1)S(1)} %collective-permute-done.18.h1) | copy-start | bytes 1179652
  234.5 6.0 %copy-start.12 = (bf16[768,256]{1,0:T(8,128)(2,1)}, bf16[768,256]{1,0:T(8,128)(2,1)S(1)}, u32[]{:S(2)}) copy-start(bf16[768,256]{1,0:T(8,128)(2,1)S(1)} %collective-permute-done.19.h2) | copy-start | bytes 1179652
  240.5 0.8 copy-start.14
  250.8 13.5 %copy-start.6 = (bf16[1536,256]{1,0:T(8,128)(2,1)S(1)}, bf16[1536,256]{1,0:T(8,128)(2,1)}, u32[]{:S(2)}) copy-start(bf16[1536,256]{1,0:T(8,128)(2,1)} %get-tuple-element.28) | copy-start | bytes 2359300
  250.8 51.3 %all-to-all-start.4 = ((bf16[32,112,256]{2,1,0:T(8,128)(2,1)}), bf16[32,112,256]{2,1,0:T(8,128)(2,1)S(1)}, u32[]{:S(2)}, u32[]{:S(2)}) async-start(bf16[32,112,256]{2,1,0:T(8,128)(2,1)} %bitcast.23), calls=%async_computation.4 | async-start | bytes 3670016 | tf_op jit(solution)/shard_map/all_to_all | solution.py:447
  264.4 11.7 %collective-permute-start.12 = (bf16[16,48,256]{2,1,0:T(8,128)(2,1)S(1)}, bf16[16,48,256]{2,1,0:T(8,128)(2,1)S(1)}, u32[]{:S(2)}, u32[]{:S(2)}) collective-permute-start(bf16[16,48,256]{2,1,0:T(8,128)(2,1)S(1)} %bitcast.33), channel_id=1, source_target_pairs={{0,32},{32,64},{64,96},{96,0},{1,33},{33,65},{65,97},{97,1},{2,34}... | collective-permute-start | bytes 1179656 | tf_op jit(solution)/shard_map/ppermute | solution.py:451
  265.0 11.2 %collective-permute-start.15 = (bf16[16,48,256]{2,1,0:T(8,128)(2,1)S(1)}, bf16[16,48,256]{2,1,0:T(8,128)(2,1)S(1)}, u32[]{:S(2)}, u32[]{:S(2)}) collective-permute-start(bf16[16,48,256]{2,1,0:T(8,128)(2,1)S(1)} %bitcast.31), channel_id=1, source_target_pairs={{0,96},{32,0},{64,32},{96,64},{1,97},{33,1},{65,33},{97,65},{2,98}... | collective-permute-start | bytes 1179656 | tf_op jit(solution)/shard_map/ppermute | solution.py:451
  267.2 17.0 %collective-permute-start.14 = (bf16[16,48,256]{2,1,0:T(8,128)(2,1)S(1)}, bf16[16,48,256]{2,1,0:T(8,128)(2,1)S(1)}, u32[]{:S(2)}, u32[]{:S(2)}) collective-permute-start(bf16[16,48,256]{2,1,0:T(8,128)(2,1)S(1)} %bitcast.34), channel_id=1, source_target_pairs={{0,96},{32,0},{64,32},{96,64},{1,97},{33,1},{65,33},{97,65},{2,98}... | collective-permute-start | bytes 1179656 | tf_op jit(solution)/shard_map/ppermute | solution.py:451
  267.4 17.1 %collective-permute-start.13 = (bf16[16,48,256]{2,1,0:T(8,128)(2,1)S(1)}, bf16[16,48,256]{2,1,0:T(8,128)(2,1)S(1)}, u32[]{:S(2)}, u32[]{:S(2)}) collective-permute-start(bf16[16,48,256]{2,1,0:T(8,128)(2,1)S(1)} %bitcast.32), channel_id=1, source_target_pairs={{0,32},{32,64},{64,96},{96,0},{1,33},{33,65},{65,97},{97,1},{2,34}... | collective-permute-start | bytes 1179656 | tf_op jit(solution)/shard_map/ppermute | solution.py:451
  276.1 18.4 %copy-start.16 = (bf16[16,48,256]{2,1,0:T(8,128)(2,1)}, bf16[16,48,256]{2,1,0:T(8,128)(2,1)S(1)}, u32[]{:S(2)}) copy-start(bf16[16,48,256]{2,1,0:T(8,128)(2,1)S(1)} %collective-permute-done.12.refs_1_) | copy-start | bytes 1179652
  276.1 16.9 %collective-permute-start.16 = (bf16[16,48,256]{2,1,0:T(8,128)(2,1)S(1)}, bf16[16,48,256]{2,1,0:T(8,128)(2,1)S(1)}, u32[]{:S(2)}, u32[]{:S(2)}) collective-permute-start(bf16[16,48,256]{2,1,0:T(8,128)(2,1)S(1)} %collective-permute-done.12.refs_1_), channel_id=1, source_target_pairs={{0,32},{32,64},{64,96},{96,0},{1,33},{33,65},{65,97},{97,1},{2,34}... | collective-permute-start | bytes 1179656 | tf_op jit(solution)/shard_map/ppermute | solution.py:451
  276.1 18.4 %copy-start.17 = (bf16[16,48,256]{2,1,0:T(8,128)(2,1)}, bf16[16,48,256]{2,1,0:T(8,128)(2,1)S(1)}, u32[]{:S(2)}) copy-start(bf16[16,48,256]{2,1,0:T(8,128)(2,1)S(1)} %collective-permute-done.15.refs_4_) | copy-start | bytes 1179652
  276.2 16.8 %collective-permute-start.17 = (bf16[16,48,256]{2,1,0:T(8,128)(2,1)S(1)}, bf16[16,48,256]{2,1,0:T(8,128)(2,1)S(1)}, u32[]{:S(2)}, u32[]{:S(2)}) collective-permute-start(bf16[16,48,256]{2,1,0:T(8,128)(2,1)S(1)} %collective-permute-done.15.refs_4_), channel_id=1, source_target_pairs={{0,96},{32,0},{64,32},{96,64},{1,97},{33,1},{65,33},{97,65},{2,98}... | collective-permute-start | bytes 1179656 | tf_op jit(solution)/shard_map/ppermute | solution.py:451
  284.1 10.4 %copy-start.18 = (bf16[16,48,256]{2,1,0:T(8,128)(2,1)}, bf16[16,48,256]{2,1,0:T(8,128)(2,1)S(1)}, u32[]{:S(2)}) copy-start(bf16[16,48,256]{2,1,0:T(8,128)(2,1)S(1)} %collective-permute-done.14.refs_3_) | copy-start | bytes 1179652
  284.6 10.0 %copy-start.19 = (bf16[16,48,256]{2,1,0:T(8,128)(2,1)}, bf16[16,48,256]{2,1,0:T(8,128)(2,1)S(1)}, u32[]{:S(2)}) copy-start(bf16[16,48,256]{2,1,0:T(8,128)(2,1)S(1)} %collective-permute-done.13.refs_2_) | copy-start | bytes 1179652
  293.0 0.8 copy-start.20
  293.8 0.7 copy-start.21
  302.2 1.2 copy-start.3
  303.4 43.4 %all-to-all-start.2 = ((bf16[32,48,896]{2,1,0:T(8,128)(2,1)}), bf16[32,48,896]{2,1,0:T(8,128)(2,1)S(1)}, u32[]{:S(2)}, u32[]{:S(2)}) async-start(bf16[32,48,896]{2,1,0:T(8,128)(2,1)} %bitcast.24), calls=%async_computation.2 | async-start | bytes 5505024 | tf_op jit(solution)/shard_map/all_to_all | solution.py:447
  346.8 1.6 copy-start.2
  348.3 73.3 %all-to-all-start.6 = ((bf16[32,3,112,256]{3,2,1,0:T(8,128)(2,1)}), bf16[32,3,112,256]{3,2,1,0:T(8,128)(2,1)}, u32[]{:S(2)}, u32[]{:S(2)}) async-start(bf16[32,3,112,256]{3,2,1,0:T(8,128)(2,1)} %update.1), calls=%async_computation.6 | async-start | bytes 11010048 | tf_op jit(solution)/shard_map/all_to_all | solution.py:447

commit v4 on v3

--- a/solution.py
+++ b/solution.py
@@ -269,70 +269,85 @@
     )(dp, x, wd)
 
 
-WEIGHT_SOURCES = 8
-WEIGHT_STEPS = HALF // WEIGHT_SOURCES
-
-
-def weight_kernel(part, count, dp, h0, h1, h2, h3, slope, *refs):
-    pieces, rest = refs[:count], refs[count:]
-    i = pl.program_id(0)
-    out, acc = rest[-2:]
-    grad = h0[...].astype(f32) + h1[...].astype(f32) + h2[...].astype(f32) + h3[...].astype(f32)
-    gg = (grad * scale_mid * slope[...]).astype(bf16).reshape(WEIGHT_SOURCES, CAP, QF)
-    at = 0
-    groups = []
-    for j in range(0, count, 4):
-        rows = pieces[j].shape[1]
-        groups.append(gg[:, at : at + rows].reshape(WEIGHT_SOURCES * rows, QF).T)
-        at += rows
+HALF_ROWS = ROWS // 2
+
+
+def weight_kernel(dp, *refs):
+    sums, slope, pieces = refs[:6], refs[6], refs[7:21]
+    out, x0, x1, parts, slopes, sems = refs[21:]
+    count = len(sums)
+    first = [pltpu.make_async_copy(r, parts.at[n], sems.at[n]) for n, r in enumerate(sums)]
+    first.append(pltpu.make_async_copy(slope, slopes, sems.at[count]))
+    count += 1
+    by_piece = []
+    for k in range(N_DP):
+        copies = []
+        for x, group in ((x0, pieces[:7]), (x1, pieces[7:])):
+            if k == 0:
+                copies.append(pltpu.make_async_copy(group[0], x.at[0], sems.at[count]))
+                count += 1
+                continue
+            for h in range(2):
+                to = x.at[k, pl.ds(HALF * h, HALF)]
+                copies.append(pltpu.make_async_copy(group[2 * k - 1 + h], to, sems.at[count]))
+                count += 1
+        by_piece.append(copies)
+    for copies in [first] + by_piece:
+        for copy in copies:
+            copy.start()
+    for copy in first:
+        copy.wait()
+    gg = []
+    for h in range(2):
+        total = parts[h].astype(f32) + parts[2 + h].astype(f32) + parts[4 + h].astype(f32)
+        total = total * scale_mid * slopes[pl.ds(HALF_ROWS * h, HALF_ROWS), :]
+        gg.append(total.astype(bf16).reshape(HALF, CAP, QF))
+    gg = jnp.concatenate(gg, axis=0)
+    cut = CHUNKS[0][1]
+    left0 = gg[:, :cut].reshape(SLOTS * cut, QF).T
+    left1 = gg[:, cut:].reshape(SLOTS * (CAP - cut), QF).T
     for k, shift in enumerate((0, 3, 1, 2)):
+        for copy in by_piece[k]:
+            copy.wait()
         q = lax.rem(dp[0] + shift, N_DP)
+        product = jnp.dot(left0, x0[k].reshape(-1, QD), preferred_element_type=f32)
+        product = product + jnp.dot(left1, x1[k].reshape(-1, QD), preferred_element_type=f32)
         to = pl.ds(pl.multiple_of(q * QD, QD), QD)
-        product = None
-        for left, ref in zip(groups, pieces[k::4]):
-            x = ref[...].reshape(-1, QD)
-            one = jnp.dot(left, x, preferred_element_type=f32)
-            product = one if product is None else product + one
-
-        @pl.when(i == 0)
-        def _():
-            acc[:, to] = product if part == 0 else rest[0][:, to] + product
-
-        @pl.when(i > 0)
-        def _():
-            if part == 0:
-                out[:, to] = acc[:, to] + product
-            else:
-                total = ((acc[:, to] + product) * scale_in).astype(bf16)
-                out[to, :] = total.T
-
-
-def weight_grads(dp, hg, slope, pieces, part, carry=()):
-    n = WEIGHT_SOURCES
-    block = n * CAP
-    steps = WEIGHT_STEPS
-    assert steps == 2
-    inputs, specs = [], []
-    for own, la, lb, ra, rb, fa, fb in pieces:
-        shape = (n,) + own.shape[1:]
-        inputs += [own] + ([la, ra, fa] if part == 0 else [lb, rb, fb])
-        specs += [pl.BlockSpec(shape, lambda i: (part * steps + i, 0, 0))]
-        specs += [pl.BlockSpec(shape, lambda i: (i, 0, 0))] * 3
-    values = pl.BlockSpec((block, QF), lambda i: (part * steps + i, 0))
-    shape = jax.ShapeDtypeStruct((QF, D), f32) if part == 0 else jax.ShapeDtypeStruct((D, QF), bf16)
-    return pl.pallas_call(
-        functools.partial(weight_kernel, part, len(inputs)),
-        grid=(steps,),
-        out_shape=shape,
-        in_specs=[sspec()]
-        + [row_block(block, QF)] * 4
-        + [values]
-        + specs
-        + [whole((QF, D))] * len(carry),
-        out_specs=whole(shape.shape),
-        scratch_shapes=[VMEM((QF, D), f32)],
-        cost_estimate=cost(ROWS * D * QF, ROWS * D + (8 << 20)),
-    )(dp, *hg, slope, *inputs, *carry)
+        out[to, :] = (product * scale_in).astype(bf16).T
+
+
+def weight_grads(dp, sums, slope, pieces):
+    inputs = [*sums, slope, *flat(pieces)]
+    return pl.pallas_call(
+        weight_kernel,
+        out_shape=jax.ShapeDtypeStruct((D, QF), bf16),
+        in_specs=[sspec()] + [pl.BlockSpec(memory_space=pl.ANY)] * len(inputs),
+        out_specs=vspec(),
+        scratch_shapes=[
+            *[VMEM((N_DP, SLOTS, hi - lo, QD), bf16) for lo, hi in CHUNKS],
+            VMEM((len(sums), HALF_ROWS, QF), bf16),
+            VMEM((ROWS, QF), f32),
+            pltpu.SemaphoreType.DMA((len(inputs),)),
+        ],
+        cost_estimate=cost(2 * ROWS * D * QF, ROWS * D * 2 + (4 << 20)),
+        name="weight_grads",
+    )(dp, *inputs)
+
+
+def add_kernel(a, b, c, d, low, high):
+    low[...] = (a[...].astype(f32) + b[...].astype(f32)).astype(bf16)
+    high[...] = (c[...].astype(f32) + d[...].astype(f32)).astype(bf16)
+
+
+def add_pairs(*arrays):
+    return pl.pallas_call(
+        add_kernel,
+        out_shape=[jax.ShapeDtypeStruct((HALF_ROWS, QF), bf16)] * 2,
+        in_specs=[vspec()] * 4,
+        out_specs=[vspec()] * 2,
+        cost_estimate=cost(2 * HALF_ROWS * QF, 3 << 20),
+        name="add_pairs",
+    )(*arrays)
 
 
 OUTPUT_SOURCES = 8
@@ -481,7 +496,7 @@
     first_rows, pos, wt = select_rows(index, placement, routes, route_weight, tokens)
     rows = (first_rows, rest_rows(pos, tokens))
     got = [exchange(x) for x in rows]
-    sent_grads, high, low = scale_rows(pos, wt, cotangent)
+    sent_grads, weight_high, weight_low = scale_rows(pos, wt, cotangent)
     got_grads = exchange(sent_grads.reshape(SLOTS, CAP, QD)).reshape(ROWS, QD)
     packed = jnp.concatenate(
         [x[0].reshape(SLOTS, PART, QF) for x in (gate_weight, first_moment, second_moment)],
@@ -490,19 +505,22 @@
     states = exchange(packed)
     pieces = [ring(x) for x in got]
     slope, h = hidden_of(dp, pieces, wg, wu)
-    carry = ()
-    hg = []
-    for part in range(2):
-        partials = partial_grads(dp, got_grads, wd, part)
-        hg.append([partials[0]] + [shift(partials[k], k) for k in range(1, N_DP)])
-    for part in range(2):
-        carry = (weight_grads(dp, hg[part], slope, pieces, part, carry),)
-    wgrad = carry[0]
+    low = partial_grads(dp, got_grads, wd, 0)
+    high = partial_grads(dp, got_grads, wd, 1)
+    far_low = shift(low[2], 1)
+    far_high = shift(high[2], -1)
+    near_low = shift(low[3], -1)
+    near_high = shift(high[1], 1)
+    pair_low, pair_high = add_pairs(low[1], far_low, high[3], far_high)
+    pair_low = shift(pair_low, 1)
+    pair_high = shift(pair_high, -1)
+    sums = (low[0], high[0], near_low, near_high, pair_low, pair_high)
+    wgrad = weight_grads(dp, sums, slope, pieces)
     got_wgrad = exchange(wgrad.reshape(SLOTS, PART, QF))
     moments = exchange(update(migration_plan, placement, got_wgrad, states))
     out = outputs_of(dp, [ring(h.reshape(SLOTS, CAP, QF))], wd)
     returned = exchange(out.reshape(SLOTS, CAP, QD)).reshape(ROWS, QD)
-    layer_output = combine(high, low, returned)
+    layer_output = combine(weight_high, weight_low, returned)
     results = finish(moments)
     return (layer_output,) + tuple(r.reshape(1, D, QF) for r in results)
 

time: 434 us -> 418 us (0.963)
  waiting for transfers between devices: 264 us -> 249 us
  Pallas kernels: 75.1 us -> 68.3 us
  starting transfers between devices: 73.7 us -> 80.1 us
    ppermute x24, waiting for transfers between devices: 110 us -> 95.2 us  [shift(): return lax.ppermute(x, 'dp', [(i, (i + by) % N_DP) for i in range(N_DP)])]
    ppermute x24, starting transfers between devices: 23.7 us -> 31 us  [shift(): return lax.ppermute(x, 'dp', [(i, (i + by) % N_DP) for i in range(N_DP)])]
    pallas_call x2, Pallas kernels: 17.8 us -> 11 us  [the longest x1 8.63 us: weight_grads(): pl.pallas_call(weight_kernel, out_shape=jax.ShapeDtypeStruct((D, QF), bf1...]
  transfers between devices with their start and end apart: 31 -> 31, of which waited for: 18 -> 15; matrix products, arithmetic and copies ran while one was open for 2% -> 2% of each run, Pallas kernels for 16% -> 15%
where the time goes in v4:
time: 418 us; the launch traced here: 411 us
  waiting for transfers between devices  249 us (60%)
  starting transfers between devices  80.1 us (19%)
  Pallas kernels  68.3 us (16%)
  local copies, waits for them, and re-layouts  7.17 us (2%)
  other arithmetic  5.78 us (1%)
    all_to_all x7, waiting for transfers between devices, exchange(): return lax.all_to_all(x, 'expert', split_axis=0, concat_axis=0, tiled=True)  154 us
    ppermute x24, waiting for transfers between devices, shift(): return lax.ppermute(x, 'dp', [(i, (i + by) % N_DP) for i in range(N_DP)])  95.2 us
    all_to_all x7, starting transfers between devices, exchange(): return lax.all_to_all(x, 'expert', split_axis=0, concat_axis=0, tiled=True)  49.1 us
    ppermute x24, starting transfers between devices, shift(): return lax.ppermute(x, 'dp', [(i, (i + by) % N_DP) for i in range(N_DP)])  31 us
    pallas_call x1, Pallas kernels, hidden_of(): pl.pallas_call(functools.partial(hidden_kernel, len(inputs)), grid=(SLOTS...  12.5 us
    pallas_call x1, Pallas kernels, update(): pl.pallas_call(update_kernel, grid_spec=pltpu.PrefetchScalarGridSpec(num_...  9.99 us
    pallas_call x2, Pallas kernels, partial_grads(): pl.pallas_call(partial_kernel, grid=(steps,), out_shape=[jax.ShapeDtypeSt...  9.12 us
    pallas_call x1, Pallas kernels, weight_grads(): pl.pallas_call(weight_kernel, out_shape=jax.ShapeDtypeStruct((D, QF), bf1...  8.63 us
  transfers between devices with their start and end apart: 31, of which 15 were waited for; matrix products, arithmetic and copies ran while one was open for 2% of the time, Pallas kernels for 15%

profile of v4, /device:TPU:1, one launch (start us, length us, event | category | flops | bytes accessed | tf_op | source)
XLA Modules:
  0.0 411.3 jit_solution(10715218753417409514)
XLA Ops:
  0.6 2.6 select_rows.1
  3.2 8.6 %all-to-all-start = ((bf16[32,16,896]{2,1,0:T(8,128)(2,1)}), bf16[32,16,896]{2,1,0:T(8,128)(2,1)S(1)}, u32[]{:S(2)}, u32[]{:S(2)}) async-start(bf16[32,16,896]{2,1,0:T(8,128)(2,1)} %get-tuple-element.29), calls=%async_computation | async-start | bytes 1835008 | tf_op jit(solution)/shard_map/all_to_all | solution.py:462
  11.8 2.8 rest_rows.1
  14.6 12.7 %all-to-all-done.refs_0_.refs_7_ = bf16[32,16,896]{2,1,0:T(8,128)(2,1)S(1)} async-done(((bf16[32,16,896]{2,1,0:T(8,128)(2,1)}), bf16[32,16,896]{2,1,0:T(8,128)(2,1)S(1)}, u32[]{:S(2)}, u32[]{:S(2)}) %all-to-all-start) | async-done | bytes 917536 | tf_op jit(solution)/shard_map/all_to_all | solution.py:462
  27.4 3.9 all-to-all-start.1
  31.3 3.4 scale_rows.1
  34.6 22.2 %all-to-all-done.1.refs_7_.refs_14_ = bf16[32,32,896]{2,1,0:T(8,128)(2,1)S(1)} async-done(((bf16[32,32,896]{2,1,0:T(8,128)(2,1)}), bf16[32,32,896]{2,1,0:T(8,128)(2,1)S(1)}, u32[]{:S(2)}, u32[]{:S(2)}) %all-to-all-start.1) | async-done | bytes 1835040 | tf_op jit(solution)/shard_map/all_to_all | solution.py:462
  56.8 5.1 %all-to-all-start.3 = ((bf16[32,48,896]{2,1,0:T(8,128)(2,1)}), bf16[32,48,896]{2,1,0:T(8,128)(2,1)}, u32[]{:S(2)}, u32[]{:S(2)}) async-start(bf16[32,48,896]{2,1,0:T(8,128)(2,1)} %bitcast.25), calls=%async_computation.3 | async-start | bytes 5505024 | tf_op jit(solution)/shard_map/all_to_all | solution.py:462
  61.9 5.8 %pad_maximum_fusion = bf16[32,336,256]{2,1,0:T(8,128)(2,1)} fusion(bf16[32,112,256]{2,1,0:T(8,128)(2,1)} %bitcast.26, bf16[32,112,256]{2,1,0:T(8,128)(2,1)} %bitcast.27, bf16[32,112,256]{2,1,0:T(8,128)(2,1)} %bitcast.28), kind=kLoop, calls=%fused_computation | loop fusion | flops 16515072 | bytes 11010048 | tf_op jit(solution)/shard_map/concatenate | solution.py:501
  67.7 29.7 %all-to-all-done.3 = bf16[32,48,896]{2,1,0:T(8,128)(2,1)} async-done(((bf16[32,48,896]{2,1,0:T(8,128)(2,1)}), bf16[32,48,896]{2,1,0:T(8,128)(2,1)}, u32[]{:S(2)}, u32[]{:S(2)}) %all-to-all-start.3) | async-done | bytes 2752544 | tf_op jit(solution)/shard_map/all_to_all | solution.py:462
  97.4 5.4 %all-to-all-start.5 = ((bf16[32,336,256]{2,1,0:T(8,128)(2,1)}), bf16[32,336,256]{2,1,0:T(8,128)(2,1)}, u32[]{:S(2)}, u32[]{:S(2)}) async-start(bf16[32,336,256]{2,1,0:T(8,128)(2,1)} %pad_maximum_fusion), calls=%async_computation.5 | async-start | bytes 11010048 | tf_op jit(solution)/shard_map/all_to_all | solution.py:462
  102.8 0.1 fusion.1
  102.9 3.8 collective-permute-start.3
  106.7 1.1 fusion
  107.8 2.7 collective-permute-start.9
  110.5 2.7 collective-permute-start.2
  113.2 3.0 collective-permute-done.3.refs_4_.refs_11_
  116.2 0.5 collective-permute-start
  116.7 2.7 collective-permute-done.1.refs_2_.refs_9_
  119.4 0.8 copy-done.7
  120.2 0.3 collective-permute-start.5
  120.5 4.6 %shard_map.139 = (bf16[768,256]{1,0:T(8,128)(2,1)}, bf16[768,256]{1,0:T(8,128)(2,1)}, bf16[768,256]{1,0:T(8,128)(2,1)}, bf16[768,256]{1,0:T(8,128)(2,1)}) custom-call(s32[1]{0:T(128)} %bitcast.4.dp, bf16[1536,896]{1,0:T(8,128)(2,1)} %bitcast.14.x, bf16[1024,896]{1,0:T(8,128)(2,1)} %bitcast.37), custom_call_target="tpu_custom_call" | custom-call | flops 1409286144 | bytes 4194304 | tf_op jit(solution)/shard_map/pallas_call | solution.py:258
  125.1 20.6 %collective-permute-done.2.refs_3_.refs_10_ = bf16[16,16,896]{2,1,0:T(8,128)(2,1)} collective-permute-done((bf16[16,16,896]{2,1,0:T(8,128)(2,1)S(1)}, bf16[16,16,896]{2,1,0:T(8,128)(2,1)}, u32[]{:S(2)}, u32[]{:S(2)}) %collective-permute-start.2) | collective-permute-done | bytes 458784 | tf_op jit(solution)/shard_map/ppermute | solution.py:466
  145.7 3.5 collective-permute-start.21
  149.2 0.0 collective-permute-done.refs_1_.refs_8_
  149.2 6.4 %collective-permute-done.5.refs_6_.refs_13_ = bf16[16,16,896]{2,1,0:T(8,128)(2,1)} collective-permute-done((bf16[16,16,896]{2,1,0:T(8,128)(2,1)}, bf16[16,16,896]{2,1,0:T(8,128)(2,1)}, u32[]{:S(2)}, u32[]{:S(2)}) %collective-permute-start.5) | collective-permute-done | bytes 458784 | tf_op jit(solution)/shard_map/ppermute | solution.py:466
  155.6 3.4 collective-permute-start.8
  159.0 0.1 collective-permute-start.11
  159.1 1.4 collective-permute-start.10
  160.5 4.5 %shard_map.138 = (bf16[768,256]{1,0:T(8,128)(2,1)}, bf16[768,256]{1,0:T(8,128)(2,1)}, bf16[768,256]{1,0:T(8,128)(2,1)}, bf16[768,256]{1,0:T(8,128)(2,1)}) custom-call(s32[1]{0:T(128)} %bitcast.4.dp, bf16[1536,896]{1,0:T(8,128)(2,1)} %bitcast.14.x, bf16[1024,896]{1,0:T(8,128)(2,1)} %bitcast.38), custom_call_target="tpu_custom_call" | custom-call | flops 1409286144 | bytes 4194304 | tf_op jit(solution)/shard_map/pallas_call | solution.py:258
  165.0 0.4 collective-permute-start.20
  165.4 32.9 %collective-permute-done.20.b = bf16[768,256]{1,0:T(8,128)(2,1)} collective-permute-done((bf16[768,256]{1,0:T(8,128)(2,1)}, bf16[768,256]{1,0:T(8,128)(2,1)}, u32[]{:S(2)}, u32[]{:S(2)}) %collective-permute-start.20) | collective-permute-done | bytes 393248 | tf_op jit(solution)/shard_map/ppermute | solution.py:466
  198.3 2.3 add_pairs.1
  200.6 7.9 %collective-permute-done.4.refs_5_.refs_12_ = bf16[16,16,896]{2,1,0:T(8,128)(2,1)S(1)} collective-permute-done((bf16[16,16,896]{2,1,0:T(8,128)(2,1)}, bf16[16,16,896]{2,1,0:T(8,128)(2,1)S(1)}, u32[]{:S(2)}, u32[]{:S(2)}) %collective-permute-start.4) | collective-permute-done | bytes 458784 | tf_op jit(solution)/shard_map/ppermute | solution.py:466
  208.5 2.7 collective-permute-start.18
  211.2 2.7 collective-permute-start.23
  213.9 12.5 %hidden.1 = (f32[1536,256]{1,0:T(8,128)}, bf16[1536,256]{1,0:T(8,128)(2,1)}) custom-call(s32[1]{0:T(128)} %bitcast.4.dp, bf16[32,16,896]{2,1,0:T(8,128)(2,1)} %copy-done.2, bf16[16,16,896]{2,1,0:T(8,128)(2,1)} %collective-permute-done.refs_1_.refs_8_, bf16[16,16,896]{2,1,0:T(8,128)(2,1)} %copy-done.7, ...), custom_call_target="tpu_custom_call" | custom-call | flops 5637144576 | bytes 18350080 | tf_op jit(solution)/shard_map/hidden/pallas_call | solution.py:225
  226.5 0.7 copy-done.9
  227.2 0.1 copy-done.10
  227.3 8.6 %weight_grads.1 = bf16[3584,256]{1,0:T(8,128)(2,1)} custom-call(s32[1]{0:T(128)} %bitcast.4.dp, bf16[768,256]{1,0:T(8,128)(2,1)} %get-tuple-element.32.refs_0_, bf16[768,256]{1,0:T(8,128)(2,1)} %get-tuple-element.33.refs_1_, bf16[768,256]{1,0:T(8,128)(2,1)} %collective-permute-done.18.refs_2_, bf16[768,256]{1,0:T(8,128)(2,1)} %collective-permute-done.19.refs_3_, ...), custom_call_target="tpu_custom_call" | custom-call | flops 2818572288 | bytes 15204352 | tf_op jit(solution)/shard_map/weight_grads/pallas_call | solution.py:321
  236.0 12.6 %all-to-all-start.4 = ((bf16[32,112,256]{2,1,0:T(8,128)(2,1)}), bf16[32,112,256]{2,1,0:T(8,128)(2,1)S(1)}, u32[]{:S(2)}, u32[]{:S(2)}) async-start(bf16[32,112,256]{2,1,0:T(8,128)(2,1)} %bitcast.23), calls=%async_computation.4 | async-start | bytes 3670016 | tf_op jit(solution)/shard_map/all_to_all | solution.py:462
  248.6 0.1 fusion.2
  248.7 0.1 collective-permute-start.12
  248.8 2.7 collective-permute-start.15
  251.4 0.0 collective-permute-start.14
  251.4 1.4 collective-permute-start.13
  252.9 7.5 %collective-permute-done.12.refs_1_ = bf16[16,48,256]{2,1,0:T(8,128)(2,1)S(1)} collective-permute-done((bf16[16,48,256]{2,1,0:T(8,128)(2,1)S(1)}, bf16[16,48,256]{2,1,0:T(8,128)(2,1)S(1)}, u32[]{:S(2)}, u32[]{:S(2)}) %collective-permute-start.12) | collective-permute-done | bytes 393248 | tf_op jit(solution)/shard_map/ppermute | solution.py:466
  260.4 2.7 collective-permute-start.17
  263.1 4.7 %collective-permute-done.14.refs_3_ = bf16[16,48,256]{2,1,0:T(8,128)(2,1)S(1)} collective-permute-done((bf16[16,48,256]{2,1,0:T(8,128)(2,1)S(1)}, bf16[16,48,256]{2,1,0:T(8,128)(2,1)S(1)}, u32[]{:S(2)}, u32[]{:S(2)}) %collective-permute-start.14) | collective-permute-done | bytes 393248 | tf_op jit(solution)/shard_map/ppermute | solution.py:466
  267.8 1.0 collective-permute-done.13.refs_2_
  268.8 8.4 %collective-permute-done.16.refs_5_ = bf16[16,48,256]{2,1,0:T(8,128)(2,1)S(1)} collective-permute-done((bf16[16,48,256]{2,1,0:T(8,128)(2,1)S(1)}, bf16[16,48,256]{2,1,0:T(8,128)(2,1)S(1)}, u32[]{:S(2)}, u32[]{:S(2)}) %collective-permute-start.16) | collective-permute-done | bytes 393248 | tf_op jit(solution)/shard_map/ppermute | solution.py:466
  277.2 0.7 copy-done.15
  278.0 0.7 copy-done.16
  278.7 7.7 %outputs.1 = bf16[1536,896]{1,0:T(8,128)(2,1)} custom-call(s32[1]{0:T(128)} %bitcast.4.dp, bf16[32,48,256]{2,1,0:T(8,128)(2,1)} %bitcast.30, bf16[16,48,256]{2,1,0:T(8,128)(2,1)} %copy-done.11, bf16[16,48,256]{2,1,0:T(8,128)(2,1)} %copy-done.14, bf16[16,48,256]{2,1,0:T(8,128)(2,1)} %copy-done.13, bf16[16,48,256]{2,1,0:T(8,128)(2,1)} %copy-done.12, ...), custom_call_target="tpu_custom_call" | custom-call | flops 2818572288 | bytes 5898240 | tf_op jit(solution)/shard_map/outputs/pallas_call | solution.py:367
  286.4 0.0 copy-start.3
  286.4 1.2 copy-done.3
  287.6 8.1 %all-to-all-start.2 = ((bf16[32,48,896]{2,1,0:T(8,128)(2,1)}), bf16[32,48,896]{2,1,0:T(8,128)(2,1)S(1)}, u32[]{:S(2)}, u32[]{:S(2)}) async-start(bf16[32,48,896]{2,1,0:T(8,128)(2,1)} %bitcast.24), calls=%async_computation.2 | async-start | bytes 5505024 | tf_op jit(solution)/shard_map/all_to_all | solution.py:462
  295.7 10.0 %update.1 = bf16[32,3,112,256]{3,2,1,0:T(8,128)(2,1)} custom-call(s32[32]{0:T(128)} %plan.1, s32[32]{0:T(128)} %placement.1, bf16[32,112,256]{2,1,0:T(8,128)(2,1)} %copy-done.3, bf16[32,336,256]{2,1,0:T(8,128)(2,1)} %all-to-all-done.5.gate.first.second, bf16[32,336,256]{2,1,0:T(8,128)(2,1)} %all-to-all-done.5.gate.first.second, ...), custom_call_target="tpu_custom_call" | custom-call | flops 18350080 | bytes 10485760 | tf_op jit(solution)/shard_map/update/pallas_call | solution.py:427
  305.7 25.3 %all-to-all-done.2 = bf16[32,48,896]{2,1,0:T(8,128)(2,1)S(1)} async-done(((bf16[32,48,896]{2,1,0:T(8,128)(2,1)}), bf16[32,48,896]{2,1,0:T(8,128)(2,1)S(1)}, u32[]{:S(2)}, u32[]{:S(2)}) %all-to-all-start.2) | async-done | bytes 2752544 | tf_op jit(solution)/shard_map/all_to_all | solution.py:462
  331.0 1.6 copy-done.1
  332.6 5.4 %all-to-all-start.6 = ((bf16[32,3,112,256]{3,2,1,0:T(8,128)(2,1)}), bf16[32,3,112,256]{3,2,1,0:T(8,128)(2,1)}, u32[]{:S(2)}, u32[]{:S(2)}) async-start(bf16[32,3,112,256]{3,2,1,0:T(8,128)(2,1)} %update.1), calls=%async_computation.6 | async-start | bytes 11010048 | tf_op jit(solution)/shard_map/all_to_all | solution.py:462
  338.0 3.7 combine.1
  341.7 64.1 %all-to-all-done.6.moments = bf16[32,3,112,256]{3,2,1,0:T(8,128)(2,1)} async-done(((bf16[32,3,112,256]{3,2,1,0:T(8,128)(2,1)}), bf16[32,3,112,256]{3,2,1,0:T(8,128)(2,1)}, u32[]{:S(2)}, u32[]{:S(2)}) %all-to-all-start.6) | async-done | bytes 5505056 | tf_op jit(solution)/shard_map/all_to_all | solution.py:462
  405.8 5.5 %finish.1 = (bf16[32,112,256]{2,1,0:T(8,128)(2,1)}, bf16[32,112,256]{2,1,0:T(8,128)(2,1)}, bf16[32,112,256]{2,1,0:T(8,128)(2,1)}) custom-call(bf16[32,3,112,256]{3,2,1,0:T(8,128)(2,1)} %all-to-all-done.6.moments), custom_call_target="tpu_custom_call" | custom-call | bytes 12582912 | tf_op jit(solution)/shard_map/finish/pallas_call | solution.py:450
  (48 shorter events, 0.1 us)
Async XLA Ops:
  3.2 24.1 %all-to-all-start = ((bf16[32,16,896]{2,1,0:T(8,128)(2,1)}), bf16[32,16,896]{2,1,0:T(8,128)(2,1)S(1)}, u32[]{:S(2)}, u32[]{:S(2)}) async-start(bf16[32,16,896]{2,1,0:T(8,128)(2,1)} %get-tuple-element.29), calls=%async_computation | async-start | bytes 1835008 | tf_op jit(solution)/shard_map/all_to_all | solution.py:462
  27.4 75.4 %copy-start.2 = (bf16[32,16,896]{2,1,0:T(8,128)(2,1)}, bf16[32,16,896]{2,1,0:T(8,128)(2,1)S(1)}, u32[]{:S(2)}) copy-start(bf16[32,16,896]{2,1,0:T(8,128)(2,1)S(1)} %all-to-all-done.refs_0_.refs_7_) | copy-start | bytes 2752516
  27.4 29.4 %all-to-all-start.1 = ((bf16[32,32,896]{2,1,0:T(8,128)(2,1)}), bf16[32,32,896]{2,1,0:T(8,128)(2,1)S(1)}, u32[]{:S(2)}, u32[]{:S(2)}) async-start(bf16[32,32,896]{2,1,0:T(8,128)(2,1)} %rest_rows.1), calls=%async_computation.1 | async-start | bytes 3670016 | tf_op jit(solution)/shard_map/all_to_all | solution.py:462
  56.8 49.9 %copy-start = (bf16[32,32,896]{2,1,0:T(8,128)(2,1)}, bf16[32,32,896]{2,1,0:T(8,128)(2,1)S(1)}, u32[]{:S(2)}) copy-start(bf16[32,32,896]{2,1,0:T(8,128)(2,1)S(1)} %all-to-all-done.1.refs_7_.refs_14_) | copy-start | bytes 5505028
  56.8 40.6 %all-to-all-start.3 = ((bf16[32,48,896]{2,1,0:T(8,128)(2,1)}), bf16[32,48,896]{2,1,0:T(8,128)(2,1)}, u32[]{:S(2)}, u32[]{:S(2)}) async-start(bf16[32,48,896]{2,1,0:T(8,128)(2,1)} %bitcast.25), calls=%async_computation.3 | async-start | bytes 5505024 | tf_op jit(solution)/shard_map/all_to_all | solution.py:462
  97.4 138.6 %all-to-all-start.5 = ((bf16[32,336,256]{2,1,0:T(8,128)(2,1)}), bf16[32,336,256]{2,1,0:T(8,128)(2,1)}, u32[]{:S(2)}, u32[]{:S(2)}) async-start(bf16[32,336,256]{2,1,0:T(8,128)(2,1)} %pad_maximum_fusion), calls=%async_computation.5 | async-start | bytes 11010048 | tf_op jit(solution)/shard_map/all_to_all | solution.py:462
  102.9 13.3 %collective-permute-start.3 = (bf16[16,16,896]{2,1,0:T(8,128)(2,1)S(1)}, bf16[16,16,896]{2,1,0:T(8,128)(2,1)}, u32[]{:S(2)}, u32[]{:S(2)}) collective-permute-start(bf16[16,16,896]{2,1,0:T(8,128)(2,1)S(1)} %get-tuple-element.48), channel_id=1, source_target_pairs={{0,96},{32,0},{64,32},{96,64},{1,97},{33,1},{65,33},{97,65},{2,98}... | collective-permute-start | bytes 1376264 | tf_op jit(solution)/shard_map/ppermute | solution.py:466
  106.7 12.7 %collective-permute-start.1 = (bf16[16,16,896]{2,1,0:T(8,128)(2,1)S(1)}, bf16[16,16,896]{2,1,0:T(8,128)(2,1)S(1)}, u32[]{:S(2)}, u32[]{:S(2)}) collective-permute-start(bf16[16,16,896]{2,1,0:T(8,128)(2,1)S(1)} %get-tuple-element.48), channel_id=1, source_target_pairs={{0,32},{32,64},{64,96},{96,0},{1,33},{33,65},{65,97},{97,1},{2,34}... | collective-permute-start | bytes 1376264 | tf_op jit(solution)/shard_map/ppermute | solution.py:466
  107.8 51.2 %collective-permute-start.9 = (bf16[16,32,896]{2,1,0:T(8,128)(2,1)}, bf16[16,32,896]{2,1,0:T(8,128)(2,1)S(1)}, u32[]{:S(2)}, u32[]{:S(2)}) collective-permute-start(bf16[16,32,896]{2,1,0:T(8,128)(2,1)} %get-tuple-element.46), channel_id=1, source_target_pairs={{0,96},{32,0},{64,32},{96,64},{1,97},{33,1},{65,33},{97,65},{2,98}... | collective-permute-start | bytes 2752520 | tf_op jit(solution)/shard_map/ppermute | solution.py:466
  110.5 48.6 %collective-permute-start.6 = (bf16[16,32,896]{2,1,0:T(8,128)(2,1)S(1)}, bf16[16,32,896]{2,1,0:T(8,128)(2,1)S(1)}, u32[]{:S(2)}, u32[]{:S(2)}) collective-permute-start(bf16[16,32,896]{2,1,0:T(8,128)(2,1)S(1)} %get-tuple-element.47), channel_id=1, source_target_pairs={{0,32},{32,64},{64,96},{96,0},{1,33},{33,65},{65,97},{97,1},{2,34}... | collective-permute-start | bytes 2752520 | tf_op jit(solution)/shard_map/ppermute | solution.py:466
  110.5 35.2 %collective-permute-start.2 = (bf16[16,16,896]{2,1,0:T(8,128)(2,1)S(1)}, bf16[16,16,896]{2,1,0:T(8,128)(2,1)}, u32[]{:S(2)}, u32[]{:S(2)}) collective-permute-start(bf16[16,16,896]{2,1,0:T(8,128)(2,1)S(1)} %get-tuple-element.49), channel_id=1, source_target_pairs={{0,96},{32,0},{64,32},{96,64},{1,97},{33,1},{65,33},{97,65},{2,98}... | collective-permute-start | bytes 1376264 | tf_op jit(solution)/shard_map/ppermute | solution.py:466
  116.2 33.0 %collective-permute-start = (bf16[16,16,896]{2,1,0:T(8,128)(2,1)S(1)}, bf16[16,16,896]{2,1,0:T(8,128)(2,1)}, u32[]{:S(2)}, u32[]{:S(2)}) collective-permute-start(bf16[16,16,896]{2,1,0:T(8,128)(2,1)S(1)} %get-tuple-element.49), channel_id=1, source_target_pairs={{0,32},{32,64},{64,96},{96,0},{1,33},{33,65},{65,97},{97,1},{2,34}... | collective-permute-start | bytes 1376264 | tf_op jit(solution)/shard_map/ppermute | solution.py:466
  119.4 0.8 copy-start.7
  120.2 35.4 %collective-permute-start.5 = (bf16[16,16,896]{2,1,0:T(8,128)(2,1)}, bf16[16,16,896]{2,1,0:T(8,128)(2,1)}, u32[]{:S(2)}, u32[]{:S(2)}) collective-permute-start(bf16[16,16,896]{2,1,0:T(8,128)(2,1)} %collective-permute-done.3.refs_4_.refs_11_), channel_id=1, source_target_pairs={{0,96},{32,0},{64,32},{96,64},{1,97},{33,1},{65,33},{97,65},{2,98}... | collective-permute-start | bytes 1376264 | tf_op jit(solution)/shard_map/ppermute | solution.py:466
  145.7 19.4 %collective-permute-start.21 = (bf16[768,256]{1,0:T(8,128)(2,1)}, bf16[768,256]{1,0:T(8,128)(2,1)}, u32[]{:S(2)}, u32[]{:S(2)}) collective-permute-start(bf16[768,256]{1,0:T(8,128)(2,1)} %get-tuple-element.39), channel_id=1, source_target_pairs={{0,96},{32,0},{64,32},{96,64},{1,97},{33,1},{65,33},{97,65},{2,98}... | collective-permute-start | bytes 1179656 | tf_op jit(solution)/shard_map/ppermute | solution.py:466
  149.2 59.3 %collective-permute-start.7 = (bf16[16,32,896]{2,1,0:T(8,128)(2,1)}, bf16[16,32,896]{2,1,0:T(8,128)(2,1)}, u32[]{:S(2)}, u32[]{:S(2)}) collective-permute-start(bf16[16,32,896]{2,1,0:T(8,128)(2,1)} %get-tuple-element.46), channel_id=1, source_target_pairs={{0,32},{32,64},{64,96},{96,0},{1,33},{33,65},{65,97},{97,1},{2,34}... | collective-permute-start | bytes 2752520 | tf_op jit(solution)/shard_map/ppermute | solution.py:466
  155.6 55.6 %collective-permute-start.8 = (bf16[16,32,896]{2,1,0:T(8,128)(2,1)S(1)}, bf16[16,32,896]{2,1,0:T(8,128)(2,1)}, u32[]{:S(2)}, u32[]{:S(2)}) collective-permute-start(bf16[16,32,896]{2,1,0:T(8,128)(2,1)S(1)} %get-tuple-element.47), channel_id=1, source_target_pairs={{0,96},{32,0},{64,32},{96,64},{1,97},{33,1},{65,33},{97,65},{2,98}... | collective-permute-start | bytes 2752520 | tf_op jit(solution)/shard_map/ppermute | solution.py:466
  159.0 41.6 %copy-start.4 = (bf16[16,32,896]{2,1,0:T(8,128)(2,1)}, bf16[16,32,896]{2,1,0:T(8,128)(2,1)S(1)}, u32[]{:S(2)}) copy-start(bf16[16,32,896]{2,1,0:T(8,128)(2,1)S(1)} %collective-permute-done.9.refs_11_.refs_18_) | copy-start | bytes 2752516
  159.0 52.2 %collective-permute-start.11 = (bf16[16,32,896]{2,1,0:T(8,128)(2,1)S(1)}, bf16[16,32,896]{2,1,0:T(8,128)(2,1)}, u32[]{:S(2)}, u32[]{:S(2)}) collective-permute-start(bf16[16,32,896]{2,1,0:T(8,128)(2,1)S(1)} %collective-permute-done.9.refs_11_.refs_18_), channel_id=1, source_target_pairs={{0,96},{32,0},{64,32},{96,64},{1,97},{33,1},{65,33},{97,65},{2,98}... | collective-permute-start | bytes 2752520 | tf_op jit(solution)/shard_map/ppermute | solution.py:466
  159.1 41.5 %copy-start.5 = (bf16[16,32,896]{2,1,0:T(8,128)(2,1)}, bf16[16,32,896]{2,1,0:T(8,128)(2,1)S(1)}, u32[]{:S(2)}) copy-start(bf16[16,32,896]{2,1,0:T(8,128)(2,1)S(1)} %collective-permute-done.6.refs_8_.refs_15_) | copy-start | bytes 2752516
  159.1 54.8 %collective-permute-start.10 = (bf16[16,32,896]{2,1,0:T(8,128)(2,1)S(1)}, bf16[16,32,896]{2,1,0:T(8,128)(2,1)}, u32[]{:S(2)}, u32[]{:S(2)}) collective-permute-start(bf16[16,32,896]{2,1,0:T(8,128)(2,1)S(1)} %collective-permute-done.6.refs_8_.refs_15_), channel_id=1, source_target_pairs={{0,32},{32,64},{64,96},{96,0},{1,33},{33,65},{65,97},{97,1},{2,34}... | collective-permute-start | bytes 2752520 | tf_op jit(solution)/shard_map/ppermute | solution.py:466
  165.0 33.3 %collective-permute-start.20 = (bf16[768,256]{1,0:T(8,128)(2,1)}, bf16[768,256]{1,0:T(8,128)(2,1)}, u32[]{:S(2)}, u32[]{:S(2)}) collective-permute-start(bf16[768,256]{1,0:T(8,128)(2,1)} %get-tuple-element.37), channel_id=1, source_target_pairs={{0,32},{32,64},{64,96},{96,0},{1,33},{33,65},{65,97},{97,1},{2,34}... | collective-permute-start | bytes 1179656 | tf_op jit(solution)/shard_map/ppermute | solution.py:466
  198.3 10.2 %collective-permute-start.4 = (bf16[16,16,896]{2,1,0:T(8,128)(2,1)}, bf16[16,16,896]{2,1,0:T(8,128)(2,1)S(1)}, u32[]{:S(2)}, u32[]{:S(2)}) collective-permute-start(bf16[16,16,896]{2,1,0:T(8,128)(2,1)} %collective-permute-done.refs_1_.refs_8_), channel_id=1, source_target_pairs={{0,32},{32,64},{64,96},{96,0},{1,33},{33,65},{65,97},{97,1},{2,34}... | collective-permute-start | bytes 1376264 | tf_op jit(solution)/shard_map/ppermute | solution.py:466
  208.5 5.4 %copy-start.8 = (bf16[16,16,896]{2,1,0:T(8,128)(2,1)}, bf16[16,16,896]{2,1,0:T(8,128)(2,1)S(1)}, u32[]{:S(2)}) copy-start(bf16[16,16,896]{2,1,0:T(8,128)(2,1)S(1)} %collective-permute-done.4.refs_5_.refs_12_) | copy-start | bytes 1376260
  208.5 17.9 %collective-permute-start.19 = (bf16[768,256]{1,0:T(8,128)(2,1)}, bf16[768,256]{1,0:T(8,128)(2,1)}, u32[]{:S(2)}, u32[]{:S(2)}) collective-permute-start(bf16[768,256]{1,0:T(8,128)(2,1)} %get-tuple-element.35), channel_id=1, source_target_pairs={{0,32},{32,64},{64,96},{96,0},{1,33},{33,65},{65,97},{97,1},{2,34}... | collective-permute-start | bytes 1179656 | tf_op jit(solution)/shard_map/ppermute | solution.py:466
  208.5 17.9 %collective-permute-start.18 = (bf16[768,256]{1,0:T(8,128)(2,1)}, bf16[768,256]{1,0:T(8,128)(2,1)}, u32[]{:S(2)}, u32[]{:S(2)}) collective-permute-start(bf16[768,256]{1,0:T(8,128)(2,1)} %get-tuple-element.34), channel_id=1, source_target_pairs={{0,96},{32,0},{64,32},{96,64},{1,97},{33,1},{65,33},{97,65},{2,98}... | collective-permute-start | bytes 1179656 | tf_op jit(solution)/shard_map/ppermute | solution.py:466
  211.2 15.2 %collective-permute-start.22 = (bf16[768,256]{1,0:T(8,128)(2,1)}, bf16[768,256]{1,0:T(8,128)(2,1)S(1)}, u32[]{:S(2)}, u32[]{:S(2)}) collective-permute-start(bf16[768,256]{1,0:T(8,128)(2,1)} %get-tuple-element.40), channel_id=1, source_target_pairs={{0,32},{32,64},{64,96},{96,0},{1,33},{33,65},{65,97},{97,1},{2,34}... | collective-permute-start | bytes 1179656 | tf_op jit(solution)/shard_map/ppermute | solution.py:466
  211.2 15.3 %collective-permute-start.23 = (bf16[768,256]{1,0:T(8,128)(2,1)}, bf16[768,256]{1,0:T(8,128)(2,1)S(1)}, u32[]{:S(2)}, u32[]{:S(2)}) collective-permute-start(bf16[768,256]{1,0:T(8,128)(2,1)} %get-tuple-element.41), channel_id=1, source_target_pairs={{0,96},{32,0},{64,32},{96,64},{1,97},{33,1},{65,33},{97,65},{2,98}... | collective-permute-start | bytes 1179656 | tf_op jit(solution)/shard_map/ppermute | solution.py:466
  226.4 0.8 copy-start.9
  226.5 0.9 copy-start.10
  236.0 12.6 %copy-start.6 = (bf16[1536,256]{1,0:T(8,128)(2,1)S(1)}, bf16[1536,256]{1,0:T(8,128)(2,1)}, u32[]{:S(2)}) copy-start(bf16[1536,256]{1,0:T(8,128)(2,1)} %get-tuple-element.30) | copy-start | bytes 2359300
  236.0 50.4 %all-to-all-start.4 = ((bf16[32,112,256]{2,1,0:T(8,128)(2,1)}), bf16[32,112,256]{2,1,0:T(8,128)(2,1)S(1)}, u32[]{:S(2)}, u32[]{:S(2)}) async-start(bf16[32,112,256]{2,1,0:T(8,128)(2,1)} %bitcast.23), calls=%async_computation.4 | async-start | bytes 3670016 | tf_op jit(solution)/shard_map/all_to_all | solution.py:462
  248.7 11.7 %collective-permute-start.12 = (bf16[16,48,256]{2,1,0:T(8,128)(2,1)S(1)}, bf16[16,48,256]{2,1,0:T(8,128)(2,1)S(1)}, u32[]{:S(2)}, u32[]{:S(2)}) collective-permute-start(bf16[16,48,256]{2,1,0:T(8,128)(2,1)S(1)} %bitcast.33), channel_id=1, source_target_pairs={{0,32},{32,64},{64,96},{96,0},{1,33},{33,65},{65,97},{97,1},{2,34}... | collective-permute-start | bytes 1179656 | tf_op jit(solution)/shard_map/ppermute | solution.py:466
  248.8 11.6 %collective-permute-start.15 = (bf16[16,48,256]{2,1,0:T(8,128)(2,1)S(1)}, bf16[16,48,256]{2,1,0:T(8,128)(2,1)S(1)}, u32[]{:S(2)}, u32[]{:S(2)}) collective-permute-start(bf16[16,48,256]{2,1,0:T(8,128)(2,1)S(1)} %bitcast.31), channel_id=1, source_target_pairs={{0,96},{32,0},{64,32},{96,64},{1,97},{33,1},{65,33},{97,65},{2,98}... | collective-permute-start | bytes 1179656 | tf_op jit(solution)/shard_map/ppermute | solution.py:466
  251.4 16.4 %collective-permute-start.14 = (bf16[16,48,256]{2,1,0:T(8,128)(2,1)S(1)}, bf16[16,48,256]{2,1,0:T(8,128)(2,1)S(1)}, u32[]{:S(2)}, u32[]{:S(2)}) collective-permute-start(bf16[16,48,256]{2,1,0:T(8,128)(2,1)S(1)} %bitcast.34), channel_id=1, source_target_pairs={{0,96},{32,0},{64,32},{96,64},{1,97},{33,1},{65,33},{97,65},{2,98}... | collective-permute-start | bytes 1179656 | tf_op jit(solution)/shard_map/ppermute | solution.py:466
  251.4 17.4 %collective-permute-start.13 = (bf16[16,48,256]{2,1,0:T(8,128)(2,1)S(1)}, bf16[16,48,256]{2,1,0:T(8,128)(2,1)S(1)}, u32[]{:S(2)}, u32[]{:S(2)}) collective-permute-start(bf16[16,48,256]{2,1,0:T(8,128)(2,1)S(1)} %bitcast.32), channel_id=1, source_target_pairs={{0,32},{32,64},{64,96},{96,0},{1,33},{33,65},{65,97},{97,1},{2,34}... | collective-permute-start | bytes 1179656 | tf_op jit(solution)/shard_map/ppermute | solution.py:466
  260.4 18.3 %copy-start.11 = (bf16[16,48,256]{2,1,0:T(8,128)(2,1)}, bf16[16,48,256]{2,1,0:T(8,128)(2,1)S(1)}, u32[]{:S(2)}) copy-start(bf16[16,48,256]{2,1,0:T(8,128)(2,1)S(1)} %collective-permute-done.12.refs_1_) | copy-start | bytes 1179652
  260.4 16.9 %collective-permute-start.16 = (bf16[16,48,256]{2,1,0:T(8,128)(2,1)S(1)}, bf16[16,48,256]{2,1,0:T(8,128)(2,1)S(1)}, u32[]{:S(2)}, u32[]{:S(2)}) collective-permute-start(bf16[16,48,256]{2,1,0:T(8,128)(2,1)S(1)} %collective-permute-done.12.refs_1_), channel_id=1, source_target_pairs={{0,32},{32,64},{64,96},{96,0},{1,33},{33,65},{65,97},{97,1},{2,34}... | collective-permute-start | bytes 1179656 | tf_op jit(solution)/shard_map/ppermute | solution.py:466
  260.4 18.3 %copy-start.12 = (bf16[16,48,256]{2,1,0:T(8,128)(2,1)}, bf16[16,48,256]{2,1,0:T(8,128)(2,1)S(1)}, u32[]{:S(2)}) copy-start(bf16[16,48,256]{2,1,0:T(8,128)(2,1)S(1)} %collective-permute-done.15.refs_4_) | copy-start | bytes 1179652
  260.4 16.8 %collective-permute-start.17 = (bf16[16,48,256]{2,1,0:T(8,128)(2,1)S(1)}, bf16[16,48,256]{2,1,0:T(8,128)(2,1)S(1)}, u32[]{:S(2)}, u32[]{:S(2)}) collective-permute-start(bf16[16,48,256]{2,1,0:T(8,128)(2,1)S(1)} %collective-permute-done.15.refs_4_), channel_id=1, source_target_pairs={{0,96},{32,0},{64,32},{96,64},{1,97},{33,1},{65,33},{97,65},{2,98}... | collective-permute-start | bytes 1179656 | tf_op jit(solution)/shard_map/ppermute | solution.py:466
  267.8 10.9 %copy-start.13 = (bf16[16,48,256]{2,1,0:T(8,128)(2,1)}, bf16[16,48,256]{2,1,0:T(8,128)(2,1)S(1)}, u32[]{:S(2)}) copy-start(bf16[16,48,256]{2,1,0:T(8,128)(2,1)S(1)} %collective-permute-done.14.refs_3_) | copy-start | bytes 1179652
  268.8 9.9 %copy-start.14 = (bf16[16,48,256]{2,1,0:T(8,128)(2,1)}, bf16[16,48,256]{2,1,0:T(8,128)(2,1)S(1)}, u32[]{:S(2)}) copy-start(bf16[16,48,256]{2,1,0:T(8,128)(2,1)S(1)} %collective-permute-done.13.refs_2_) | copy-start | bytes 1179652
  277.2 0.7 copy-start.15
  278.0 0.7 copy-start.16
  286.4 1.2 copy-start.3
  287.6 43.4 %all-to-all-start.2 = ((bf16[32,48,896]{2,1,0:T(8,128)(2,1)}), bf16[32,48,896]{2,1,0:T(8,128)(2,1)S(1)}, u32[]{:S(2)}, u32[]{:S(2)}) async-start(bf16[32,48,896]{2,1,0:T(8,128)(2,1)} %bitcast.24), calls=%async_computation.2 | async-start | bytes 5505024 | tf_op jit(solution)/shard_map/all_to_all | solution.py:462
  331.0 1.6 copy-start.1
  332.6 73.3 %all-to-all-start.6 = ((bf16[32,3,112,256]{3,2,1,0:T(8,128)(2,1)}), bf16[32,3,112,256]{3,2,1,0:T(8,128)(2,1)}, u32[]{:S(2)}, u32[]{:S(2)}) async-start(bf16[32,3,112,256]{3,2,1,0:T(8,128)(2,1)} %update.1), calls=%async_computation.6 | async-start | bytes 11010048 | tf_op jit(solution)/shard_map/all_to_all | solution.py:462

commit v5 on v4

--- a/solution.py
+++ b/solution.py
@@ -167,39 +167,20 @@
     return pl.BlockSpec((block, width), lambda i: (i, 0))
 
 
-def piece_specs(n, pieces):
-    half = HALF // n
-    specs = []
-    for group in pieces:
-        shape = (n,) + group[0].shape[1:]
-        own = pl.BlockSpec(shape, lambda i: (i, 0, 0))
-        low = pl.BlockSpec(shape, lambda i: (jnp.minimum(i, half - 1), 0, 0))
-        high = pl.BlockSpec(shape, lambda i: (jnp.maximum(i - half, 0), 0, 0))
-        specs += [own] + [low, high] * 3
-    return specs
+def half_of(n, pieces, part):
+    inputs, specs = [], []
+    for own, la, lb, ra, rb, fa, fb in pieces:
+        shape = (n,) + own.shape[1:]
+        inputs += [own] + ([la, ra, fa] if part == 0 else [lb, rb, fb])
+        specs += [pl.BlockSpec(shape, lambda i: (part * (HALF // n) + i, 0, 0))]
+        specs += [pl.BlockSpec(shape, lambda i: (i, 0, 0))] * 3
+    return inputs, specs
 
 
 def whole(shape):
     return pl.BlockSpec(shape, lambda i: (0,) * len(shape))
 
 
-def gather_pieces(n, dp, pieces, out):
-    first = pl.program_id(0) < HALF // n
-    at = 0
-    for j in range(0, len(pieces), 7):
-        own, la, lb, ra, rb, fa, fb = pieces[j : j + 7]
-        rows, width = own.shape[1:]
-        for shift, x in (
-            (0, own[...]),
-            (3, jnp.where(first, la[...], lb[...])),
-            (1, jnp.where(first, ra[...], rb[...])),
-            (2, jnp.where(first, fa[...], fb[...])),
-        ):
-            q = lax.rem(dp[0] + shift, N_DP)
-            out[:, at : at + rows, pl.ds(pl.multiple_of(q * width, width), width)] = x
-        at += rows
-
-
 def flat(pieces):
     return [x for group in pieces for x in group]
 
@@ -209,7 +190,13 @@
 
 def hidden_kernel(count, dp, *refs):
     pieces, (wg, wu, slope_out, h_out, gathered) = refs[:count], refs[count:]
-    gather_pieces(HIDDEN_SOURCES, dp, pieces, gathered)
+    at = 0
+    for j in range(0, count, N_DP):
+        rows = pieces[j].shape[1]
+        for shift, ref in zip((0, 3, 1, 2), pieces[j : j + N_DP]):
+            q = lax.rem(dp[0] + shift, N_DP)
+            gathered[:, at : at + rows, pl.ds(pl.multiple_of(q * QD, QD), QD)] = ref[...]
+        at += rows
     x = gathered[...].reshape(HIDDEN_SOURCES * CAP, D)
     g = jnp.dot(x, wg[...], preferred_element_type=f32) * scale_in
     u = jnp.dot(x, wu[...], preferred_element_type=f32) * scale_in
@@ -218,22 +205,22 @@
     h_out[...] = (g * s * u).astype(bf16)
 
 
-def hidden_of(dp, pieces, wg, wu):
+def hidden_of(dp, pieces, wg, wu, part):
     n = HIDDEN_SOURCES
     block = n * CAP
-    inputs = flat(pieces)
+    rows = ROWS // 2
+    inputs, specs = half_of(n, pieces, part)
     return pl.pallas_call(
         functools.partial(hidden_kernel, len(inputs)),
-        grid=(SLOTS // n,),
+        grid=(HALF // n,),
         out_shape=[
-            jax.ShapeDtypeStruct((ROWS, QF), f32),
-            jax.ShapeDtypeStruct((ROWS, QF), bf16),
+            jax.ShapeDtypeStruct((rows, QF), f32),
+            jax.ShapeDtypeStruct((rows, QF), bf16),
         ],
-        in_specs=[sspec()] + piece_specs(n, pieces) + [whole((D, QF)), whole((D, QF))],
+        in_specs=[sspec()] + specs + [whole((D, QF)), whole((D, QF))],
         out_specs=[row_block(block, QF)] * 2,
         scratch_shapes=[VMEM((n, CAP, D), bf16)],
-        cost_estimate=cost(4 * ROWS * D * QF, ROWS * D * 2 + 8 * D * QF),
-        name="hidden",
+        cost_estimate=cost(4 * rows * D * QF, rows * D * 2 + 8 * D * QF),
     )(dp, *inputs, wg, wu)
 
 
@@ -273,12 +260,13 @@
 
 
 def weight_kernel(dp, *refs):
-    sums, slope, pieces = refs[:6], refs[6], refs[7:21]
-    out, x0, x1, parts, slopes, sems = refs[21:]
+    sums, slope, pieces = refs[:6], refs[6:8], refs[8:22]
+    out, x0, x1, parts, slopes, sems = refs[22:]
     count = len(sums)
     first = [pltpu.make_async_copy(r, parts.at[n], sems.at[n]) for n, r in enumerate(sums)]
-    first.append(pltpu.make_async_copy(slope, slopes, sems.at[count]))
-    count += 1
+    for h, ref in enumerate(slope):
+        first.append(pltpu.make_async_copy(ref, slopes.at[h], sems.at[count]))
+        count += 1
     by_piece = []
     for k in range(N_DP):
         copies = []
@@ -300,7 +288,7 @@
     gg = []
     for h in range(2):
         total = parts[h].astype(f32) + parts[2 + h].astype(f32) + parts[4 + h].astype(f32)
-        total = total * scale_mid * slopes[pl.ds(HALF_ROWS * h, HALF_ROWS), :]
+        total = total * scale_mid * slopes[h]
         gg.append(total.astype(bf16).reshape(HALF, CAP, QF))
     gg = jnp.concatenate(gg, axis=0)
     cut = CHUNKS[0][1]
@@ -317,7 +305,7 @@
 
 
 def weight_grads(dp, sums, slope, pieces):
-    inputs = [*sums, slope, *flat(pieces)]
+    inputs = [*sums, *slope, *flat(pieces)]
     return pl.pallas_call(
         weight_kernel,
         out_shape=jax.ShapeDtypeStruct((D, QF), bf16),
@@ -326,7 +314,7 @@
         scratch_shapes=[
             *[VMEM((N_DP, SLOTS, hi - lo, QD), bf16) for lo, hi in CHUNKS],
             VMEM((len(sums), HALF_ROWS, QF), bf16),
-            VMEM((ROWS, QF), f32),
+            VMEM((2, HALF_ROWS, QF), f32),
             pltpu.SemaphoreType.DMA((len(inputs),)),
         ],
         cost_estimate=cost(2 * ROWS * D * QF, ROWS * D * 2 + (4 << 20)),
@@ -355,7 +343,11 @@
 
 def output_kernel(count, dp, *refs):
     pieces, (wd, out, gathered) = refs[:count], refs[count:]
-    gather_pieces(OUTPUT_SOURCES, dp, pieces, gathered)
+    first = pl.program_id(0) < HALF // OUTPUT_SOURCES
+    for j, shift in zip(range(0, count, 2), (0, 3, 1, 2)):
+        q = lax.rem(dp[0] + shift, N_DP)
+        to = pl.ds(pl.multiple_of(q * QF, QF), QF)
+        gathered[:, :, to] = jnp.where(first, pieces[j][...], pieces[j + 1][...])
     x = gathered[...].reshape(OUTPUT_SOURCES * CAP, FF)
     total = jnp.dot(x, wd[...], preferred_element_type=f32)
     out[...] = (total * scale_mid).astype(bf16)
@@ -363,37 +355,28 @@
 
 def outputs_of(dp, pieces, wd):
     n = OUTPUT_SOURCES
-    inputs = flat(pieces)
-    return pl.pallas_call(
-        functools.partial(output_kernel, len(inputs)),
+    half = HALF // n
+    shape = (n, CAP, QF)
+    low = pl.BlockSpec(shape, lambda i: (jnp.minimum(i, half - 1), 0, 0))
+    high = pl.BlockSpec(shape, lambda i: (jnp.maximum(i - half, 0), 0, 0))
+    return pl.pallas_call(
+        functools.partial(output_kernel, len(pieces)),
         grid=(SLOTS // n,),
         out_shape=jax.ShapeDtypeStruct((ROWS, QD), bf16),
-        in_specs=[sspec()] + piece_specs(n, pieces) + [whole((FF, QD))],
+        in_specs=[sspec()] + [low, high] * N_DP + [whole((FF, QD))],
         out_specs=row_block(n * CAP, QD),
         scratch_shapes=[VMEM((n, CAP, FF), bf16)],
         cost_estimate=cost(2 * ROWS * FF * QD, ROWS * (FF + QD) * 2),
         name="outputs",
-    )(dp, *inputs, wd)
-
-
-def combine_kernel(high, low, rows, out):
-    total = jnp.zeros(out.shape, f32)
+    )(dp, *pieces, wd)
+
+
+def combine(high, low, rows):
+    total = None
     for part in (high, low):
-        total = total + lax.dot_general(
-            part[...], rows[...], (((0,), (0,)), ((), ())), preferred_element_type=f32
-        )
-    out[...] = total.astype(bf16)
-
-
-def combine(high, low, rows):
-    return pl.pallas_call(
-        combine_kernel,
-        out_shape=jax.ShapeDtypeStruct((TOK, QD), bf16),
-        in_specs=[vspec()] * 3,
-        out_specs=vspec(),
-        cost_estimate=cost(4 * ROWS * TOK * QD, 4 << 20),
-        name="combine",
-    )(high, low, rows)
+        one = lax.dot_general(part, rows, (((0,), (0,)), ((), ())), preferred_element_type=f32)
+        total = one if total is None else total + one
+    return total.astype(bf16)
 
 
 UPDATE_ROWS = 16
@@ -445,7 +428,7 @@
 
 
 def finish(moments):
-    n = 8
+    n = 16
     part = pl.BlockSpec((n, PART, QF), lambda i: (i, 0, 0))
     return pl.pallas_call(
         finish_kernel,
@@ -466,15 +449,14 @@
     return lax.ppermute(x, "dp", [(i, (i + by) % N_DP) for i in range(N_DP)])
 
 
-def ring(x):
-    low, high = x[:HALF], x[HALF:]
+def ring(low, high):
     la = shift(low, 1)
     rb = shift(high, -1)
     lb = shift(high, 1)
     ra = shift(low, -1)
     fa = shift(la, 1)
     fb = shift(rb, -1)
-    return (x, la, lb, ra, rb, fa, fb)
+    return (la, lb, ra, rb, fa, fb)
 
 
 def device_step(
@@ -503,8 +485,8 @@
         axis=1,
     )
     states = exchange(packed)
-    pieces = [ring(x) for x in got]
-    slope, h = hidden_of(dp, pieces, wg, wu)
+    pieces = [(x, *ring(x[:HALF], x[HALF:])) for x in got]
+    slope, h = zip(*[hidden_of(dp, pieces, wg, wu, part) for part in range(2)])
     low = partial_grads(dp, got_grads, wd, 0)
     high = partial_grads(dp, got_grads, wd, 1)
     far_low = shift(low[2], 1)
@@ -518,7 +500,8 @@
     wgrad = weight_grads(dp, sums, slope, pieces)
     got_wgrad = exchange(wgrad.reshape(SLOTS, PART, QF))
     moments = exchange(update(migration_plan, placement, got_wgrad, states))
-    out = outputs_of(dp, [ring(h.reshape(SLOTS, CAP, QF))], wd)
+    h = [x.reshape(HALF, CAP, QF) for x in h]
+    out = outputs_of(dp, (*h, *ring(*h)), wd)
     returned = exchange(out.reshape(SLOTS, CAP, QD)).reshape(ROWS, QD)
     layer_output = combine(weight_high, weight_low, returned)
     results = finish(moments)

time: 418 us -> 427 us (1.022)
  waiting for transfers between devices: 249 us -> 264 us
  starting transfers between devices: 80.1 us -> 74.1 us
    ppermute x24, waiting for transfers between devices: 95.2 us -> 108 us  [shift(): return lax.ppermute(x, 'dp', [(i, (i + by) % N_DP) for i in range(N_DP)])]
    ppermute x24, starting transfers between devices: 31 us -> 26.2 us  [shift(): return lax.ppermute(x, 'dp', [(i, (i + by) % N_DP) for i in range(N_DP)])]
  transfers between devices with their start and end apart: 31 -> 31, of which waited for: 15 -> 14; matrix products, arithmetic and copies ran while one was open for 2% -> 2% of each run, Pallas kernels for 15% -> 14%
where the time goes in v5:
time: 427 us; the launch traced here: 420 us
  waiting for transfers between devices  264 us (62%)
  starting transfers between devices  74.1 us (17%)
  Pallas kernels  67 us (16%)
  local copies, waits for them, and re-layouts  6.19 us (1%)
  other arithmetic  5.78 us (1%)
    all_to_all x7, waiting for transfers between devices, exchange(): return lax.all_to_all(x, 'expert', split_axis=0, concat_axis=0, tiled=True)  155 us
    ppermute x24, waiting for transfers between devices, shift(): return lax.ppermute(x, 'dp', [(i, (i + by) % N_DP) for i in range(N_DP)])  108 us
    all_to_all x7, starting transfers between devices, exchange(): return lax.all_to_all(x, 'expert', split_axis=0, concat_axis=0, tiled=True)  47.9 us
    ppermute x24, starting transfers between devices, shift(): return lax.ppermute(x, 'dp', [(i, (i + by) % N_DP) for i in range(N_DP)])  26.2 us
    pallas_call x2, Pallas kernels, hidden_of(): pl.pallas_call(functools.partial(hidden_kernel, len(inputs)), grid=(HALF...  15.9 us
    pallas_call x1, Pallas kernels, update(): pl.pallas_call(update_kernel, grid_spec=pltpu.PrefetchScalarGridSpec(num_...  10 us
    pallas_call x2, Pallas kernels, partial_grads(): pl.pallas_call(partial_kernel, grid=(steps,), out_shape=[jax.ShapeDtypeSt...  9.32 us
    pallas_call x1, Pallas kernels, weight_grads(): pl.pallas_call(weight_kernel, out_shape=jax.ShapeDtypeStruct((D, QF), bf1...  8.64 us
  transfers between devices with their start and end apart: 31, of which 14 were waited for; matrix products, arithmetic and copies ran while one was open for 2% of the time, Pallas kernels for 14%

profile of v5, /device:TPU:1, one launch (start us, length us, event | category | flops | bytes accessed | tf_op | source)
XLA Modules:
  0.0 419.6 jit_solution(3211123096829409511)
XLA Ops:
  0.6 2.6 select_rows.1
  3.2 8.6 %all-to-all-start = ((bf16[32,16,896]{2,1,0:T(8,128)(2,1)}), bf16[32,16,896]{2,1,0:T(8,128)(2,1)S(1)}, u32[]{:S(2)}, u32[]{:S(2)}) async-start(bf16[32,16,896]{2,1,0:T(8,128)(2,1)} %get-tuple-element.30), calls=%async_computation | async-start | bytes 1835008 | tf_op jit(solution)/shard_map/all_to_all | solution.py:445
  11.8 2.8 rest_rows.1
  14.6 12.7 %all-to-all-done.refs_0_.refs_8_ = bf16[32,16,896]{2,1,0:T(8,128)(2,1)S(1)} async-done(((bf16[32,16,896]{2,1,0:T(8,128)(2,1)}), bf16[32,16,896]{2,1,0:T(8,128)(2,1)S(1)}, u32[]{:S(2)}, u32[]{:S(2)}) %all-to-all-start) | async-done | bytes 917536 | tf_op jit(solution)/shard_map/all_to_all | solution.py:445
  27.4 3.9 all-to-all-start.1
  31.3 3.4 scale_rows.1
  34.6 22.1 %all-to-all-done.1.refs_4_.refs_15_ = bf16[32,32,896]{2,1,0:T(8,128)(2,1)S(1)} async-done(((bf16[32,32,896]{2,1,0:T(8,128)(2,1)}), bf16[32,32,896]{2,1,0:T(8,128)(2,1)S(1)}, u32[]{:S(2)}, u32[]{:S(2)}) %all-to-all-start.1) | async-done | bytes 1835040 | tf_op jit(solution)/shard_map/all_to_all | solution.py:445
  56.8 5.1 %all-to-all-start.3 = ((bf16[32,48,896]{2,1,0:T(8,128)(2,1)}), bf16[32,48,896]{2,1,0:T(8,128)(2,1)}, u32[]{:S(2)}, u32[]{:S(2)}) async-start(bf16[32,48,896]{2,1,0:T(8,128)(2,1)} %bitcast.34), calls=%async_computation.3 | async-start | bytes 5505024 | tf_op jit(solution)/shard_map/all_to_all | solution.py:445
  61.9 5.8 %pad_maximum_fusion = bf16[32,336,256]{2,1,0:T(8,128)(2,1)} fusion(bf16[32,112,256]{2,1,0:T(8,128)(2,1)} %bitcast.35, bf16[32,112,256]{2,1,0:T(8,128)(2,1)} %bitcast.36, bf16[32,112,256]{2,1,0:T(8,128)(2,1)} %bitcast.27), kind=kLoop, calls=%fused_computation | loop fusion | flops 16515072 | bytes 11010048 | tf_op jit(solution)/shard_map/concatenate | solution.py:483
  67.7 29.7 %all-to-all-done.3 = bf16[32,48,896]{2,1,0:T(8,128)(2,1)} async-done(((bf16[32,48,896]{2,1,0:T(8,128)(2,1)}), bf16[32,48,896]{2,1,0:T(8,128)(2,1)}, u32[]{:S(2)}, u32[]{:S(2)}) %all-to-all-start.3) | async-done | bytes 2752544 | tf_op jit(solution)/shard_map/all_to_all | solution.py:445
  97.4 5.4 %all-to-all-start.5 = ((bf16[32,336,256]{2,1,0:T(8,128)(2,1)}), bf16[32,336,256]{2,1,0:T(8,128)(2,1)}, u32[]{:S(2)}, u32[]{:S(2)}) async-start(bf16[32,336,256]{2,1,0:T(8,128)(2,1)} %pad_maximum_fusion), calls=%async_computation.5 | async-start | bytes 11010048 | tf_op jit(solution)/shard_map/all_to_all | solution.py:445
  102.8 0.8 fusion.2
  103.6 3.8 collective-permute-start.7
  107.4 0.0 collective-permute-start.6
  107.4 1.4 fusion.1
  108.8 2.7 collective-permute-start.10
  111.5 0.0 collective-permute-start
  111.5 5.4 %collective-permute-done.7.refs_2_.refs_12_ = bf16[16,16,896]{2,1,0:T(8,128)(2,1)S(1)} collective-permute-done((bf16[16,16,896]{2,1,0:T(8,128)(2,1)S(1)}, bf16[16,16,896]{2,1,0:T(8,128)(2,1)S(1)}, u32[]{:S(2)}, u32[]{:S(2)}) %collective-permute-start.7) | collective-permute-done | bytes 458784 | tf_op jit(solution)/shard_map/ppermute | solution.py:449
  116.9 3.5 collective-permute-start.1
  120.4 0.1 collective-permute-start.8
  120.5 4.5 %shard_map.140 = (bf16[768,256]{1,0:T(8,128)(2,1)}, bf16[768,256]{1,0:T(8,128)(2,1)}, bf16[768,256]{1,0:T(8,128)(2,1)}, bf16[768,256]{1,0:T(8,128)(2,1)}) custom-call(s32[1]{0:T(128)} %bitcast.4.dp, bf16[1536,896]{1,0:T(8,128)(2,1)} %bitcast.13.x, bf16[1024,896]{1,0:T(8,128)(2,1)} %bitcast.38), custom_call_target="tpu_custom_call" | custom-call | flops 1409286144 | bytes 4194304 | tf_op jit(solution)/shard_map/pallas_call | solution.py:245
  125.0 24.6 %collective-permute-done.refs_1_.refs_9_ = bf16[16,16,896]{2,1,0:T(8,128)(2,1)S(1)} collective-permute-done((bf16[16,16,896]{2,1,0:T(8,128)(2,1)}, bf16[16,16,896]{2,1,0:T(8,128)(2,1)S(1)}, u32[]{:S(2)}, u32[]{:S(2)}) %collective-permute-start) | collective-permute-done | bytes 458784 | tf_op jit(solution)/shard_map/ppermute | solution.py:449
  149.6 0.0 collective-permute-start.20
  149.6 0.8 copy-done.7
  150.4 0.0 collective-permute-done.1.refs_2_.refs_11_
  150.4 5.8 %collective-permute-done.8.refs_3_.refs_14_ = bf16[16,16,896]{2,1,0:T(8,128)(2,1)} collective-permute-done((bf16[16,16,896]{2,1,0:T(8,128)(2,1)S(1)}, bf16[16,16,896]{2,1,0:T(8,128)(2,1)}, u32[]{:S(2)}, u32[]{:S(2)}) %collective-permute-start.8) | collective-permute-done | bytes 458784 | tf_op jit(solution)/shard_map/ppermute | solution.py:449
  156.2 3.5 collective-permute-start.4
  159.7 0.1 collective-permute-start.11
  159.8 4.8 %shard_map.141 = (bf16[768,256]{1,0:T(8,128)(2,1)}, bf16[768,256]{1,0:T(8,128)(2,1)}, bf16[768,256]{1,0:T(8,128)(2,1)}, bf16[768,256]{1,0:T(8,128)(2,1)}) custom-call(s32[1]{0:T(128)} %bitcast.4.dp, bf16[1536,896]{1,0:T(8,128)(2,1)} %bitcast.13.x, bf16[1024,896]{1,0:T(8,128)(2,1)} %bitcast.39), custom_call_target="tpu_custom_call" | custom-call | flops 1409286144 | bytes 4194304 | tf_op jit(solution)/shard_map/pallas_call | solution.py:245
  164.6 0.1 collective-permute-start.21
  164.7 1.4 collective-permute-start.5
  166.1 40.4 %collective-permute-done.21.d = bf16[768,256]{1,0:T(8,128)(2,1)} collective-permute-done((bf16[768,256]{1,0:T(8,128)(2,1)}, bf16[768,256]{1,0:T(8,128)(2,1)}, u32[]{:S(2)}, u32[]{:S(2)}) %collective-permute-start.21) | collective-permute-done | bytes 393248 | tf_op jit(solution)/shard_map/ppermute | solution.py:449
  206.5 2.3 add_pairs.1
  208.9 10.1 %collective-permute-done.2.refs_3_.refs_13_ = bf16[16,16,896]{2,1,0:T(8,128)(2,1)S(1)} collective-permute-done((bf16[16,16,896]{2,1,0:T(8,128)(2,1)}, bf16[16,16,896]{2,1,0:T(8,128)(2,1)S(1)}, u32[]{:S(2)}, u32[]{:S(2)}) %collective-permute-start.2) | collective-permute-done | bytes 458784 | tf_op jit(solution)/shard_map/ppermute | solution.py:449
  218.9 1.2 collective-permute-start.18
  220.1 0.3 collective-permute-start.19
  220.4 0.1 collective-permute-start.22
  220.5 2.6 collective-permute-start.23
  223.1 8.0 %shard_map.139 = (f32[768,256]{1,0:T(8,128)}, bf16[768,256]{1,0:T(8,128)(2,1)}) custom-call(s32[1]{0:T(128)} %bitcast.4.dp, bf16[32,16,896]{2,1,0:T(8,128)(2,1)} %copy-done.1, bf16[16,16,896]{2,1,0:T(8,128)(2,1)} %collective-permute-done.6.refs_1_.refs_10_, bf16[16,16,896]{2,1,0:T(8,128)(2,1)} %copy-done.6, ...), custom_call_target="tpu_custom_call" | custom-call | flops 2818572288 | bytes 12845056 | tf_op jit(solution)/shard_map/pallas_call | solution.py:213
  231.1 7.9 %shard_map.138 = (f32[768,256]{1,0:T(8,128)}, bf16[768,256]{1,0:T(8,128)(2,1)}) custom-call(s32[1]{0:T(128)} %bitcast.4.dp, bf16[32,16,896]{2,1,0:T(8,128)(2,1)} %copy-done.1, bf16[16,16,896]{2,1,0:T(8,128)(2,1)} %copy-done.7, bf16[16,16,896]{2,1,0:T(8,128)(2,1)} %collective-permute-done.1.refs_2_.refs_11_, bf16[16,16,896]{2,1,0:T(8,128)(2,1)} %copy-done.8, ...), custom_call_target="tpu_custom_call" | custom-call | flops 2818572288 | bytes 12845056 | tf_op jit(solution)/shard_map/pallas_call | solution.py:213
  239.1 0.8 copy-done.11
  239.8 8.6 %weight_grads.1 = bf16[3584,256]{1,0:T(8,128)(2,1)} custom-call(s32[1]{0:T(128)} %bitcast.4.dp, bf16[768,256]{1,0:T(8,128)(2,1)} %get-tuple-element.35.refs_0_, bf16[768,256]{1,0:T(8,128)(2,1)} %get-tuple-element.36.refs_1_, bf16[768,256]{1,0:T(8,128)(2,1)} %collective-permute-done.18.refs_2_, bf16[768,256]{1,0:T(8,128)(2,1)} %collective-permute-done.19.refs_3_, ...), custom_call_target="tpu_custom_call" | custom-call | flops 2818572288 | bytes 15204352 | tf_op jit(solution)/shard_map/weight_grads/pallas_call | solution.py:309
  248.5 11.1 %all-to-all-start.4 = ((bf16[32,112,256]{2,1,0:T(8,128)(2,1)}), bf16[32,112,256]{2,1,0:T(8,128)(2,1)S(1)}, u32[]{:S(2)}, u32[]{:S(2)}) async-start(bf16[32,112,256]{2,1,0:T(8,128)(2,1)} %bitcast.30), calls=%async_computation.4 | async-start | bytes 3670016 | tf_op jit(solution)/shard_map/all_to_all | solution.py:445
  259.6 1.5 collective-permute-start.15
  261.2 0.0 collective-permute-start.13
  261.2 2.7 collective-permute-start.14
  263.9 6.3 %collective-permute-done.15.refs_5_ = bf16[16,48,256]{2,1,0:T(8,128)(2,1)S(1)} collective-permute-done((bf16[16,48,256]{2,1,0:T(8,128)(2,1)S(1)}, bf16[16,48,256]{2,1,0:T(8,128)(2,1)S(1)}, u32[]{:S(2)}, u32[]{:S(2)}) %collective-permute-start.15) | collective-permute-done | bytes 393248 | tf_op jit(solution)/shard_map/ppermute | solution.py:449
  270.2 2.7 collective-permute-start.17
  272.8 8.1 %collective-permute-done.13.refs_3_ = bf16[16,48,256]{2,1,0:T(8,128)(2,1)S(1)} collective-permute-done((bf16[16,48,256]{2,1,0:T(8,128)(2,1)S(1)}, bf16[16,48,256]{2,1,0:T(8,128)(2,1)S(1)}, u32[]{:S(2)}, u32[]{:S(2)}) %collective-permute-start.13) | collective-permute-done | bytes 393248 | tf_op jit(solution)/shard_map/ppermute | solution.py:449
  281.0 6.1 %collective-permute-done.17.refs_7_ = bf16[16,48,256]{2,1,0:T(8,128)(2,1)S(1)} collective-permute-done((bf16[16,48,256]{2,1,0:T(8,128)(2,1)S(1)}, bf16[16,48,256]{2,1,0:T(8,128)(2,1)S(1)}, u32[]{:S(2)}, u32[]{:S(2)}) %collective-permute-start.17) | collective-permute-done | bytes 393248 | tf_op jit(solution)/shard_map/ppermute | solution.py:449
  287.1 0.8 copy-done.18
  287.9 1.6 collective-permute-done.16.refs_6_
  289.5 7.6 %outputs.1 = bf16[1536,896]{1,0:T(8,128)(2,1)} custom-call(s32[1]{0:T(128)} %bitcast.4.dp, bf16[16,48,256]{2,1,0:T(8,128)(2,1)} %bitcast.47, bf16[16,48,256]{2,1,0:T(8,128)(2,1)} %bitcast.44, bf16[16,48,256]{2,1,0:T(8,128)(2,1)} %copy-done.15, bf16[16,48,256]{2,1,0:T(8,128)(2,1)} %copy-done.16, bf16[16,48,256]{2,1,0:T(8,128)(2,1)} %copy-done.17, ...), custom_call_target="tpu_custom_call" | custom-call | flops 2818572288 | bytes 5898240 | tf_op jit(solution)/shard_map/outputs/pallas_call | solution.py:362
  297.1 0.0 copy-start.2
  297.1 1.2 copy-done.2
  298.3 8.4 %all-to-all-start.2 = ((bf16[32,48,896]{2,1,0:T(8,128)(2,1)}), bf16[32,48,896]{2,1,0:T(8,128)(2,1)S(1)}, u32[]{:S(2)}, u32[]{:S(2)}) async-start(bf16[32,48,896]{2,1,0:T(8,128)(2,1)} %bitcast.33), calls=%async_computation.2 | async-start | bytes 5505024 | tf_op jit(solution)/shard_map/all_to_all | solution.py:445
  306.7 10.0 %update.1 = bf16[32,3,112,256]{3,2,1,0:T(8,128)(2,1)} custom-call(s32[32]{0:T(128)} %plan.1, s32[32]{0:T(128)} %placement.1, bf16[32,112,256]{2,1,0:T(8,128)(2,1)} %copy-done.2, bf16[32,336,256]{2,1,0:T(8,128)(2,1)} %all-to-all-done.5.gate.first.second, bf16[32,336,256]{2,1,0:T(8,128)(2,1)} %all-to-all-done.5.gate.first.second, ...), custom_call_target="tpu_custom_call" | custom-call | flops 18350080 | bytes 10485760 | tf_op jit(solution)/shard_map/update/pallas_call | solution.py:410
  316.7 25.3 %all-to-all-done.2 = bf16[32,48,896]{2,1,0:T(8,128)(2,1)S(1)} async-done(((bf16[32,48,896]{2,1,0:T(8,128)(2,1)}), bf16[32,48,896]{2,1,0:T(8,128)(2,1)S(1)}, u32[]{:S(2)}, u32[]{:S(2)}) %all-to-all-start.2) | async-done | bytes 2752544 | tf_op jit(solution)/shard_map/all_to_all | solution.py:445
  342.0 5.4 %all-to-all-start.6 = ((bf16[32,3,112,256]{3,2,1,0:T(8,128)(2,1)}), bf16[32,3,112,256]{3,2,1,0:T(8,128)(2,1)}, u32[]{:S(2)}, u32[]{:S(2)}) async-start(bf16[32,3,112,256]{3,2,1,0:T(8,128)(2,1)} %update.1), calls=%async_computation.6 | async-start | bytes 11010048 | tf_op jit(solution)/shard_map/all_to_all | solution.py:445
  347.4 0.6 fusion.3
  348.0 0.4 copy-done.9
  348.4 1.3 fusion
  349.7 65.6 %all-to-all-done.6.moments = bf16[32,3,112,256]{3,2,1,0:T(8,128)(2,1)} async-done(((bf16[32,3,112,256]{3,2,1,0:T(8,128)(2,1)}), bf16[32,3,112,256]{3,2,1,0:T(8,128)(2,1)}, u32[]{:S(2)}, u32[]{:S(2)}) %all-to-all-start.6) | async-done | bytes 5505056 | tf_op jit(solution)/shard_map/all_to_all | solution.py:445
  415.3 4.4 %finish.1 = (bf16[32,112,256]{2,1,0:T(8,128)(2,1)}, bf16[32,112,256]{2,1,0:T(8,128)(2,1)}, bf16[32,112,256]{2,1,0:T(8,128)(2,1)}) custom-call(bf16[32,3,112,256]{3,2,1,0:T(8,128)(2,1)} %all-to-all-done.6.moments), custom_call_target="tpu_custom_call" | custom-call | bytes 12582912 | tf_op jit(solution)/shard_map/finish/pallas_call | solution.py:433
  (53 shorter events, 0.1 us)
Async XLA Ops:
  3.2 24.1 %all-to-all-start = ((bf16[32,16,896]{2,1,0:T(8,128)(2,1)}), bf16[32,16,896]{2,1,0:T(8,128)(2,1)S(1)}, u32[]{:S(2)}, u32[]{:S(2)}) async-start(bf16[32,16,896]{2,1,0:T(8,128)(2,1)} %get-tuple-element.30), calls=%async_computation | async-start | bytes 1835008 | tf_op jit(solution)/shard_map/all_to_all | solution.py:445
  27.4 75.4 %copy-start.1 = (bf16[32,16,896]{2,1,0:T(8,128)(2,1)}, bf16[32,16,896]{2,1,0:T(8,128)(2,1)S(1)}, u32[]{:S(2)}) copy-start(bf16[32,16,896]{2,1,0:T(8,128)(2,1)S(1)} %all-to-all-done.refs_0_.refs_8_) | copy-start | bytes 2752516
  27.4 29.4 %all-to-all-start.1 = ((bf16[32,32,896]{2,1,0:T(8,128)(2,1)}), bf16[32,32,896]{2,1,0:T(8,128)(2,1)S(1)}, u32[]{:S(2)}, u32[]{:S(2)}) async-start(bf16[32,32,896]{2,1,0:T(8,128)(2,1)} %rest_rows.1), calls=%async_computation.1 | async-start | bytes 3670016 | tf_op jit(solution)/shard_map/all_to_all | solution.py:445
  56.8 50.6 %copy-start = (bf16[32,32,896]{2,1,0:T(8,128)(2,1)}, bf16[32,32,896]{2,1,0:T(8,128)(2,1)S(1)}, u32[]{:S(2)}) copy-start(bf16[32,32,896]{2,1,0:T(8,128)(2,1)S(1)} %all-to-all-done.1.refs_4_.refs_15_) | copy-start | bytes 5505028
  56.8 40.6 %all-to-all-start.3 = ((bf16[32,48,896]{2,1,0:T(8,128)(2,1)}), bf16[32,48,896]{2,1,0:T(8,128)(2,1)}, u32[]{:S(2)}, u32[]{:S(2)}) async-start(bf16[32,48,896]{2,1,0:T(8,128)(2,1)} %bitcast.34), calls=%async_computation.3 | async-start | bytes 5505024 | tf_op jit(solution)/shard_map/all_to_all | solution.py:445
  97.4 151.1 %all-to-all-start.5 = ((bf16[32,336,256]{2,1,0:T(8,128)(2,1)}), bf16[32,336,256]{2,1,0:T(8,128)(2,1)}, u32[]{:S(2)}, u32[]{:S(2)}) async-start(bf16[32,336,256]{2,1,0:T(8,128)(2,1)} %pad_maximum_fusion), calls=%async_computation.5 | async-start | bytes 11010048 | tf_op jit(solution)/shard_map/all_to_all | solution.py:445
  103.6 13.2 %collective-permute-start.7 = (bf16[16,16,896]{2,1,0:T(8,128)(2,1)S(1)}, bf16[16,16,896]{2,1,0:T(8,128)(2,1)S(1)}, u32[]{:S(2)}, u32[]{:S(2)}) collective-permute-start(bf16[16,16,896]{2,1,0:T(8,128)(2,1)S(1)} %get-tuple-element.52), channel_id=1, source_target_pairs={{0,96},{32,0},{64,32},{96,64},{1,97},{33,1},{65,33},{97,65},{2,98}... | collective-permute-start | bytes 1376264 | tf_op jit(solution)/shard_map/ppermute | solution.py:449
  107.4 13.0 %collective-permute-start.6 = (bf16[16,16,896]{2,1,0:T(8,128)(2,1)S(1)}, bf16[16,16,896]{2,1,0:T(8,128)(2,1)}, u32[]{:S(2)}, u32[]{:S(2)}) collective-permute-start(bf16[16,16,896]{2,1,0:T(8,128)(2,1)S(1)} %get-tuple-element.52), channel_id=1, source_target_pairs={{0,32},{32,64},{64,96},{96,0},{1,33},{33,65},{65,97},{97,1},{2,34}... | collective-permute-start | bytes 1376264 | tf_op jit(solution)/shard_map/ppermute | solution.py:449
  108.8 50.9 %collective-permute-start.10 = (bf16[16,32,896]{2,1,0:T(8,128)(2,1)}, bf16[16,32,896]{2,1,0:T(8,128)(2,1)S(1)}, u32[]{:S(2)}, u32[]{:S(2)}) collective-permute-start(bf16[16,32,896]{2,1,0:T(8,128)(2,1)} %get-tuple-element.50), channel_id=1, source_target_pairs={{0,96},{32,0},{64,32},{96,64},{1,97},{33,1},{65,33},{97,65},{2,98}... | collective-permute-start | bytes 2752520 | tf_op jit(solution)/shard_map/ppermute | solution.py:449
  111.5 53.1 %collective-permute-start.3 = (bf16[16,32,896]{2,1,0:T(8,128)(2,1)}, bf16[16,32,896]{2,1,0:T(8,128)(2,1)S(1)}, u32[]{:S(2)}, u32[]{:S(2)}) collective-permute-start(bf16[16,32,896]{2,1,0:T(8,128)(2,1)} %get-tuple-element.51), channel_id=1, source_target_pairs={{0,32},{32,64},{64,96},{96,0},{1,33},{33,65},{65,97},{97,1},{2,34}... | collective-permute-start | bytes 2752520 | tf_op jit(solution)/shard_map/ppermute | solution.py:449
  111.5 38.1 %collective-permute-start = (bf16[16,16,896]{2,1,0:T(8,128)(2,1)}, bf16[16,16,896]{2,1,0:T(8,128)(2,1)S(1)}, u32[]{:S(2)}, u32[]{:S(2)}) collective-permute-start(bf16[16,16,896]{2,1,0:T(8,128)(2,1)} %get-tuple-element.53), channel_id=1, source_target_pairs={{0,32},{32,64},{64,96},{96,0},{1,33},{33,65},{65,97},{97,1},{2,34}... | collective-permute-start | bytes 1376264 | tf_op jit(solution)/shard_map/ppermute | solution.py:449
  116.9 47.7 %copy-start.6 = (bf16[16,16,896]{2,1,0:T(8,128)(2,1)}, bf16[16,16,896]{2,1,0:T(8,128)(2,1)S(1)}, u32[]{:S(2)}) copy-start(bf16[16,16,896]{2,1,0:T(8,128)(2,1)S(1)} %collective-permute-done.7.refs_2_.refs_12_) | copy-start | bytes 1376260
  116.9 33.5 %collective-permute-start.1 = (bf16[16,16,896]{2,1,0:T(8,128)(2,1)}, bf16[16,16,896]{2,1,0:T(8,128)(2,1)}, u32[]{:S(2)}, u32[]{:S(2)}) collective-permute-start(bf16[16,16,896]{2,1,0:T(8,128)(2,1)} %get-tuple-element.53), channel_id=1, source_target_pairs={{0,96},{32,0},{64,32},{96,64},{1,97},{33,1},{65,33},{97,65},{2,98}... | collective-permute-start | bytes 1376264 | tf_op jit(solution)/shard_map/ppermute | solution.py:449
  120.4 35.8 %collective-permute-start.8 = (bf16[16,16,896]{2,1,0:T(8,128)(2,1)S(1)}, bf16[16,16,896]{2,1,0:T(8,128)(2,1)}, u32[]{:S(2)}, u32[]{:S(2)}) collective-permute-start(bf16[16,16,896]{2,1,0:T(8,128)(2,1)S(1)} %collective-permute-done.7.refs_2_.refs_12_), channel_id=1, source_target_pairs={{0,96},{32,0},{64,32},{96,64},{1,97},{33,1},{65,33},{97,65},{2,98}... | collective-permute-start | bytes 1376264 | tf_op jit(solution)/shard_map/ppermute | solution.py:449
  149.6 0.8 copy-start.7
  149.6 15.1 %collective-permute-start.20 = (bf16[768,256]{1,0:T(8,128)(2,1)}, bf16[768,256]{1,0:T(8,128)(2,1)}, u32[]{:S(2)}, u32[]{:S(2)}) collective-permute-start(bf16[768,256]{1,0:T(8,128)(2,1)} %get-tuple-element.40), channel_id=1, source_target_pairs={{0,32},{32,64},{64,96},{96,0},{1,33},{33,65},{65,97},{97,1},{2,34}... | collective-permute-start | bytes 1179656 | tf_op jit(solution)/shard_map/ppermute | solution.py:449
  150.4 69.8 %collective-permute-start.9 = (bf16[16,32,896]{2,1,0:T(8,128)(2,1)}, bf16[16,32,896]{2,1,0:T(8,128)(2,1)S(1)}, u32[]{:S(2)}, u32[]{:S(2)}) collective-permute-start(bf16[16,32,896]{2,1,0:T(8,128)(2,1)} %get-tuple-element.50), channel_id=1, source_target_pairs={{0,32},{32,64},{64,96},{96,0},{1,33},{33,65},{65,97},{97,1},{2,34}... | collective-permute-start | bytes 2752520 | tf_op jit(solution)/shard_map/ppermute | solution.py:449
  156.2 64.2 %collective-permute-start.4 = (bf16[16,32,896]{2,1,0:T(8,128)(2,1)}, bf16[16,32,896]{2,1,0:T(8,128)(2,1)}, u32[]{:S(2)}, u32[]{:S(2)}) collective-permute-start(bf16[16,32,896]{2,1,0:T(8,128)(2,1)} %get-tuple-element.51), channel_id=1, source_target_pairs={{0,96},{32,0},{64,32},{96,64},{1,97},{33,1},{65,33},{97,65},{2,98}... | collective-permute-start | bytes 2752520 | tf_op jit(solution)/shard_map/ppermute | solution.py:449
  159.7 49.2 %copy-start.3 = (bf16[16,32,896]{2,1,0:T(8,128)(2,1)}, bf16[16,32,896]{2,1,0:T(8,128)(2,1)S(1)}, u32[]{:S(2)}) copy-start(bf16[16,32,896]{2,1,0:T(8,128)(2,1)S(1)} %collective-permute-done.10.refs_6_.refs_19_) | copy-start | bytes 2752516
  159.7 60.8 %collective-permute-start.11 = (bf16[16,32,896]{2,1,0:T(8,128)(2,1)S(1)}, bf16[16,32,896]{2,1,0:T(8,128)(2,1)}, u32[]{:S(2)}, u32[]{:S(2)}) collective-permute-start(bf16[16,32,896]{2,1,0:T(8,128)(2,1)S(1)} %collective-permute-done.10.refs_6_.refs_19_), channel_id=1, source_target_pairs={{0,96},{32,0},{64,32},{96,64},{1,97},{33,1},{65,33},{97,65},{2,98}... | collective-permute-start | bytes 2752520 | tf_op jit(solution)/shard_map/ppermute | solution.py:449
  164.6 66.5 %copy-start.4 = (bf16[16,32,896]{2,1,0:T(8,128)(2,1)}, bf16[16,32,896]{2,1,0:T(8,128)(2,1)S(1)}, u32[]{:S(2)}) copy-start(bf16[16,32,896]{2,1,0:T(8,128)(2,1)S(1)} %collective-permute-done.3.refs_5_.refs_16_) | copy-start | bytes 2752516
  164.6 42.0 %collective-permute-start.21 = (bf16[768,256]{1,0:T(8,128)(2,1)}, bf16[768,256]{1,0:T(8,128)(2,1)}, u32[]{:S(2)}, u32[]{:S(2)}) collective-permute-start(bf16[768,256]{1,0:T(8,128)(2,1)} %get-tuple-element.42), channel_id=1, source_target_pairs={{0,96},{32,0},{64,32},{96,64},{1,97},{33,1},{65,33},{97,65},{2,98}... | collective-permute-start | bytes 1179656 | tf_op jit(solution)/shard_map/ppermute | solution.py:449
  164.7 66.4 %collective-permute-start.5 = (bf16[16,32,896]{2,1,0:T(8,128)(2,1)S(1)}, bf16[16,32,896]{2,1,0:T(8,128)(2,1)}, u32[]{:S(2)}, u32[]{:S(2)}) collective-permute-start(bf16[16,32,896]{2,1,0:T(8,128)(2,1)S(1)} %collective-permute-done.3.refs_5_.refs_16_), channel_id=1, source_target_pairs={{0,32},{32,64},{64,96},{96,0},{1,33},{33,65},{65,97},{97,1},{2,34}... | collective-permute-start | bytes 2752520 | tf_op jit(solution)/shard_map/ppermute | solution.py:449
  206.5 12.4 %collective-permute-start.2 = (bf16[16,16,896]{2,1,0:T(8,128)(2,1)}, bf16[16,16,896]{2,1,0:T(8,128)(2,1)S(1)}, u32[]{:S(2)}, u32[]{:S(2)}) collective-permute-start(bf16[16,16,896]{2,1,0:T(8,128)(2,1)} %copy-done.7), channel_id=1, source_target_pairs={{0,32},{32,64},{64,96},{96,0},{1,33},{33,65},{65,97},{97,1},{2,34}... | collective-permute-start | bytes 1376264 | tf_op jit(solution)/shard_map/ppermute | solution.py:449
  218.9 12.1 %copy-start.8 = (bf16[16,16,896]{2,1,0:T(8,128)(2,1)}, bf16[16,16,896]{2,1,0:T(8,128)(2,1)S(1)}, u32[]{:S(2)}) copy-start(bf16[16,16,896]{2,1,0:T(8,128)(2,1)S(1)} %collective-permute-done.2.refs_3_.refs_13_) | copy-start | bytes 1376260
  218.9 20.1 %collective-permute-start.18 = (bf16[768,256]{1,0:T(8,128)(2,1)}, bf16[768,256]{1,0:T(8,128)(2,1)}, u32[]{:S(2)}, u32[]{:S(2)}) collective-permute-start(bf16[768,256]{1,0:T(8,128)(2,1)} %get-tuple-element.37), channel_id=1, source_target_pairs={{0,96},{32,0},{64,32},{96,64},{1,97},{33,1},{65,33},{97,65},{2,98}... | collective-permute-start | bytes 1179656 | tf_op jit(solution)/shard_map/ppermute | solution.py:449
  220.1 3.0 copy-start.5
  220.1 18.9 %collective-permute-start.19 = (bf16[768,256]{1,0:T(8,128)(2,1)}, bf16[768,256]{1,0:T(8,128)(2,1)}, u32[]{:S(2)}, u32[]{:S(2)}) collective-permute-start(bf16[768,256]{1,0:T(8,128)(2,1)} %get-tuple-element.38), channel_id=1, source_target_pairs={{0,32},{32,64},{64,96},{96,0},{1,33},{33,65},{65,97},{97,1},{2,34}... | collective-permute-start | bytes 1179656 | tf_op jit(solution)/shard_map/ppermute | solution.py:449
  220.4 18.6 %collective-permute-start.22 = (bf16[768,256]{1,0:T(8,128)(2,1)}, bf16[768,256]{1,0:T(8,128)(2,1)}, u32[]{:S(2)}, u32[]{:S(2)}) collective-permute-start(bf16[768,256]{1,0:T(8,128)(2,1)} %get-tuple-element.43), channel_id=1, source_target_pairs={{0,32},{32,64},{64,96},{96,0},{1,33},{33,65},{65,97},{97,1},{2,34}... | collective-permute-start | bytes 1179656 | tf_op jit(solution)/shard_map/ppermute | solution.py:449
  220.5 18.6 %collective-permute-start.23 = (bf16[768,256]{1,0:T(8,128)(2,1)}, bf16[768,256]{1,0:T(8,128)(2,1)S(1)}, u32[]{:S(2)}, u32[]{:S(2)}) collective-permute-start(bf16[768,256]{1,0:T(8,128)(2,1)} %get-tuple-element.44), channel_id=1, source_target_pairs={{0,96},{32,0},{64,32},{96,64},{1,97},{33,1},{65,33},{97,65},{2,98}... | collective-permute-start | bytes 1179656 | tf_op jit(solution)/shard_map/ppermute | solution.py:449
  239.1 0.8 copy-start.11
  248.5 11.2 %copy-start.12 = (bf16[768,256]{1,0:T(8,128)(2,1)S(1)}, bf16[768,256]{1,0:T(8,128)(2,1)}, u32[]{:S(2)}) copy-start(bf16[768,256]{1,0:T(8,128)(2,1)} %get-tuple-element.32) | copy-start | bytes 1179652
  248.5 12.7 %copy-start.13 = (bf16[768,256]{1,0:T(8,128)(2,1)S(1)}, bf16[768,256]{1,0:T(8,128)(2,1)}, u32[]{:S(2)}) copy-start(bf16[768,256]{1,0:T(8,128)(2,1)} %get-tuple-element.31) | copy-start | bytes 1179652
  248.5 48.6 %all-to-all-start.4 = ((bf16[32,112,256]{2,1,0:T(8,128)(2,1)}), bf16[32,112,256]{2,1,0:T(8,128)(2,1)S(1)}, u32[]{:S(2)}, u32[]{:S(2)}) async-start(bf16[32,112,256]{2,1,0:T(8,128)(2,1)} %bitcast.30), calls=%async_computation.4 | async-start | bytes 3670016 | tf_op jit(solution)/shard_map/all_to_all | solution.py:445
  259.6 10.5 %collective-permute-start.15 = (bf16[16,48,256]{2,1,0:T(8,128)(2,1)S(1)}, bf16[16,48,256]{2,1,0:T(8,128)(2,1)S(1)}, u32[]{:S(2)}, u32[]{:S(2)}) collective-permute-start(bf16[16,48,256]{2,1,0:T(8,128)(2,1)S(1)} %bitcast.45), channel_id=1, source_target_pairs={{0,96},{32,0},{64,32},{96,64},{1,97},{33,1},{65,33},{97,65},{2,98}... | collective-permute-start | bytes 1179656 | tf_op jit(solution)/shard_map/ppermute | solution.py:449
  261.2 11.7 %collective-permute-start.12 = (bf16[16,48,256]{2,1,0:T(8,128)(2,1)S(1)}, bf16[16,48,256]{2,1,0:T(8,128)(2,1)S(1)}, u32[]{:S(2)}, u32[]{:S(2)}) collective-permute-start(bf16[16,48,256]{2,1,0:T(8,128)(2,1)S(1)} %bitcast.48), channel_id=1, source_target_pairs={{0,32},{32,64},{64,96},{96,0},{1,33},{33,65},{65,97},{97,1},{2,34}... | collective-permute-start | bytes 1179656 | tf_op jit(solution)/shard_map/ppermute | solution.py:449
  261.2 19.8 %collective-permute-start.13 = (bf16[16,48,256]{2,1,0:T(8,128)(2,1)S(1)}, bf16[16,48,256]{2,1,0:T(8,128)(2,1)S(1)}, u32[]{:S(2)}, u32[]{:S(2)}) collective-permute-start(bf16[16,48,256]{2,1,0:T(8,128)(2,1)S(1)} %bitcast.46), channel_id=1, source_target_pairs={{0,32},{32,64},{64,96},{96,0},{1,33},{33,65},{65,97},{97,1},{2,34}... | collective-permute-start | bytes 1179656 | tf_op jit(solution)/shard_map/ppermute | solution.py:449
  261.2 19.8 %collective-permute-start.14 = (bf16[16,48,256]{2,1,0:T(8,128)(2,1)S(1)}, bf16[16,48,256]{2,1,0:T(8,128)(2,1)S(1)}, u32[]{:S(2)}, u32[]{:S(2)}) collective-permute-start(bf16[16,48,256]{2,1,0:T(8,128)(2,1)S(1)} %bitcast.49), channel_id=1, source_target_pairs={{0,96},{32,0},{64,32},{96,64},{1,97},{33,1},{65,33},{97,65},{2,98}... | collective-permute-start | bytes 1179656 | tf_op jit(solution)/shard_map/ppermute | solution.py:449
  270.2 19.4 %copy-start.14 = (bf16[16,48,256]{2,1,0:T(8,128)(2,1)}, bf16[16,48,256]{2,1,0:T(8,128)(2,1)S(1)}, u32[]{:S(2)}) copy-start(bf16[16,48,256]{2,1,0:T(8,128)(2,1)S(1)} %collective-permute-done.15.refs_5_) | copy-start | bytes 1179652
  270.2 17.0 %collective-permute-start.17 = (bf16[16,48,256]{2,1,0:T(8,128)(2,1)S(1)}, bf16[16,48,256]{2,1,0:T(8,128)(2,1)S(1)}, u32[]{:S(2)}, u32[]{:S(2)}) collective-permute-start(bf16[16,48,256]{2,1,0:T(8,128)(2,1)S(1)} %collective-permute-done.15.refs_5_), channel_id=1, source_target_pairs={{0,96},{32,0},{64,32},{96,64},{1,97},{33,1},{65,33},{97,65},{2,98}... | collective-permute-start | bytes 1179656 | tf_op jit(solution)/shard_map/ppermute | solution.py:449
  272.8 16.7 %copy-start.15 = (bf16[16,48,256]{2,1,0:T(8,128)(2,1)}, bf16[16,48,256]{2,1,0:T(8,128)(2,1)S(1)}, u32[]{:S(2)}) copy-start(bf16[16,48,256]{2,1,0:T(8,128)(2,1)S(1)} %collective-permute-done.12.refs_2_) | copy-start | bytes 1179652
  272.8 16.7 %collective-permute-start.16 = (bf16[16,48,256]{2,1,0:T(8,128)(2,1)S(1)}, bf16[16,48,256]{2,1,0:T(8,128)(2,1)}, u32[]{:S(2)}, u32[]{:S(2)}) collective-permute-start(bf16[16,48,256]{2,1,0:T(8,128)(2,1)S(1)} %collective-permute-done.12.refs_2_), channel_id=1, source_target_pairs={{0,32},{32,64},{64,96},{96,0},{1,33},{33,65},{65,97},{97,1},{2,34}... | collective-permute-start | bytes 1179656 | tf_op jit(solution)/shard_map/ppermute | solution.py:449
  281.0 6.1 %copy-start.16 = (bf16[16,48,256]{2,1,0:T(8,128)(2,1)}, bf16[16,48,256]{2,1,0:T(8,128)(2,1)S(1)}, u32[]{:S(2)}) copy-start(bf16[16,48,256]{2,1,0:T(8,128)(2,1)S(1)} %collective-permute-done.13.refs_3_) | copy-start | bytes 1179652
  281.0 6.1 %copy-start.17 = (bf16[16,48,256]{2,1,0:T(8,128)(2,1)}, bf16[16,48,256]{2,1,0:T(8,128)(2,1)S(1)}, u32[]{:S(2)}) copy-start(bf16[16,48,256]{2,1,0:T(8,128)(2,1)S(1)} %collective-permute-done.14.refs_4_) | copy-start | bytes 1179652
  287.1 0.8 copy-start.18
  297.1 1.2 copy-start.2
  298.3 43.7 %all-to-all-start.2 = ((bf16[32,48,896]{2,1,0:T(8,128)(2,1)}), bf16[32,48,896]{2,1,0:T(8,128)(2,1)S(1)}, u32[]{:S(2)}, u32[]{:S(2)}) async-start(bf16[32,48,896]{2,1,0:T(8,128)(2,1)} %bitcast.33), calls=%async_computation.2 | async-start | bytes 5505024 | tf_op jit(solution)/shard_map/all_to_all | solution.py:445
  316.7 30.7 %copy-start.10 = (bf16[1536,128]{1,0:T(8,128)(2,1)S(1)}, bf16[1536,128]{1,0:T(8,128)(2,1)}, u32[]{:S(2)}) copy-start(bf16[1536,128]{1,0:T(8,128)(2,1)} %get-tuple-element.33) | copy-start | bytes 1179652
  342.0 73.3 %all-to-all-start.6 = ((bf16[32,3,112,256]{3,2,1,0:T(8,128)(2,1)}), bf16[32,3,112,256]{3,2,1,0:T(8,128)(2,1)}, u32[]{:S(2)}, u32[]{:S(2)}) async-start(bf16[32,3,112,256]{3,2,1,0:T(8,128)(2,1)} %update.1), calls=%async_computation.6 | async-start | bytes 11010048 | tf_op jit(solution)/shard_map/all_to_all | solution.py:445
  347.4 1.0 copy-start.9
